TPU v7x, 768 devices: a whole 4x8x12 slice. The times are simulated.
768 devices in a mesh: section: 8 (over y), shard: 96 (over z, x, core).
Axes of the slice: x: 4, y: 8, z: 12, core: 2. Of those that a mesh axis runs over, the one named last changes fastest.
Arguments:
- features: bfloat16 [2, 96, 64, 1536], P(None, 'shard'), may hold values from -6 to 6
- window_building_index: int32 [2, 96], P(None, 'shard'), may hold values from 0 to 127
- building_embeddings: bfloat16 [128, 1536], replicated, may hold values from -6 to 6
- dilation_exponent: int32 [8], P('section'), may hold values from 0 to 5
- weights: bfloat16 [8, 2, 1536, 1536], P('section', None, 'shard'), may hold values from -0.109375 to 0.109375
- cotangent: bfloat16 [2, 96, 64, 1536], P(None, 'shard'), may hold values from -0.053955078 to 0.053955078
Outputs:
- grad_weights: float32 [8, 2, 1536, 1536], P('section', None, 'shard')
All inputs are finite; a program needn't handle non-finite values.
Results may differ from a plain program's by a relative error of at most 0.017.
Values may be sent and summed in bfloat16 or wider, within the bound.
No kernel may reach another device: no remote copies, remote signals or barrier semaphores. Data moves between devices by JAX's collectives and lax.ppermute only.
A program may use at most 128 MiB of HBM per device.

v0:
```python
import jax
import jax.numpy as jnp
from jax import lax
from jax.experimental import pallas as pl
from jax.experimental.pallas import tpu as pltpu
from jax.sharding import Mesh, PartitionSpec as P

SECTIONS, HIGH, LOW, ACROSS, CORES = 8, 4, 3, 4, 2
OWN = 16
BLOCK = 256
CHUNKS = 4
LIMIT = 20 * 1024 * 1024
SHARD = ("zh", "zl", "x", "core")
DEEP = ("zh", "zl")
ROW = ("x", "core")
WIDE = ("zl", "x", "core")


def shifted(values, hours, limit_low):
    length = values.shape[0]
    row = lax.broadcasted_iota(jnp.int32, values.shape, 0)
    if limit_low:
        return jnp.where(row >= hours, pltpu.roll(values, hours, 0), 0.0)
    return jnp.where(row < length - hours, pltpu.roll(values, length - hours, 0), 0.0)


def norm_of(x_full):
    inverse = lax.rsqrt(jnp.mean(x_full * x_full, axis=-1, keepdims=True) + 1e-06)
    return inverse, x_full * inverse


def settle_body(*refs):
    count = (len(refs) - 2) // 2
    sems = refs[-1]
    copies = [
        pltpu.make_async_copy(refs[i], refs[count + 1 + i], sems.at[i]) for i in range(count)
    ]
    for copy in copies:
        copy.start()
    for copy in copies:
        copy.wait()


def settle(arrays, after):
    size = sum(v.size * v.dtype.itemsize for v in arrays)
    return pl.pallas_call(
        settle_body,
        out_shape=tuple(pltpu.VMEM(v.shape, v.dtype) for v in arrays),
        in_specs=[pl.BlockSpec(memory_space=pltpu.HBM)] * len(arrays) + [pl.BlockSpec(memory_space=pl.ANY)],
        out_specs=tuple(VMEM for _ in arrays),
        scratch_shapes=[pltpu.SemaphoreType.DMA((len(arrays),))],
        cost_estimate=pl.CostEstimate(flops=0, transcendentals=0, bytes_accessed=4 * size),
        compiler_params=pltpu.CompilerParams(vmem_limit_bytes=LIMIT),
        name="settle",
    )(*(pltpu.with_memory_space_constraint(v, pltpu.HBM) for v in arrays), after)


def ordered(meta, current, moved):
    even = meta[2] == 0
    first = jnp.where(even, current, moved).astype(jnp.bfloat16)
    second = jnp.where(even, moved, current).astype(jnp.bfloat16)
    return first, second


def forward_part(meta, x_ref, own_ref, other_ref, x_out, xs, zs, acts):
    slot = meta[0]
    x_full = x_ref[...].astype(jnp.float32)
    _, normed = norm_of(x_full)
    rounded = normed.astype(jnp.bfloat16)
    xs[slot] = x_ref[...]
    acts[slot] = rounded
    current = rounded.astype(jnp.float32)
    first, second = ordered(meta, current, shifted(current, meta[1], True))
    for start in range(0, x_ref.shape[1], BLOCK):
        cols = slice(start, start + BLOCK)
        pre = jnp.dot(first, own_ref[:, cols], preferred_element_type=jnp.float32)
        pre += jnp.dot(second, other_ref[:, cols], preferred_element_type=jnp.float32)
        zs[slot, :, cols] = pre
        x_out[:, cols] = (x_ref[:, cols].astype(jnp.float32) + pre * jax.nn.sigmoid(pre)).astype(jnp.bfloat16)


def backward_part(meta, g_ref, own_ref, other_ref, xs, zs, g_out, dzs, da):
    slot = meta[3]
    pre = zs[slot]
    sigma = jax.nn.sigmoid(pre)
    d_pre = g_ref[...].astype(jnp.float32) * sigma * (1.0 + pre * (1.0 - sigma))
    d_pre = d_pre.astype(jnp.bfloat16)
    dzs[slot] = d_pre
    current = d_pre.astype(jnp.float32)
    first, second = ordered(meta, current, shifted(current, meta[1], False))
    dims = (((1,), (1,)), ((), ()))
    for start in range(0, g_ref.shape[1], BLOCK):
        rows = slice(start, start + BLOCK)
        part = lax.dot_general(first, own_ref[rows, :], dims, preferred_element_type=jnp.float32)
        part += lax.dot_general(second, other_ref[rows, :], dims, preferred_element_type=jnp.float32)
        da[:, rows] = part
    inverse, normed = norm_of(xs[slot].astype(jnp.float32))
    d_norm = da[...]
    mean = jnp.mean(d_norm * normed, axis=-1, keepdims=True)
    g_out[...] = (g_ref[...].astype(jnp.float32) + inverse * (d_norm - normed * mean)).astype(jnp.bfloat16)


def forward_body(meta, x_ref, own_ref, other_ref, keep_x, keep_z, keep_a, x_out, xs, zs, acts):
    del keep_x, keep_z, keep_a
    forward_part(meta, x_ref, own_ref, other_ref, x_out, xs, zs, acts)


def backward_body(meta, g_ref, own_ref, other_ref, xs, zs, keep_d, g_out, dzs, da):
    del keep_d
    backward_part(meta, g_ref, own_ref, other_ref, xs, zs, g_out, dzs, da)


def last_body(meta, g_ref, own_ref, other_ref, xs, zs, keep_d, g_out, turned, dzs, da):
    backward_body(meta, g_ref, own_ref, other_ref, xs, zs, keep_d, g_out, dzs, da)
    hours_all = jnp.concatenate([dzs[i].astype(jnp.float32) for i in range(dzs.shape[0] - 1)], axis=0)
    turned[...] = hours_all.T.astype(jnp.bfloat16)


def weights_body(meta, turned, source_ref, out, every, sides, total, sems):
    depth = every.shape[0] // CHUNKS
    copies = []
    for index in range(CHUNKS):
        span = slice(index * depth, (index + 1) * depth)
        copies.append(pltpu.make_async_copy(source_ref.at[span], every.at[span], sems.at[index]))
        copies[-1].start()
    members = every.shape[0] // turned.shape[1]
    piece = turned.shape[0] // members
    length = turned.shape[1] // 2
    hours = meta[1]
    current = turned[...].astype(jnp.float32)
    lane = lax.broadcasted_iota(jnp.int32, current.shape, 1) % length
    moved = jnp.where(lane < length - hours, pltpu.roll(current, 2 * length - hours, 1), 0.0)
    for source in range(members):
        span = slice(source * piece, (source + 1) * piece)
        lanes = slice(source * 2 * length, (source + 1) * 2 * length)
        sides[:piece, lanes] = current[span].astype(jnp.bfloat16)
        sides[piece:, lanes] = moved[span].astype(jnp.bfloat16)
    chips = BLOCK // (CORES * OWN)
    for index in range(CHUNKS):
        copies[index].wait()
        span = slice(index * depth, (index + 1) * depth)
        for block, start in enumerate(range(0, every.shape[1], BLOCK)):
            cols = slice(start, start + BLOCK)
            part = jnp.dot(sides[:, span], every[span, cols], preferred_element_type=jnp.float32)
            if index > 0:
                part += total[:, cols]
            if index < CHUNKS - 1:
                total[:, cols] = part
                continue
            part = part.T.reshape(chips, CORES, OWN, 2 * piece).astype(jnp.bfloat16)
            for core in range(CORES):
                out[core, block * chips : (block + 1) * chips] = part[:, core]


def weight_partials(meta, turned, every):
    tokens, width = every.shape
    piece = width * turned.shape[1] // tokens
    return pl.pallas_call(
        weights_body,
        out_shape=jax.ShapeDtypeStruct((CORES, width // (CORES * OWN), OWN, 2 * piece), jnp.bfloat16),
        in_specs=[SMEM, VMEM, pl.BlockSpec(memory_space=pltpu.HBM)],
        out_specs=VMEM,
        scratch_shapes=[
            pltpu.VMEM(every.shape, every.dtype),
            pltpu.VMEM((2 * piece, tokens), jnp.bfloat16),
            pltpu.VMEM((2 * piece, width), jnp.float32),
            pltpu.SemaphoreType.DMA((CHUNKS,)),
        ],
        compiler_params=pltpu.CompilerParams(vmem_limit_bytes=LIMIT),
        name="weight_partials",
    )(meta, turned, pltpu.with_memory_space_constraint(every, pltpu.HBM))


def turn_body(
    meta, x_ref, g_ref, own_ref, other_ref, keep_x, keep_z, keep_a, keep_d, x_out, g_out, xs, zs, acts, dzs, da
):
    del keep_x, keep_z, keep_a, keep_d
    forward_part(meta, x_ref, own_ref, other_ref, x_out, xs, zs, acts)
    backward_part(meta, g_ref, own_ref, other_ref, xs, zs, g_out, dzs, da)


VMEM = pl.BlockSpec(memory_space=pltpu.VMEM)
SMEM = pl.BlockSpec(memory_space=pltpu.SMEM)


def run(body, name, meta, free, weights, kept, read, scratch, extra=()):
    operands = (meta, *free, *weights, *read, *kept)
    first = len(operands) - len(kept)
    return pl.pallas_call(
        body,
        out_shape=tuple(jax.ShapeDtypeStruct(v.shape, v.dtype) for v in (*free, *extra))
        + tuple(pltpu.VMEM(v.shape, v.dtype) for v in kept),
        in_specs=[SMEM] + [VMEM] * (len(operands) - 1),
        out_specs=tuple(VMEM for _ in range(len(free) + len(extra) + len(kept))),
        scratch_shapes=scratch,
        input_output_aliases={first + i: len(free) + len(extra) + i for i in range(len(kept))},
        compiler_params=pltpu.CompilerParams(vmem_limit_bytes=LIMIT),
        name=name,
    )(*operands)


def shards(features, index, table, exponent, weights, cotangent):
    here = lax.axis_index("section")
    micro, _, length, width = features.shape
    hours = jnp.left_shift(jnp.int32(1), exponent[0])
    onehot = (index[:, :, None] == jnp.arange(table.shape[0], dtype=jnp.int32)).astype(jnp.bfloat16)
    bias = jnp.einsum("mwb,bc->mwc", onehot, table, preferred_element_type=jnp.float32)
    inputs = (features.astype(jnp.float32) + bias[:, :, None, :]).astype(jnp.bfloat16)[:, 0]
    upstream = cotangent[:, 0]
    core = lax.axis_index("core")
    tap = weights[0]
    copies = jnp.broadcast_to(tap[None], (ACROSS,) + tap.shape).reshape(ACROSS * CORES * OWN, width)
    row = lax.all_to_all(copies, ROW, 0, 0, tiled=True)
    own = lax.all_gather(row, DEEP, axis=0, tiled=True)
    other = lax.ppermute(own, "core", [(0, 1), (1, 0)])

    ticks = SECTIONS + micro - 1
    slots = (micro + 1, length, width)
    xs = jnp.zeros(slots, jnp.bfloat16)
    acts = jnp.zeros(slots, jnp.bfloat16)
    zs = jnp.zeros(slots, jnp.float32)
    dzs = jnp.zeros(slots, jnp.bfloat16)
    scratch = [pltpu.VMEM((length, width), jnp.float32)]

    def slot_of(order):
        return jnp.where(jnp.logical_and(order >= 0, order < micro), order, micro)

    def meta_of(ahead, behind):
        parts = [slot_of(ahead - here), hours, core, slot_of(behind - (SECTIONS - 1 - here))]
        return jnp.stack(parts).astype(jnp.int32)

    upward = [(i, i + 1) for i in range(SECTIONS - 1)]
    downward = [(i + 1, i) for i in range(SECTIONS - 1)]

    block = inputs[0]
    grad = upstream[0]
    near = settle((own,), inputs) + settle((other,), inputs)
    for tick in range(ticks + SECTIONS - 1):
        behind = tick - (SECTIONS - 1)
        meta = meta_of(tick, behind)
        if 0 < tick < micro:
            block = jnp.where(here == 0, inputs[tick], block)
        if 0 < behind < micro:
            grad = jnp.where(here == SECTIONS - 1, upstream[behind], grad)
        if behind < 0:
            block, xs, zs, acts = run(forward_body, "layer_forward", meta, (block,), near, (xs, zs, acts), (), [])
            lead = block
        elif tick < ticks:
            block, grad, xs, zs, acts, dzs = run(
                turn_body, "layer_turn", meta, (block, grad), near, (xs, zs, acts, dzs), (), scratch
            )
            lead = grad
        elif tick == ticks + SECTIONS - 2:
            turned = jax.ShapeDtypeStruct((width, micro * length), jnp.bfloat16)
            grad, turned, dzs = run(
                last_body, "layer_last", meta, (grad,), near, (dzs,), (xs, zs), scratch, (turned,)
            )
        else:
            grad, dzs = run(backward_body, "layer_backward", meta, (grad,), near, (dzs,), (xs, zs), scratch)
            lead = grad
        if tick < ticks + SECTIONS - 2:
            near = settle((own, other), lead)
        if tick < ticks - 1:
            block = lax.ppermute(block, "section", upward)
        if 0 <= behind and tick < ticks + SECTIONS - 2:
            grad = lax.ppermute(grad, "section", downward)
        if tick == ticks + 1:
            every, grad = lax.optimization_barrier((every, grad))
            every = lax.all_gather(every, ROW, axis=0, tiled=False)
        if tick == ticks - 1:
            done = acts[:micro]
            depth = lax.axis_index("zl")
            turns = [[(i, (i + k) % LOW) for i in range(LOW)] for k in range(LOW)]
            moved = [done] + [lax.ppermute(done, "zl", turns[k]) for k in range(1, LOW)]
            every = jnp.stack(
                [
                    jnp.where(depth == j, moved[0], jnp.where((depth - j) % LOW == 1, moved[1], moved[2]))
                    for j in range(LOW)
                ]
            )

    members = LOW * ACROSS * CORES
    piece = width // members
    theirs = lax.all_to_all(turned, ROW + ("zl",), 0, 0, tiled=True)
    partial = weight_partials(meta, theirs, every.reshape(members * micro * length, width))
    both = lax.all_to_all(partial, "core", 0, 0, tiled=True).transpose(1, 0, 2, 3)
    spread = lax.all_to_all(both, DEEP + ("x",), 0, 0, tiled=True)
    back = jnp.sum(spread.reshape(HIGH, members * OWN, 2 * piece).astype(jnp.float32), axis=0)
    back = back.reshape(LOW, ACROSS * CORES, OWN, 2, piece)
    owned = back.transpose(3, 2, 1, 0, 4).reshape(2, OWN, width)
    return owned[None]


def solution(mesh):
    fine = Mesh(mesh.devices.reshape(SECTIONS, HIGH, LOW, ACROSS, CORES), ("section",) + SHARD)
    placed = (
        P(None, SHARD, None, None),
        P(None, SHARD),
        P(),
        P("section"),
        P("section", None, SHARD, None),
        P(None, SHARD, None, None),
    )
    return jax.shard_map(
        shards, mesh=fine, in_specs=placed, out_specs=P("section", None, SHARD, None), check_vma=False
    )
```

profile of v0, /device:TPU:24, one launch (start us, length us, event | category | flops | bytes accessed | tf_op | source)
XLA Modules:
  0.0 378.0 jit_solution(14250808480592500398)
XLA Ops:
  7.5 13.1 %all_to_all.33 = bf16[8,16,1536]{2,1,0:T(8,128)(2,1)} all-to-all(bf16[8,16,1536]{2,1,0:T(8,128)(2,1)S(1)} %bitcast.70), channel_id=1, replica_groups=mesh['section'=8,'zh'=4,'zl'=3,'x'=4,'core'=2] {'x','core'}, dimensions={0} | all-to-all | bytes 786432 | tf_op jit(solution)/shard_map/all_to_all | solution.py:213
  20.7 74.3 %all-gather.4.cloned.1.call-done.refs_0_ = bf16[1536,1536]{1,0:T(8,128)(2,1)} async-done(((bf16[128,1536]{1,0:T(8,128)(2,1)}), bf16[1536,1536]{1,0:T(8,128)(2,1)}) %all-gather.4.cloned.1.call-update) | async-done | bytes 4718608 | tf_op jit(solution)/shard_map/all_gather | solution.py:214
  95.0 1.9 collective-permute-start
  100.7 2.3 settle.17.own_ref
  103.1 2.1 collective-permute-done.refs_0_.refs_1_
  105.2 2.3 settle.18.other_ref
  107.7 2.5 layer_forward.7
  110.2 4.6 %collective-permute-start.1 = (bf16[64,1536]{1,0:T(8,128)(2,1)S(1)}, bf16[64,1536]{1,0:T(8,128)(2,1)S(1)}, u32[]{:S(2)}, u32[]{:S(2)}) collective-permute-start(bf16[64,1536]{1,0:T(8,128)(2,1)S(1)} %get-tuple-element.89.refs_2_), channel_id=1, source_target_pairs={{0,96},{96,192},{192,288},{288,384},{384,480},{480,576},{576,672},... | collective-permute-start | bytes 589832 | tf_op jit(solution)/shard_map/ppermute | solution.py:264
  114.9 3.8 %settle.19 = (bf16[1536,1536]{1,0:T(8,128)(2,1)S(1)}, bf16[1536,1536]{1,0:T(8,128)(2,1)S(1)}) custom-call(bf16[1536,1536]{1,0:T(8,128)(2,1)} %all-gather.4.cloned.1.call-done.refs_0_, bf16[1536,1536]{1,0:T(8,128)(2,1)} %collective-permute-done.refs_0_.refs_1_, bf16[64,1536]{1,0:T(8,128)(2,1)S(1)} %get-tuple-element.89.refs_2_), custom_call_target="tpu_custom_call" | custom-call | bytes 37748736 | tf_op jit(solution)/shard_map/settle/pallas_call | solution.py:46
  119.3 2.5 layer_forward.8
  121.8 5.6 %collective-permute-start.2 = (bf16[64,1536]{1,0:T(8,128)(2,1)S(1)}, bf16[64,1536]{1,0:T(8,128)(2,1)S(1)}, u32[]{:S(2)}, u32[]{:S(2)}) collective-permute-start(bf16[64,1536]{1,0:T(8,128)(2,1)S(1)} %get-tuple-element.95.refs_2_), channel_id=1, source_target_pairs={{0,96},{96,192},{192,288},{288,384},{384,480},{480,576},{576,672},... | collective-permute-start | bytes 589832 | tf_op jit(solution)/shard_map/ppermute | solution.py:264
  127.5 3.8 %settle.20 = (bf16[1536,1536]{1,0:T(8,128)(2,1)S(1)}, bf16[1536,1536]{1,0:T(8,128)(2,1)S(1)}) custom-call(bf16[1536,1536]{1,0:T(8,128)(2,1)} %all-gather.4.cloned.1.call-done.refs_0_, bf16[1536,1536]{1,0:T(8,128)(2,1)} %collective-permute-done.refs_0_.refs_1_, bf16[64,1536]{1,0:T(8,128)(2,1)S(1)} %get-tuple-element.95.refs_2_), custom_call_target="tpu_custom_call" | custom-call | bytes 37748736 | tf_op jit(solution)/shard_map/settle/pallas_call | solution.py:46
  131.3 2.5 layer_forward.9
  133.8 5.3 %collective-permute-start.3 = (bf16[64,1536]{1,0:T(8,128)(2,1)S(1)}, bf16[64,1536]{1,0:T(8,128)(2,1)S(1)}, u32[]{:S(2)}, u32[]{:S(2)}) collective-permute-start(bf16[64,1536]{1,0:T(8,128)(2,1)S(1)} %get-tuple-element.101.refs_2_), channel_id=1, source_target_pairs={{0,96},{96,192},{192,288},{288,384},{384,480},{480,576},{576,672},... | collective-permute-start | bytes 589832 | tf_op jit(solution)/shard_map/ppermute | solution.py:264
  139.2 3.8 %settle.21 = (bf16[1536,1536]{1,0:T(8,128)(2,1)S(1)}, bf16[1536,1536]{1,0:T(8,128)(2,1)S(1)}) custom-call(bf16[1536,1536]{1,0:T(8,128)(2,1)} %all-gather.4.cloned.1.call-done.refs_0_, bf16[1536,1536]{1,0:T(8,128)(2,1)} %collective-permute-done.refs_0_.refs_1_, bf16[64,1536]{1,0:T(8,128)(2,1)S(1)} %get-tuple-element.101.refs_2_), custom_call_target="tpu_custom_call" | custom-call | bytes 37748736 | tf_op jit(solution)/shard_map/settle/pallas_call | solution.py:46
  143.0 2.5 layer_forward.10
  145.5 4.9 %collective-permute-start.4 = (bf16[64,1536]{1,0:T(8,128)(2,1)S(1)}, bf16[64,1536]{1,0:T(8,128)(2,1)S(1)}, u32[]{:S(2)}, u32[]{:S(2)}) collective-permute-start(bf16[64,1536]{1,0:T(8,128)(2,1)S(1)} %get-tuple-element.107.refs_2_), channel_id=1, source_target_pairs={{0,96},{96,192},{192,288},{288,384},{384,480},{480,576},{576,672},... | collective-permute-start | bytes 589832 | tf_op jit(solution)/shard_map/ppermute | solution.py:264
  150.5 3.8 %settle.22 = (bf16[1536,1536]{1,0:T(8,128)(2,1)S(1)}, bf16[1536,1536]{1,0:T(8,128)(2,1)S(1)}) custom-call(bf16[1536,1536]{1,0:T(8,128)(2,1)} %all-gather.4.cloned.1.call-done.refs_0_, bf16[1536,1536]{1,0:T(8,128)(2,1)} %collective-permute-done.refs_0_.refs_1_, bf16[64,1536]{1,0:T(8,128)(2,1)S(1)} %get-tuple-element.107.refs_2_), custom_call_target="tpu_custom_call" | custom-call | bytes 37748736 | tf_op jit(solution)/shard_map/settle/pallas_call | solution.py:46
  154.3 2.5 layer_forward.11
  156.7 4.9 %collective-permute-start.5 = (bf16[64,1536]{1,0:T(8,128)(2,1)S(1)}, bf16[64,1536]{1,0:T(8,128)(2,1)S(1)}, u32[]{:S(2)}, u32[]{:S(2)}) collective-permute-start(bf16[64,1536]{1,0:T(8,128)(2,1)S(1)} %get-tuple-element.113.refs_2_), channel_id=1, source_target_pairs={{0,96},{96,192},{192,288},{288,384},{384,480},{480,576},{576,672},... | collective-permute-start | bytes 589832 | tf_op jit(solution)/shard_map/ppermute | solution.py:264
  161.7 3.8 %settle.23 = (bf16[1536,1536]{1,0:T(8,128)(2,1)S(1)}, bf16[1536,1536]{1,0:T(8,128)(2,1)S(1)}) custom-call(bf16[1536,1536]{1,0:T(8,128)(2,1)} %all-gather.4.cloned.1.call-done.refs_0_, bf16[1536,1536]{1,0:T(8,128)(2,1)} %collective-permute-done.refs_0_.refs_1_, bf16[64,1536]{1,0:T(8,128)(2,1)S(1)} %get-tuple-element.113.refs_2_), custom_call_target="tpu_custom_call" | custom-call | bytes 37748736 | tf_op jit(solution)/shard_map/settle/pallas_call | solution.py:46
  165.5 2.5 layer_forward.12
  168.0 4.9 %collective-permute-start.6 = (bf16[64,1536]{1,0:T(8,128)(2,1)S(1)}, bf16[64,1536]{1,0:T(8,128)(2,1)S(1)}, u32[]{:S(2)}, u32[]{:S(2)}) collective-permute-start(bf16[64,1536]{1,0:T(8,128)(2,1)S(1)} %get-tuple-element.119.refs_2_), channel_id=1, source_target_pairs={{0,96},{96,192},{192,288},{288,384},{384,480},{480,576},{576,672},... | collective-permute-start | bytes 589832 | tf_op jit(solution)/shard_map/ppermute | solution.py:264
  173.0 3.8 %settle.24 = (bf16[1536,1536]{1,0:T(8,128)(2,1)S(1)}, bf16[1536,1536]{1,0:T(8,128)(2,1)S(1)}) custom-call(bf16[1536,1536]{1,0:T(8,128)(2,1)} %all-gather.4.cloned.1.call-done.refs_0_, bf16[1536,1536]{1,0:T(8,128)(2,1)} %collective-permute-done.refs_0_.refs_1_, bf16[64,1536]{1,0:T(8,128)(2,1)S(1)} %get-tuple-element.119.refs_2_), custom_call_target="tpu_custom_call" | custom-call | bytes 37748736 | tf_op jit(solution)/shard_map/settle/pallas_call | solution.py:46
  176.8 2.5 layer_forward.13
  179.3 5.0 %collective-permute-start.7 = (bf16[64,1536]{1,0:T(8,128)(2,1)S(1)}, bf16[64,1536]{1,0:T(8,128)(2,1)S(1)}, u32[]{:S(2)}, u32[]{:S(2)}) collective-permute-start(bf16[64,1536]{1,0:T(8,128)(2,1)S(1)} %get-tuple-element.125.refs_2_), channel_id=1, source_target_pairs={{0,96},{96,192},{192,288},{288,384},{384,480},{480,576},{576,672},... | collective-permute-start | bytes 589832 | tf_op jit(solution)/shard_map/ppermute | solution.py:264
  184.4 3.8 %settle.25 = (bf16[1536,1536]{1,0:T(8,128)(2,1)S(1)}, bf16[1536,1536]{1,0:T(8,128)(2,1)S(1)}) custom-call(bf16[1536,1536]{1,0:T(8,128)(2,1)} %all-gather.4.cloned.1.call-done.refs_0_, bf16[1536,1536]{1,0:T(8,128)(2,1)} %collective-permute-done.refs_0_.refs_1_, bf16[64,1536]{1,0:T(8,128)(2,1)S(1)} %get-tuple-element.125.refs_2_), custom_call_target="tpu_custom_call" | custom-call | bytes 37748736 | tf_op jit(solution)/shard_map/settle/pallas_call | solution.py:46
  188.3 5.6 %layer_turn.2 = (bf16[64,1536]{1,0:T(8,128)(2,1)S(1)}, bf16[64,1536]{1,0:T(8,128)(2,1)S(1)}, bf16[3,64,1536]{2,1,0:T(8,128)(2,1)S(1)}, f32[3,64,1536]{2,1,0:T(8,...) custom-call(s32[4]{0:T(128)S(1)} %pad_add_fusion.6.meta, ...), custom_call_target="tpu_custom_call", output_to_operand_aliasing={{2}: (5, {}), {3}: (6, {}), {4}: (7, {}), {5}: (8, {})} | custom-call | tf_op jit(solution)/shard_map/layer_turn/pallas_call | solution.py:189
  196.6 5.3 %collective-permute-start.8 = (bf16[64,1536]{1,0:T(8,128)(2,1)}, bf16[64,1536]{1,0:T(8,128)(2,1)S(1)}, u32[]{:S(2)}, u32[]{:S(2)}) collective-permute-start(bf16[64,1536]{1,0:T(8,128)(2,1)} %copy-done.2), channel_id=1, source_target_pairs={{0,96},{96,192},{192,288},{288,384},{384,480},{480,576},{576,672},... | collective-permute-start | bytes 589832 | tf_op jit(solution)/shard_map/ppermute | solution.py:264
  201.9 3.8 %settle.26 = (bf16[1536,1536]{1,0:T(8,128)(2,1)S(1)}, bf16[1536,1536]{1,0:T(8,128)(2,1)S(1)}) custom-call(bf16[1536,1536]{1,0:T(8,128)(2,1)} %all-gather.4.cloned.1.call-done.refs_0_, bf16[1536,1536]{1,0:T(8,128)(2,1)} %collective-permute-done.refs_0_.refs_1_, bf16[64,1536]{1,0:T(8,128)(2,1)S(1)} %get-tuple-element.132.refs_2_), custom_call_target="tpu_custom_call" | custom-call | bytes 37748736 | tf_op jit(solution)/shard_map/settle/pallas_call | solution.py:46
  205.7 5.5 %layer_turn.3 = (bf16[64,1536]{1,0:T(8,128)(2,1)}, bf16[64,1536]{1,0:T(8,128)(2,1)S(1)}, bf16[3,64,1536]{2,1,0:T(8,128)(2,1)S(1)}, f32[3,64,1536]{2,1,0:T(8,128)...) custom-call(s32[4]{0:T(128)S(1)} %pad_add_fusion.5.meta, ...), custom_call_target="tpu_custom_call", output_to_operand_aliasing={{2}: (5, {}), {3}: (6, {}), {4}: (7, {}), {5}: (8, {})} | custom-call | tf_op jit(solution)/shard_map/layer_turn/pallas_call | solution.py:189
  211.3 1.9 collective-permute-start.12
  214.0 3.0 collective-permute-start.10
  217.0 3.7 collective-permute-start.11
  220.8 3.8 %settle.27 = (bf16[1536,1536]{1,0:T(8,128)(2,1)S(1)}, bf16[1536,1536]{1,0:T(8,128)(2,1)S(1)}) custom-call(bf16[1536,1536]{1,0:T(8,128)(2,1)} %all-gather.4.cloned.1.call-done.refs_0_, bf16[1536,1536]{1,0:T(8,128)(2,1)} %collective-permute-done.refs_0_.refs_1_, bf16[64,1536]{1,0:T(8,128)(2,1)S(1)} %get-tuple-element.140.refs_2_), custom_call_target="tpu_custom_call" | custom-call | bytes 37748736 | tf_op jit(solution)/shard_map/settle/pallas_call | solution.py:46
  224.6 3.7 layer_backward.6
  228.3 1.9 collective-permute-start.13
  230.4 3.8 %settle.28 = (bf16[1536,1536]{1,0:T(8,128)(2,1)S(1)}, bf16[1536,1536]{1,0:T(8,128)(2,1)S(1)}) custom-call(bf16[1536,1536]{1,0:T(8,128)(2,1)} %all-gather.4.cloned.1.call-done.refs_0_, bf16[1536,1536]{1,0:T(8,128)(2,1)} %collective-permute-done.refs_0_.refs_1_, bf16[64,1536]{1,0:T(8,128)(2,1)S(1)} %get-tuple-element.146.refs_2_), custom_call_target="tpu_custom_call" | custom-call | bytes 37748736 | tf_op jit(solution)/shard_map/settle/pallas_call | solution.py:46
  234.2 2.9 collective-permute-done.13.g_ref
  237.1 3.7 layer_backward.7
  240.8 1.9 collective-permute-start.14
  245.1 4.4 %collective-permute-done.14.g_ref = bf16[64,1536]{1,0:T(8,128)(2,1)S(1)} collective-permute-done((bf16[64,1536]{1,0:T(8,128)(2,1)S(1)}, bf16[64,1536]{1,0:T(8,128)(2,1)S(1)}, u32[]{:S(2)}, u32[]{:S(2)}) %collective-permute-start.14) | collective-permute-done | bytes 196640 | tf_op jit(solution)/shard_map/ppermute | solution.py:266
  249.7 3.8 %settle.29 = (bf16[1536,1536]{1,0:T(8,128)(2,1)S(1)}, bf16[1536,1536]{1,0:T(8,128)(2,1)S(1)}) custom-call(bf16[1536,1536]{1,0:T(8,128)(2,1)} %all-gather.4.cloned.1.call-done.refs_0_, bf16[1536,1536]{1,0:T(8,128)(2,1)} %collective-permute-done.refs_0_.refs_1_, bf16[64,1536]{1,0:T(8,128)(2,1)S(1)} %get-tuple-element.150.refs_2_), custom_call_target="tpu_custom_call" | custom-call | bytes 37748736 | tf_op jit(solution)/shard_map/settle/pallas_call | solution.py:46
  253.5 3.6 layer_backward.8
  257.1 2.1 collective-permute-start.15
  259.3 3.8 %settle.30 = (bf16[1536,1536]{1,0:T(8,128)(2,1)S(1)}, bf16[1536,1536]{1,0:T(8,128)(2,1)S(1)}) custom-call(bf16[1536,1536]{1,0:T(8,128)(2,1)} %all-gather.4.cloned.1.call-done.refs_0_, bf16[1536,1536]{1,0:T(8,128)(2,1)} %collective-permute-done.refs_0_.refs_1_, bf16[64,1536]{1,0:T(8,128)(2,1)S(1)} %get-tuple-element.155.refs_2_), custom_call_target="tpu_custom_call" | custom-call | bytes 37748736 | tf_op jit(solution)/shard_map/settle/pallas_call | solution.py:46
  263.1 4.6 %collective-permute-done.15.g_ref = bf16[64,1536]{1,0:T(8,128)(2,1)S(1)} collective-permute-done((bf16[64,1536]{1,0:T(8,128)(2,1)S(1)}, bf16[64,1536]{1,0:T(8,128)(2,1)S(1)}, u32[]{:S(2)}, u32[]{:S(2)}) %collective-permute-start.15) | collective-permute-done | bytes 196640 | tf_op jit(solution)/shard_map/ppermute | solution.py:266
  267.7 3.6 layer_backward.9
  271.3 1.9 collective-permute-start.16
  273.3 4.0 %settle.31 = (bf16[1536,1536]{1,0:T(8,128)(2,1)S(1)}, bf16[1536,1536]{1,0:T(8,128)(2,1)S(1)}) custom-call(bf16[1536,1536]{1,0:T(8,128)(2,1)} %all-gather.4.cloned.1.call-done.refs_0_, bf16[1536,1536]{1,0:T(8,128)(2,1)} %collective-permute-done.refs_0_.refs_1_, bf16[64,1536]{1,0:T(8,128)(2,1)S(1)} %get-tuple-element.159.refs_2_), custom_call_target="tpu_custom_call" | custom-call | bytes 37748736 | tf_op jit(solution)/shard_map/settle/pallas_call | solution.py:46
  277.3 4.0 %collective-permute-done.16.g_ref = bf16[64,1536]{1,0:T(8,128)(2,1)S(1)} collective-permute-done((bf16[64,1536]{1,0:T(8,128)(2,1)S(1)}, bf16[64,1536]{1,0:T(8,128)(2,1)S(1)}, u32[]{:S(2)}, u32[]{:S(2)}) %collective-permute-start.16) | collective-permute-done | bytes 196640 | tf_op jit(solution)/shard_map/ppermute | solution.py:266
  281.4 3.6 layer_backward.10
  285.0 1.9 collective-permute-start.17
  287.0 4.0 %settle.32 = (bf16[1536,1536]{1,0:T(8,128)(2,1)S(1)}, bf16[1536,1536]{1,0:T(8,128)(2,1)S(1)}) custom-call(bf16[1536,1536]{1,0:T(8,128)(2,1)} %all-gather.4.cloned.1.call-done.refs_0_, bf16[1536,1536]{1,0:T(8,128)(2,1)} %collective-permute-done.refs_0_.refs_1_, bf16[64,1536]{1,0:T(8,128)(2,1)S(1)} %get-tuple-element.163.refs_2_), custom_call_target="tpu_custom_call" | custom-call | bytes 37748736 | tf_op jit(solution)/shard_map/settle/pallas_call | solution.py:46
  291.0 3.3 collective-permute-done.17.g_ref
  294.3 3.6 layer_backward.11
  297.9 1.9 collective-permute-start.18
  299.9 3.9 %settle.33 = (bf16[1536,1536]{1,0:T(8,128)(2,1)S(1)}, bf16[1536,1536]{1,0:T(8,128)(2,1)S(1)}) custom-call(bf16[1536,1536]{1,0:T(8,128)(2,1)} %all-gather.4.cloned.1.call-done.refs_0_, bf16[1536,1536]{1,0:T(8,128)(2,1)} %collective-permute-done.refs_0_.refs_1_, bf16[64,1536]{1,0:T(8,128)(2,1)S(1)} %get-tuple-element.167.refs_2_), custom_call_target="tpu_custom_call" | custom-call | bytes 37748736 | tf_op jit(solution)/shard_map/settle/pallas_call | solution.py:46
  303.8 2.9 collective-permute-done.18.g_ref
  306.7 4.3 %layer_last.1 = (bf16[64,1536]{1,0:T(8,128)(2,1)}, bf16[1536,128]{1,0:T(8,128)(2,1)S(1)}, bf16[3,64,1536]{2,1,0:T(8,128)(2,1)S(1)}) custom-call(s32[4]{0:T(128)S(1)} %pad_add_fusion.meta, bf16[64,1536]{1,0:T(8,128)(2,1)S(1)} %collective-permute-done.18.g_ref, bf16[1536,1536]{1,0:T(8,128)(2,1)S(1)} %get-tuple-element.168.own_ref, ...), custom_call_target="tpu_custom_call", output_to_operand_aliasing={{2}: (6, {})} | custom-call | tf_op jit(solution)/shard_map/layer_last/pallas_call | solution.py:189
  311.0 16.5 %all_to_all.34 = bf16[24,64,128]{2,1,0:T(8,128)(2,1)S(1)} all-to-all(bf16[24,64,128]{2,1,0:T(8,128)(2,1)S(1)} %bitcast.64), channel_id=1, replica_groups=mesh['section'=8,'zh'=4,'zl'=3,'x'=4,'core'=2] {'x','core','zl'}, dimensions={0} | all-to-all | bytes 786432 | tf_op jit(solution)/shard_map/all_to_all | solution.py:284
  327.5 5.0 %weight_partials.1 = bf16[2,48,16,128]{3,2,1,0:T(8,128)(2,1)S(1)} custom-call(s32[4]{0:T(128)S(1)} %pad_add_fusion.meta, bf16[1536,128]{1,0:T(8,128)(2,1)S(1)} %bitcast.63, bf16[3072,1536]{1,0:T(8,128)(2,1)} %bitcast.65), custom_call_target="tpu_custom_call" | custom-call | tf_op jit(solution)/shard_map/weight_partials/pallas_call | solution.py:158
  332.5 4.0 %all_to_all.35 = bf16[2,48,16,128]{3,2,1,0:T(8,128)(2,1)S(1)} all-to-all(bf16[2,48,16,128]{3,2,1,0:T(8,128)(2,1)S(1)} %weight_partials.1), channel_id=1, replica_groups=mesh['section'=8,'zh'=4,'zl'=3,'x'=4,'core'=2] {'core'}, dimensions={0} | all-to-all | bytes 786432 | tf_op jit(solution)/shard_map/all_to_all | solution.py:286
  336.6 33.0 %all_to_all.36 = bf16[48,2,16,128]{3,2,1,0:T(8,128)(2,1)S(1)} all-to-all(bf16[48,2,16,128]{3,2,1,0:T(8,128)(2,1)S(1)} %copy.45), channel_id=1, replica_groups=mesh['section'=8,'zh'=4,'zl'=3,'x'=4,'core'=2] {'zh','zl','x'}, dimensions={0} | all-to-all | bytes 786432 | tf_op jit(solution)/shard_map/all_to_all | solution.py:287
  (64 shorter events, 13.6 us)
Async XLA Ops:
  6.5 91.1 %copy-start = (bf16[128,1536]{1,0:T(8,128)(2,1)S(1)}, bf16[128,1536]{1,0:T(8,128)(2,1)}, u32[]{:S(2)}) copy-start(bf16[128,1536]{1,0:T(8,128)(2,1)} %param.8) | copy-start | bytes 1179652
  6.5 88.5 %all-gather.4.cloned.1.call-start = ((), (), s32[]{:S(2)}) async-start(), calls=%async_computation.4 | async-start | bytes 5111808 | tf_op jit(solution)/shard_map/all_gather | solution.py:214
  20.7 306.8 %all-gather.6.cloned.1.call-start = ((), (), s32[]{:S(2)}) async-start(), calls=%async_computation.5 | async-start | bytes 10616832 | tf_op jit(solution)/shard_map/all_gather | solution.py:269
  95.0 10.1 %collective-permute-start = (bf16[1536,1536]{1,0:T(8,128)(2,1)}, bf16[1536,1536]{1,0:T(8,128)(2,1)}, u32[]{:S(2)}, u32[]{:S(2)}) collective-permute-start(bf16[1536,1536]{1,0:T(8,128)(2,1)} %all-gather.4.cloned.1.call-done.refs_0_), channel_id=1, source_target_pairs={{0,1},{1,0},{2,3},{3,2},{4,5},{5,4},{6,7},{7,6},{8,9},{9,8},{10,11... | collective-permute-start | bytes 14155784 | tf_op jit(solution)/shard_map/ppermute | solution.py:215
  110.2 9.1 %collective-permute-start.1 = (bf16[64,1536]{1,0:T(8,128)(2,1)S(1)}, bf16[64,1536]{1,0:T(8,128)(2,1)S(1)}, u32[]{:S(2)}, u32[]{:S(2)}) collective-permute-start(bf16[64,1536]{1,0:T(8,128)(2,1)S(1)} %get-tuple-element.89.refs_2_), channel_id=1, source_target_pairs={{0,96},{96,192},{192,288},{288,384},{384,480},{480,576},{576,672},... | collective-permute-start | bytes 589832 | tf_op jit(solution)/shard_map/ppermute | solution.py:264
  121.8 9.5 %collective-permute-start.2 = (bf16[64,1536]{1,0:T(8,128)(2,1)S(1)}, bf16[64,1536]{1,0:T(8,128)(2,1)S(1)}, u32[]{:S(2)}, u32[]{:S(2)}) collective-permute-start(bf16[64,1536]{1,0:T(8,128)(2,1)S(1)} %get-tuple-element.95.refs_2_), channel_id=1, source_target_pairs={{0,96},{96,192},{192,288},{288,384},{384,480},{480,576},{576,672},... | collective-permute-start | bytes 589832 | tf_op jit(solution)/shard_map/ppermute | solution.py:264
  133.8 9.2 %collective-permute-start.3 = (bf16[64,1536]{1,0:T(8,128)(2,1)S(1)}, bf16[64,1536]{1,0:T(8,128)(2,1)S(1)}, u32[]{:S(2)}, u32[]{:S(2)}) collective-permute-start(bf16[64,1536]{1,0:T(8,128)(2,1)S(1)} %get-tuple-element.101.refs_2_), channel_id=1, source_target_pairs={{0,96},{96,192},{192,288},{288,384},{384,480},{480,576},{576,672},... | collective-permute-start | bytes 589832 | tf_op jit(solution)/shard_map/ppermute | solution.py:264
  145.5 8.8 %collective-permute-start.4 = (bf16[64,1536]{1,0:T(8,128)(2,1)S(1)}, bf16[64,1536]{1,0:T(8,128)(2,1)S(1)}, u32[]{:S(2)}, u32[]{:S(2)}) collective-permute-start(bf16[64,1536]{1,0:T(8,128)(2,1)S(1)} %get-tuple-element.107.refs_2_), channel_id=1, source_target_pairs={{0,96},{96,192},{192,288},{288,384},{384,480},{480,576},{576,672},... | collective-permute-start | bytes 589832 | tf_op jit(solution)/shard_map/ppermute | solution.py:264
  156.7 8.8 %collective-permute-start.5 = (bf16[64,1536]{1,0:T(8,128)(2,1)S(1)}, bf16[64,1536]{1,0:T(8,128)(2,1)S(1)}, u32[]{:S(2)}, u32[]{:S(2)}) collective-permute-start(bf16[64,1536]{1,0:T(8,128)(2,1)S(1)} %get-tuple-element.113.refs_2_), channel_id=1, source_target_pairs={{0,96},{96,192},{192,288},{288,384},{384,480},{480,576},{576,672},... | collective-permute-start | bytes 589832 | tf_op jit(solution)/shard_map/ppermute | solution.py:264
  168.0 8.8 %collective-permute-start.6 = (bf16[64,1536]{1,0:T(8,128)(2,1)S(1)}, bf16[64,1536]{1,0:T(8,128)(2,1)S(1)}, u32[]{:S(2)}, u32[]{:S(2)}) collective-permute-start(bf16[64,1536]{1,0:T(8,128)(2,1)S(1)} %get-tuple-element.119.refs_2_), channel_id=1, source_target_pairs={{0,96},{96,192},{192,288},{288,384},{384,480},{480,576},{576,672},... | collective-permute-start | bytes 589832 | tf_op jit(solution)/shard_map/ppermute | solution.py:264
  176.8 7.5 %copy-start.3 = (bf16[2,1,64,1536]{3,2,1,0:T(8,128)(2,1)S(1)}, bf16[2,1,64,1536]{3,2,1,0:T(8,128)(2,1)}, u32[]{:S(2)}) copy-start(bf16[2,1,64,1536]{3,2,1,0:T(8,128)(2,1)} %param.11) | copy-start | bytes 1179652
  179.3 9.0 %collective-permute-start.7 = (bf16[64,1536]{1,0:T(8,128)(2,1)S(1)}, bf16[64,1536]{1,0:T(8,128)(2,1)S(1)}, u32[]{:S(2)}, u32[]{:S(2)}) collective-permute-start(bf16[64,1536]{1,0:T(8,128)(2,1)S(1)} %get-tuple-element.125.refs_2_), channel_id=1, source_target_pairs={{0,96},{96,192},{192,288},{288,384},{384,480},{480,576},{576,672},... | collective-permute-start | bytes 589832 | tf_op jit(solution)/shard_map/ppermute | solution.py:264
  193.9 0.7 copy-start.2
  194.6 11.1 %collective-permute-start.9 = (bf16[64,1536]{1,0:T(8,128)(2,1)S(1)}, bf16[64,1536]{1,0:T(8,128)(2,1)S(1)}, u32[]{:S(2)}, u32[]{:S(2)}) collective-permute-start(bf16[64,1536]{1,0:T(8,128)(2,1)S(1)} %get-tuple-element.132.refs_2_), channel_id=1, source_target_pairs={{96,0},{192,96},{288,192},{384,288},{480,384},{576,480},{672,576},... | collective-permute-start | bytes 589832 | tf_op jit(solution)/shard_map/ppermute | solution.py:266
  196.6 9.1 %copy-start.4 = (bf16[2,1,64,1536]{3,2,1,0:T(8,128)(2,1)S(1)}, bf16[2,1,64,1536]{3,2,1,0:T(8,128)(2,1)}, u32[]{:S(2)}) copy-start(bf16[2,1,64,1536]{3,2,1,0:T(8,128)(2,1)} %param.11) | copy-start | bytes 1179652
  196.6 9.1 %collective-permute-start.8 = (bf16[64,1536]{1,0:T(8,128)(2,1)}, bf16[64,1536]{1,0:T(8,128)(2,1)S(1)}, u32[]{:S(2)}, u32[]{:S(2)}) collective-permute-start(bf16[64,1536]{1,0:T(8,128)(2,1)} %copy-done.2), channel_id=1, source_target_pairs={{0,96},{96,192},{192,288},{288,384},{384,480},{480,576},{576,672},... | collective-permute-start | bytes 589832 | tf_op jit(solution)/shard_map/ppermute | solution.py:264
  211.3 13.4 %collective-permute-start.12 = (bf16[64,1536]{1,0:T(8,128)(2,1)S(1)}, bf16[64,1536]{1,0:T(8,128)(2,1)S(1)}, u32[]{:S(2)}, u32[]{:S(2)}) collective-permute-start(bf16[64,1536]{1,0:T(8,128)(2,1)S(1)} %get-tuple-element.140.refs_2_), channel_id=1, source_target_pairs={{96,0},{192,96},{288,192},{384,288},{480,384},{576,480},{672,576},... | collective-permute-start | bytes 589832 | tf_op jit(solution)/shard_map/ppermute | solution.py:266
  214.0 28.7 %collective-permute-start.10 = (bf16[2,64,1536]{2,1,0:T(8,128)(2,1)}, bf16[2,64,1536]{2,1,0:T(8,128)(2,1)}, u32[]{:S(2)}, u32[]{:S(2)}) collective-permute-start(bf16[2,64,1536]{2,1,0:T(8,128)(2,1)} %slice.23), channel_id=1, source_target_pairs={{0,8},{8,16},{16,0},{1,9},{9,17},{17,1},{2,10},{10,18},{18,2},{3,1... | collective-permute-start | bytes 1179656 | tf_op jit(solution)/shard_map/ppermute | solution.py:274
  217.0 25.7 %collective-permute-start.11 = (bf16[2,64,1536]{2,1,0:T(8,128)(2,1)}, bf16[2,64,1536]{2,1,0:T(8,128)(2,1)}, u32[]{:S(2)}, u32[]{:S(2)}) collective-permute-start(bf16[2,64,1536]{2,1,0:T(8,128)(2,1)} %slice.23), channel_id=1, source_target_pairs={{0,16},{8,0},{16,8},{1,17},{9,1},{17,9},{2,18},{10,2},{18,10},{3,1... | collective-permute-start | bytes 1179656 | tf_op jit(solution)/shard_map/ppermute | solution.py:274
  228.3 8.8 %collective-permute-start.13 = (bf16[64,1536]{1,0:T(8,128)(2,1)S(1)}, bf16[64,1536]{1,0:T(8,128)(2,1)S(1)}, u32[]{:S(2)}, u32[]{:S(2)}) collective-permute-start(bf16[64,1536]{1,0:T(8,128)(2,1)S(1)} %get-tuple-element.146.refs_2_), channel_id=1, source_target_pairs={{96,0},{192,96},{288,192},{384,288},{480,384},{576,480},{672,576},... | collective-permute-start | bytes 589832 | tf_op jit(solution)/shard_map/ppermute | solution.py:266
  240.8 8.8 %collective-permute-start.14 = (bf16[64,1536]{1,0:T(8,128)(2,1)S(1)}, bf16[64,1536]{1,0:T(8,128)(2,1)S(1)}, u32[]{:S(2)}, u32[]{:S(2)}) collective-permute-start(bf16[64,1536]{1,0:T(8,128)(2,1)S(1)} %get-tuple-element.150.refs_2_), channel_id=1, source_target_pairs={{96,0},{192,96},{288,192},{384,288},{480,384},{576,480},{672,576},... | collective-permute-start | bytes 589832 | tf_op jit(solution)/shard_map/ppermute | solution.py:266
  257.1 10.6 %collective-permute-start.15 = (bf16[64,1536]{1,0:T(8,128)(2,1)S(1)}, bf16[64,1536]{1,0:T(8,128)(2,1)S(1)}, u32[]{:S(2)}, u32[]{:S(2)}) collective-permute-start(bf16[64,1536]{1,0:T(8,128)(2,1)S(1)} %get-tuple-element.155.refs_2_), channel_id=1, source_target_pairs={{96,0},{192,96},{288,192},{384,288},{480,384},{576,480},{672,576},... | collective-permute-start | bytes 589832 | tf_op jit(solution)/shard_map/ppermute | solution.py:266
  271.3 10.0 %collective-permute-start.16 = (bf16[64,1536]{1,0:T(8,128)(2,1)S(1)}, bf16[64,1536]{1,0:T(8,128)(2,1)S(1)}, u32[]{:S(2)}, u32[]{:S(2)}) collective-permute-start(bf16[64,1536]{1,0:T(8,128)(2,1)S(1)} %get-tuple-element.159.refs_2_), channel_id=1, source_target_pairs={{96,0},{192,96},{288,192},{384,288},{480,384},{576,480},{672,576},... | collective-permute-start | bytes 589832 | tf_op jit(solution)/shard_map/ppermute | solution.py:266
  285.0 9.3 %collective-permute-start.17 = (bf16[64,1536]{1,0:T(8,128)(2,1)S(1)}, bf16[64,1536]{1,0:T(8,128)(2,1)S(1)}, u32[]{:S(2)}, u32[]{:S(2)}) collective-permute-start(bf16[64,1536]{1,0:T(8,128)(2,1)S(1)} %get-tuple-element.163.refs_2_), channel_id=1, source_target_pairs={{96,0},{192,96},{288,192},{384,288},{480,384},{576,480},{672,576},... | collective-permute-start | bytes 589832 | tf_op jit(solution)/shard_map/ppermute | solution.py:266
  297.9 8.8 %collective-permute-start.18 = (bf16[64,1536]{1,0:T(8,128)(2,1)S(1)}, bf16[64,1536]{1,0:T(8,128)(2,1)S(1)}, u32[]{:S(2)}, u32[]{:S(2)}) collective-permute-start(bf16[64,1536]{1,0:T(8,128)(2,1)S(1)} %get-tuple-element.167.refs_2_), channel_id=1, source_target_pairs={{96,0},{192,96},{288,192},{384,288},{480,384},{576,480},{672,576},... | collective-permute-start | bytes 589832 | tf_op jit(solution)/shard_map/ppermute | solution.py:266
  327.5 43.6 %copy-start.1 = (bf16[128,1536]{1,0:T(8,128)(2,1)S(1)}, bf16[128,1536]{1,0:T(8,128)(2,1)}, u32[]{:S(2)}) copy-start(bf16[128,1536]{1,0:T(8,128)(2,1)} %param.8) | copy-start | bytes 1179652
Sparse Core Ops, SparseCore 0:
  20.8 74.1 all-gather.3
  249.7 61.2 all-gather.5
where the time goes:
time: 379 us; the launch traced here: 378 us
  Pallas kernels  122 us (32%)
  waiting for transfers between devices  99.1 us (26%)
  blocking collectives  66.7 us (18%)
  starting transfers between devices  64.6 us (17%)
  between operations  14.9 us (4%)
  other arithmetic  5.86 us (2%)
  local copies, waits for them, and re-layouts  4.28 us (1%)
    all_gather x1, waiting for transfers between devices, shards(): own = lax.all_gather(row, DEEP, axis=0, tiled=True)  74.3 us
    pallas_call x17, Pallas kernels, settle(): pl.pallas_call(settle_body, out_shape=tuple((pltpu.VMEM(v.shape, v.dtype)...  62.1 us
    pallas_call x16, Pallas kernels, run(): pl.pallas_call(body, out_shape=tuple((jax.ShapeDtypeStruct(v.shape, v.dty...  54.6 us
    ppermute x8, starting transfers between devices, shards(): block = lax.ppermute(block, 'section', upward)  40.4 us
    all_to_all x1, blocking collectives, shards(): spread = lax.all_to_all(both, DEEP + ('x',), 0, 0, tiled=True)  33 us
    ppermute x8, waiting for transfers between devices, shards(): grad = lax.ppermute(grad, 'section', downward)  22.1 us
    all_to_all x1, blocking collectives, shards(): theirs = lax.all_to_all(turned, ROW + ('zl',), 0, 0, tiled=True)  16.5 us
    ppermute x8, starting transfers between devices, shards(): grad = lax.ppermute(grad, 'section', downward)  15.6 us
  transfers between devices with their start and end apart: 21, of which 9 were waited for; matrix products, arithmetic and copies ran while one was open for 2% of the time, Pallas kernels for 23%

commit v1 on v0

--- a/solution.py
+++ b/solution.py
@@ -9,6 +9,7 @@
 OWN = 16
 BLOCK = 256
 CHUNKS = 4
+NEAR = 768
 LIMIT = 20 * 1024 * 1024
 SHARD = ("zh", "zl", "x", "core")
 DEEP = ("zh", "zl")
@@ -32,20 +33,25 @@
 def settle_body(*refs):
     count = (len(refs) - 2) // 2
     sems = refs[-1]
-    copies = [
-        pltpu.make_async_copy(refs[i], refs[count + 1 + i], sems.at[i]) for i in range(count)
-    ]
+    copies = []
+    for i in range(count):
+        source, target = refs[i], refs[count + 1 + i]
+        if source.shape != target.shape:
+            source = source.at[:, : target.shape[1]]
+        copies.append(pltpu.make_async_copy(source, target, sems.at[i]))
     for copy in copies:
         copy.start()
     for copy in copies:
         copy.wait()
 
 
-def settle(arrays, after):
+def settle(arrays, after, widths=None):
     size = sum(v.size * v.dtype.itemsize for v in arrays)
     return pl.pallas_call(
         settle_body,
-        out_shape=tuple(pltpu.VMEM(v.shape, v.dtype) for v in arrays),
+        out_shape=tuple(
+            pltpu.VMEM((v.shape[0], w), v.dtype) for v, w in zip(arrays, widths or [v.shape[1] for v in arrays])
+        ),
         in_specs=[pl.BlockSpec(memory_space=pltpu.HBM)] * len(arrays) + [pl.BlockSpec(memory_space=pl.ANY)],
         out_specs=tuple(VMEM for _ in arrays),
         scratch_shapes=[pltpu.SemaphoreType.DMA((len(arrays),))],
@@ -62,8 +68,13 @@
     return first, second
 
 
-def forward_part(meta, x_ref, own_ref, other_ref, x_out, xs, zs, acts):
+def forward_part(meta, x_ref, own_ref, other_ref, x_out, xs, zs, acts, rest=None):
     slot = meta[0]
+    near = other_ref.shape[1]
+    if rest is not None:
+        far_ref, buffer, sem = rest
+        fetch = pltpu.make_async_copy(far_ref.at[:, near:], buffer, sem)
+        fetch.start()
     x_full = x_ref[...].astype(jnp.float32)
     _, normed = norm_of(x_full)
     rounded = normed.astype(jnp.bfloat16)
@@ -74,7 +85,13 @@
     for start in range(0, x_ref.shape[1], BLOCK):
         cols = slice(start, start + BLOCK)
         pre = jnp.dot(first, own_ref[:, cols], preferred_element_type=jnp.float32)
-        pre += jnp.dot(second, other_ref[:, cols], preferred_element_type=jnp.float32)
+        if start == near:
+            fetch.wait()
+        if start < near:
+            tile = other_ref[:, cols]
+        else:
+            tile = buffer[:, start - near : start - near + BLOCK]
+        pre += jnp.dot(second, tile, preferred_element_type=jnp.float32)
         zs[slot, :, cols] = pre
         x_out[:, cols] = (x_ref[:, cols].astype(jnp.float32) + pre * jax.nn.sigmoid(pre)).astype(jnp.bfloat16)
 
@@ -100,9 +117,11 @@
     g_out[...] = (g_ref[...].astype(jnp.float32) + inverse * (d_norm - normed * mean)).astype(jnp.bfloat16)
 
 
-def forward_body(meta, x_ref, own_ref, other_ref, keep_x, keep_z, keep_a, x_out, xs, zs, acts):
+def forward_body(
+    meta, x_ref, own_ref, other_ref, far_ref, keep_x, keep_z, keep_a, x_out, xs, zs, acts, buffer, sem
+):
     del keep_x, keep_z, keep_a
-    forward_part(meta, x_ref, own_ref, other_ref, x_out, xs, zs, acts)
+    forward_part(meta, x_ref, own_ref, other_ref, x_out, xs, zs, acts, (far_ref, buffer, sem))
 
 
 def backward_body(meta, g_ref, own_ref, other_ref, xs, zs, keep_d, g_out, dzs, da):
@@ -135,11 +154,10 @@
         lanes = slice(source * 2 * length, (source + 1) * 2 * length)
         sides[:piece, lanes] = current[span].astype(jnp.bfloat16)
         sides[piece:, lanes] = moved[span].astype(jnp.bfloat16)
-    chips = BLOCK // (CORES * OWN)
     for index in range(CHUNKS):
         copies[index].wait()
         span = slice(index * depth, (index + 1) * depth)
-        for block, start in enumerate(range(0, every.shape[1], BLOCK)):
+        for start in range(0, every.shape[1], BLOCK):
             cols = slice(start, start + BLOCK)
             part = jnp.dot(sides[:, span], every[span, cols], preferred_element_type=jnp.float32)
             if index > 0:
@@ -147,9 +165,7 @@
             if index < CHUNKS - 1:
                 total[:, cols] = part
                 continue
-            part = part.T.reshape(chips, CORES, OWN, 2 * piece).astype(jnp.bfloat16)
-            for core in range(CORES):
-                out[core, block * chips : (block + 1) * chips] = part[:, core]
+            out[cols, :] = part.T.astype(jnp.bfloat16)
 
 
 def weight_partials(meta, turned, every):
@@ -157,7 +173,7 @@
     piece = width * turned.shape[1] // tokens
     return pl.pallas_call(
         weights_body,
-        out_shape=jax.ShapeDtypeStruct((CORES, width // (CORES * OWN), OWN, 2 * piece), jnp.bfloat16),
+        out_shape=jax.ShapeDtypeStruct((width, 2 * piece), jnp.bfloat16),
         in_specs=[SMEM, VMEM, pl.BlockSpec(memory_space=pltpu.HBM)],
         out_specs=VMEM,
         scratch_shapes=[
@@ -181,16 +197,20 @@
 
 VMEM = pl.BlockSpec(memory_space=pltpu.VMEM)
 SMEM = pl.BlockSpec(memory_space=pltpu.SMEM)
-
-
-def run(body, name, meta, free, weights, kept, read, scratch, extra=()):
+HBM = pl.BlockSpec(memory_space=pltpu.HBM)
+
+
+def run(body, name, meta, free, weights, kept, read, scratch, extra=(), far=None):
     operands = (meta, *free, *weights, *read, *kept)
     first = len(operands) - len(kept)
     return pl.pallas_call(
         body,
         out_shape=tuple(jax.ShapeDtypeStruct(v.shape, v.dtype) for v in (*free, *extra))
         + tuple(pltpu.VMEM(v.shape, v.dtype) for v in kept),
-        in_specs=[SMEM] + [VMEM] * (len(operands) - 1),
+        in_specs=[SMEM]
+        + [VMEM] * (len(free) + len(weights))
+        + [far or VMEM] * len(read)
+        + [VMEM] * len(kept),
         out_specs=tuple(VMEM for _ in range(len(free) + len(extra) + len(kept))),
         scratch_shapes=scratch,
         input_output_aliases={first + i: len(free) + len(extra) + i for i in range(len(kept))},
@@ -221,6 +241,7 @@
     zs = jnp.zeros(slots, jnp.float32)
     dzs = jnp.zeros(slots, jnp.bfloat16)
     scratch = [pltpu.VMEM((length, width), jnp.float32)]
+    streams = [pltpu.VMEM((width, width - NEAR), jnp.bfloat16), pltpu.SemaphoreType.DMA]
 
     def slot_of(order):
         return jnp.where(jnp.logical_and(order >= 0, order < micro), order, micro)
@@ -234,7 +255,7 @@
 
     block = inputs[0]
     grad = upstream[0]
-    near = settle((own,), inputs) + settle((other,), inputs)
+    near = settle((own,), inputs) + settle((other,), inputs, (NEAR,))
     for tick in range(ticks + SECTIONS - 1):
         behind = tick - (SECTIONS - 1)
         meta = meta_of(tick, behind)
@@ -243,7 +264,10 @@
         if 0 < behind < micro:
             grad = jnp.where(here == SECTIONS - 1, upstream[behind], grad)
         if behind < 0:
-            block, xs, zs, acts = run(forward_body, "layer_forward", meta, (block,), near, (xs, zs, acts), (), [])
+            far = pltpu.with_memory_space_constraint(other, pltpu.HBM)
+            block, xs, zs, acts = run(
+                forward_body, "layer_forward", meta, (block,), near, (xs, zs, acts), (far,), streams, far=HBM
+            )
             lead = block
         elif tick < ticks:
             block, grad, xs, zs, acts, dzs = run(
@@ -259,7 +283,8 @@
             grad, dzs = run(backward_body, "layer_backward", meta, (grad,), near, (dzs,), (xs, zs), scratch)
             lead = grad
         if tick < ticks + SECTIONS - 2:
-            near = settle((own, other), lead)
+            part = NEAR if behind < -1 else width
+            near = settle((own, other), lead, (width, part))
         if tick < ticks - 1:
             block = lax.ppermute(block, "section", upward)
         if 0 <= behind and tick < ticks + SECTIONS - 2:
@@ -283,11 +308,11 @@
     piece = width // members
     theirs = lax.all_to_all(turned, ROW + ("zl",), 0, 0, tiled=True)
     partial = weight_partials(meta, theirs, every.reshape(members * micro * length, width))
-    both = lax.all_to_all(partial, "core", 0, 0, tiled=True).transpose(1, 0, 2, 3)
-    spread = lax.all_to_all(both, DEEP + ("x",), 0, 0, tiled=True)
-    back = jnp.sum(spread.reshape(HIGH, members * OWN, 2 * piece).astype(jnp.float32), axis=0)
-    back = back.reshape(LOW, ACROSS * CORES, OWN, 2, piece)
-    owned = back.transpose(3, 2, 1, 0, 4).reshape(2, OWN, width)
+    spread = lax.all_to_all(partial, DEEP, 0, 0, tiled=True)
+    total = jnp.sum(spread.reshape(HIGH, LOW * ACROSS * CORES * OWN, 2 * piece).astype(jnp.float32), axis=0)
+    total = total.reshape(LOW, ACROSS * CORES, OWN, 2 * piece).transpose(1, 0, 2, 3)
+    back = lax.all_to_all(total, ROW, 0, 0, tiled=True).reshape(ACROSS * CORES, LOW, OWN, 2, piece)
+    owned = back.transpose(3, 2, 0, 1, 4).reshape(2, OWN, width)
     return owned[None]
 
 

time: 379 us -> 387 us (1.021)
    pallas_call x16, Pallas kernels: 54.6 us -> 62.5 us  [run(): pl.pallas_call(body, out_shape=tuple((jax.ShapeDtypeStruct(v.shape, v.dty...]
    pallas_call x18, Pallas kernels: 67 us -> 62.3 us  [the longest x17 57.4 us: settle(): pl.pallas_call(settle_body, out_shape=tuple((pltpu.VMEM((v.shape[0], w),...]
  transfers between devices with their start and end apart: 21 -> 21, of which waited for: 9 -> 10; matrix products, arithmetic and copies ran while one was open for 2% -> 2% of each run, Pallas kernels for 23% -> 21%
where the time goes in v1:
time: 387 us; the launch traced here: 386 us
  Pallas kernels  125 us (32%)
  waiting for transfers between devices  100 us (26%)
  blocking collectives  67.8 us (18%)
  starting transfers between devices  67.4 us (17%)
  between operations  14.9 us (4%)
  other arithmetic  5.86 us (2%)
  local copies, waits for them, and re-layouts  4.27 us (1%)
    all_gather x1, waiting for transfers between devices, shards(): own = lax.all_gather(row, DEEP, axis=0, tiled=True)  74.3 us
    pallas_call x16, Pallas kernels, run(): pl.pallas_call(body, out_shape=tuple((jax.ShapeDtypeStruct(v.shape, v.dty...  62.5 us
    pallas_call x17, Pallas kernels, settle(): pl.pallas_call(settle_body, out_shape=tuple((pltpu.VMEM((v.shape[0], w),...  57.4 us
    ppermute x8, starting transfers between devices, shards(): block = lax.ppermute(block, 'section', upward)  43.2 us
    all_to_all x1, blocking collectives, shards(): spread = lax.all_to_all(partial, DEEP, 0, 0, tiled=True)  28.9 us
    ppermute x8, waiting for transfers between devices, shards(): grad = lax.ppermute(grad, 'section', downward)  22.1 us
    all_to_all x1, blocking collectives, shards(): theirs = lax.all_to_all(turned, ROW + ('zl',), 0, 0, tiled=True)  16.5 us
    ppermute x8, starting transfers between devices, shards(): grad = lax.ppermute(grad, 'section', downward)  15.6 us
  transfers between devices with their start and end apart: 21, of which 10 were waited for; matrix products, arithmetic and copies ran while one was open for 2% of the time, Pallas kernels for 21%

profile of v1, /device:TPU:24, one launch (start us, length us, event | category | flops | bytes accessed | tf_op | source)
XLA Modules:
  0.0 386.1 jit_solution(13452266389254449726)
XLA Ops:
  7.5 13.1 %all_to_all.37 = bf16[8,16,1536]{2,1,0:T(8,128)(2,1)} all-to-all(bf16[8,16,1536]{2,1,0:T(8,128)(2,1)S(1)} %bitcast.77), channel_id=1, replica_groups=mesh['section'=8,'zh'=4,'zl'=3,'x'=4,'core'=2] {'x','core'}, dimensions={0} | all-to-all | bytes 786432 | tf_op jit(solution)/shard_map/all_to_all | solution.py:233
  20.7 74.3 %all-gather.4.cloned.1.call-done.refs_0_ = bf16[1536,1536]{1,0:T(8,128)(2,1)} async-done(((bf16[128,1536]{1,0:T(8,128)(2,1)}), bf16[1536,1536]{1,0:T(8,128)(2,1)}) %all-gather.4.cloned.1.call-update) | async-done | bytes 4718608 | tf_op jit(solution)/shard_map/all_gather | solution.py:234
  95.0 1.9 collective-permute-start
  100.7 2.3 settle.17.own_ref
  103.1 2.1 collective-permute-done.refs_0_.far_ref.refs_1_
  107.1 3.6 layer_forward.7
  110.7 4.6 %collective-permute-start.1 = (bf16[64,1536]{1,0:T(8,128)(2,1)S(1)}, bf16[64,1536]{1,0:T(8,128)(2,1)S(1)}, u32[]{:S(2)}, u32[]{:S(2)}) collective-permute-start(bf16[64,1536]{1,0:T(8,128)(2,1)S(1)} %get-tuple-element.89.refs_2_), channel_id=1, source_target_pairs={{0,96},{96,192},{192,288},{288,384},{384,480},{480,576},{576,672},... | collective-permute-start | bytes 589832 | tf_op jit(solution)/shard_map/ppermute | solution.py:289
  115.4 3.1 settle.19
  119.8 3.6 layer_forward.8
  123.4 5.6 %collective-permute-start.2 = (bf16[64,1536]{1,0:T(8,128)(2,1)S(1)}, bf16[64,1536]{1,0:T(8,128)(2,1)S(1)}, u32[]{:S(2)}, u32[]{:S(2)}) collective-permute-start(bf16[64,1536]{1,0:T(8,128)(2,1)S(1)} %get-tuple-element.95.refs_2_), channel_id=1, source_target_pairs={{0,96},{96,192},{192,288},{288,384},{384,480},{480,576},{576,672},... | collective-permute-start | bytes 589832 | tf_op jit(solution)/shard_map/ppermute | solution.py:289
  129.1 3.1 settle.20
  132.6 3.6 layer_forward.9
  136.2 5.6 %collective-permute-start.3 = (bf16[64,1536]{1,0:T(8,128)(2,1)S(1)}, bf16[64,1536]{1,0:T(8,128)(2,1)S(1)}, u32[]{:S(2)}, u32[]{:S(2)}) collective-permute-start(bf16[64,1536]{1,0:T(8,128)(2,1)S(1)} %get-tuple-element.101.refs_2_), channel_id=1, source_target_pairs={{0,96},{96,192},{192,288},{288,384},{384,480},{480,576},{576,672},... | collective-permute-start | bytes 589832 | tf_op jit(solution)/shard_map/ppermute | solution.py:289
  141.9 3.1 settle.21
  145.0 3.6 layer_forward.10
  148.7 5.5 %collective-permute-start.4 = (bf16[64,1536]{1,0:T(8,128)(2,1)S(1)}, bf16[64,1536]{1,0:T(8,128)(2,1)S(1)}, u32[]{:S(2)}, u32[]{:S(2)}) collective-permute-start(bf16[64,1536]{1,0:T(8,128)(2,1)S(1)} %get-tuple-element.107.refs_2_), channel_id=1, source_target_pairs={{0,96},{96,192},{192,288},{288,384},{384,480},{480,576},{576,672},... | collective-permute-start | bytes 589832 | tf_op jit(solution)/shard_map/ppermute | solution.py:289
  154.3 3.1 settle.22
  157.4 3.6 layer_forward.11
  161.0 5.5 %collective-permute-start.5 = (bf16[64,1536]{1,0:T(8,128)(2,1)S(1)}, bf16[64,1536]{1,0:T(8,128)(2,1)S(1)}, u32[]{:S(2)}, u32[]{:S(2)}) collective-permute-start(bf16[64,1536]{1,0:T(8,128)(2,1)S(1)} %get-tuple-element.113.refs_2_), channel_id=1, source_target_pairs={{0,96},{96,192},{192,288},{288,384},{384,480},{480,576},{576,672},... | collective-permute-start | bytes 589832 | tf_op jit(solution)/shard_map/ppermute | solution.py:289
  166.7 3.1 settle.23
  169.8 3.6 layer_forward.12
  173.4 5.7 %collective-permute-start.6 = (bf16[64,1536]{1,0:T(8,128)(2,1)S(1)}, bf16[64,1536]{1,0:T(8,128)(2,1)S(1)}, u32[]{:S(2)}, u32[]{:S(2)}) collective-permute-start(bf16[64,1536]{1,0:T(8,128)(2,1)S(1)} %get-tuple-element.119.refs_2_), channel_id=1, source_target_pairs={{0,96},{96,192},{192,288},{288,384},{384,480},{480,576},{576,672},... | collective-permute-start | bytes 589832 | tf_op jit(solution)/shard_map/ppermute | solution.py:289
  179.2 3.1 settle.24
  182.4 3.6 layer_forward.13
  186.0 5.3 %collective-permute-start.7 = (bf16[64,1536]{1,0:T(8,128)(2,1)S(1)}, bf16[64,1536]{1,0:T(8,128)(2,1)S(1)}, u32[]{:S(2)}, u32[]{:S(2)}) collective-permute-start(bf16[64,1536]{1,0:T(8,128)(2,1)S(1)} %get-tuple-element.125.refs_2_), channel_id=1, source_target_pairs={{0,96},{96,192},{192,288},{288,384},{384,480},{480,576},{576,672},... | collective-permute-start | bytes 589832 | tf_op jit(solution)/shard_map/ppermute | solution.py:289
  191.5 3.8 settle.25
  195.3 5.6 %layer_turn.2 = (bf16[64,1536]{1,0:T(8,128)(2,1)S(1)}, bf16[64,1536]{1,0:T(8,128)(2,1)S(1)}, bf16[3,64,1536]{2,1,0:T(8,128)(2,1)S(1)}, f32[3,64,1536]{2,1,0:T(8,...) custom-call(s32[4]{0:T(128)S(1)} %pad_add_fusion.6.meta, ...), custom_call_target="tpu_custom_call", output_to_operand_aliasing={{2}: (5, {}), {3}: (6, {}), {4}: (7, {}), {5}: (8, {})} | custom-call | tf_op jit(solution)/shard_map/layer_turn/pallas_call | solution.py:206
  201.6 1.9 collective-permute-start.9
  203.7 5.3 %collective-permute-start.8 = (bf16[64,1536]{1,0:T(8,128)(2,1)}, bf16[64,1536]{1,0:T(8,128)(2,1)S(1)}, u32[]{:S(2)}, u32[]{:S(2)}) collective-permute-start(bf16[64,1536]{1,0:T(8,128)(2,1)} %copy-done.2), channel_id=1, source_target_pairs={{0,96},{96,192},{192,288},{288,384},{384,480},{480,576},{576,672},... | collective-permute-start | bytes 589832 | tf_op jit(solution)/shard_map/ppermute | solution.py:289
  208.9 3.8 settle.26
  212.8 5.5 %layer_turn.3 = (bf16[64,1536]{1,0:T(8,128)(2,1)}, bf16[64,1536]{1,0:T(8,128)(2,1)S(1)}, bf16[3,64,1536]{2,1,0:T(8,128)(2,1)S(1)}, f32[3,64,1536]{2,1,0:T(8,128)...) custom-call(s32[4]{0:T(128)S(1)} %pad_add_fusion.5.meta, ...), custom_call_target="tpu_custom_call", output_to_operand_aliasing={{2}: (5, {}), {3}: (6, {}), {4}: (7, {}), {5}: (8, {})} | custom-call | tf_op jit(solution)/shard_map/layer_turn/pallas_call | solution.py:206
  218.3 1.9 collective-permute-start.12
  221.0 3.0 collective-permute-start.10
  224.1 3.7 collective-permute-start.11
  227.9 3.8 settle.27
  231.7 3.7 layer_backward.6
  235.3 1.9 collective-permute-start.13
  237.4 3.8 settle.28
  241.2 2.9 collective-permute-done.13.g_ref
  244.1 3.7 layer_backward.7
  247.8 2.1 collective-permute-start.14
  252.4 4.2 %collective-permute-done.14.g_ref = bf16[64,1536]{1,0:T(8,128)(2,1)S(1)} collective-permute-done((bf16[64,1536]{1,0:T(8,128)(2,1)S(1)}, bf16[64,1536]{1,0:T(8,128)(2,1)S(1)}, u32[]{:S(2)}, u32[]{:S(2)}) %collective-permute-start.14) | collective-permute-done | bytes 196640 | tf_op jit(solution)/shard_map/ppermute | solution.py:291
  256.7 3.8 settle.29
  260.5 3.6 layer_backward.8
  264.1 1.9 collective-permute-start.15
  266.1 3.8 settle.30
  269.9 4.8 %collective-permute-done.15.g_ref = bf16[64,1536]{1,0:T(8,128)(2,1)S(1)} collective-permute-done((bf16[64,1536]{1,0:T(8,128)(2,1)S(1)}, bf16[64,1536]{1,0:T(8,128)(2,1)S(1)}, u32[]{:S(2)}, u32[]{:S(2)}) %collective-permute-start.15) | collective-permute-done | bytes 196640 | tf_op jit(solution)/shard_map/ppermute | solution.py:291
  274.7 3.6 layer_backward.9
  278.3 1.9 collective-permute-start.16
  280.4 4.0 %settle.31 = (bf16[1536,1536]{1,0:T(8,128)(2,1)S(1)}, bf16[1536,1536]{1,0:T(8,128)(2,1)S(1)}) custom-call(bf16[1536,1536]{1,0:T(8,128)(2,1)} %all-gather.4.cloned.1.call-done.refs_0_, bf16[1536,1536]{1,0:T(8,128)(2,1)} %collective-permute-done.refs_0_.far_ref.refs_1_, bf16[64,1536]{1,0:T(8,128)(2,1)S(1)} %get-tuple-element.159.refs_2_), custom_call_target="tpu_custom_call" | custom-call | bytes 37748736 | tf_op jit(solution)/shard_map/settle/pallas_call | solution.py:50
  284.3 4.0 %collective-permute-done.16.g_ref = bf16[64,1536]{1,0:T(8,128)(2,1)S(1)} collective-permute-done((bf16[64,1536]{1,0:T(8,128)(2,1)S(1)}, bf16[64,1536]{1,0:T(8,128)(2,1)S(1)}, u32[]{:S(2)}, u32[]{:S(2)}) %collective-permute-start.16) | collective-permute-done | bytes 196640 | tf_op jit(solution)/shard_map/ppermute | solution.py:291
  288.4 3.6 layer_backward.10
  292.0 1.9 collective-permute-start.17
  294.0 4.0 %settle.32 = (bf16[1536,1536]{1,0:T(8,128)(2,1)S(1)}, bf16[1536,1536]{1,0:T(8,128)(2,1)S(1)}) custom-call(bf16[1536,1536]{1,0:T(8,128)(2,1)} %all-gather.4.cloned.1.call-done.refs_0_, bf16[1536,1536]{1,0:T(8,128)(2,1)} %collective-permute-done.refs_0_.far_ref.refs_1_, bf16[64,1536]{1,0:T(8,128)(2,1)S(1)} %get-tuple-element.163.refs_2_), custom_call_target="tpu_custom_call" | custom-call | bytes 37748736 | tf_op jit(solution)/shard_map/settle/pallas_call | solution.py:50
  298.0 3.3 collective-permute-done.17.g_ref
  301.3 3.6 layer_backward.11
  304.9 1.9 collective-permute-start.18
  307.0 3.9 %settle.33 = (bf16[1536,1536]{1,0:T(8,128)(2,1)S(1)}, bf16[1536,1536]{1,0:T(8,128)(2,1)S(1)}) custom-call(bf16[1536,1536]{1,0:T(8,128)(2,1)} %all-gather.4.cloned.1.call-done.refs_0_, bf16[1536,1536]{1,0:T(8,128)(2,1)} %collective-permute-done.refs_0_.far_ref.refs_1_, bf16[64,1536]{1,0:T(8,128)(2,1)S(1)} %get-tuple-element.167.refs_2_), custom_call_target="tpu_custom_call" | custom-call | bytes 37748736 | tf_op jit(solution)/shard_map/settle/pallas_call | solution.py:50
  310.9 2.9 collective-permute-done.18.g_ref
  313.7 4.3 %layer_last.1 = (bf16[64,1536]{1,0:T(8,128)(2,1)}, bf16[1536,128]{1,0:T(8,128)(2,1)S(1)}, bf16[3,64,1536]{2,1,0:T(8,128)(2,1)S(1)}) custom-call(s32[4]{0:T(128)S(1)} %pad_add_fusion.meta, bf16[64,1536]{1,0:T(8,128)(2,1)S(1)} %collective-permute-done.18.g_ref, bf16[1536,1536]{1,0:T(8,128)(2,1)S(1)} %get-tuple-element.168.own_ref, ...), custom_call_target="tpu_custom_call", output_to_operand_aliasing={{2}: (6, {})} | custom-call | tf_op jit(solution)/shard_map/layer_last/pallas_call | solution.py:206
  318.0 16.5 %all_to_all.38 = bf16[24,64,128]{2,1,0:T(8,128)(2,1)S(1)} all-to-all(bf16[24,64,128]{2,1,0:T(8,128)(2,1)S(1)} %bitcast.72), channel_id=1, replica_groups=mesh['section'=8,'zh'=4,'zl'=3,'x'=4,'core'=2] {'x','core','zl'}, dimensions={0} | all-to-all | bytes 786432 | tf_op jit(solution)/shard_map/all_to_all | solution.py:309
  334.6 5.0 %weight_partials.1 = bf16[1536,128]{1,0:T(8,128)(2,1)S(1)} custom-call(s32[4]{0:T(128)S(1)} %pad_add_fusion.meta, bf16[1536,128]{1,0:T(8,128)(2,1)S(1)} %bitcast.70, bf16[3072,1536]{1,0:T(8,128)(2,1)} %bitcast.73), custom_call_target="tpu_custom_call" | custom-call | tf_op jit(solution)/shard_map/weight_partials/pallas_call | solution.py:174
  339.6 28.9 %all_to_all.39 = bf16[12,128,128]{2,1,0:T(8,128)(2,1)S(1)} all-to-all(bf16[12,128,128]{2,1,0:T(8,128)(2,1)S(1)} %bitcast.71), channel_id=1, replica_groups=mesh['section'=8,'zh'=4,'zl'=3,'x'=4,'core'=2] {'zh','zl'}, dimensions={0} | all-to-all | bytes 786432 | tf_op jit(solution)/shard_map/all_to_all | solution.py:311
  368.5 9.3 %all_to_all.40 = f32[8,3,16,128]{3,2,1,0:T(8,128)S(1)} all-to-all(f32[8,3,16,128]{3,2,1,0:T(8,128)S(1)} %copy.46), channel_id=1, replica_groups=mesh['section'=8,'zh'=4,'zl'=3,'x'=4,'core'=2] {'x','core'}, dimensions={0} | all-to-all | bytes 393216 | tf_op jit(solution)/shard_map/all_to_all | solution.py:314
  (64 shorter events, 14.4 us)
Async XLA Ops:
  6.5 91.1 %copy-start = (bf16[128,1536]{1,0:T(8,128)(2,1)S(1)}, bf16[128,1536]{1,0:T(8,128)(2,1)}, u32[]{:S(2)}) copy-start(bf16[128,1536]{1,0:T(8,128)(2,1)} %param.8) | copy-start | bytes 1179652
  6.5 88.5 %all-gather.4.cloned.1.call-start = ((), (), s32[]{:S(2)}) async-start(), calls=%async_computation.4 | async-start | bytes 5111808 | tf_op jit(solution)/shard_map/all_gather | solution.py:234
  20.7 313.9 %all-gather.6.cloned.1.call-start = ((), (), s32[]{:S(2)}) async-start(), calls=%async_computation.5 | async-start | bytes 10616832 | tf_op jit(solution)/shard_map/all_gather | solution.py:294
  95.0 10.1 %collective-permute-start = (bf16[1536,1536]{1,0:T(8,128)(2,1)}, bf16[1536,1536]{1,0:T(8,128)(2,1)}, u32[]{:S(2)}, u32[]{:S(2)}) collective-permute-start(bf16[1536,1536]{1,0:T(8,128)(2,1)} %all-gather.4.cloned.1.call-done.refs_0_), channel_id=1, source_target_pairs={{0,1},{1,0},{2,3},{3,2},{4,5},{5,4},{6,7},{7,6},{8,9},{9,8},{10,11... | collective-permute-start | bytes 14155784 | tf_op jit(solution)/shard_map/ppermute | solution.py:235
  110.7 9.1 %collective-permute-start.1 = (bf16[64,1536]{1,0:T(8,128)(2,1)S(1)}, bf16[64,1536]{1,0:T(8,128)(2,1)S(1)}, u32[]{:S(2)}, u32[]{:S(2)}) collective-permute-start(bf16[64,1536]{1,0:T(8,128)(2,1)S(1)} %get-tuple-element.89.refs_2_), channel_id=1, source_target_pairs={{0,96},{96,192},{192,288},{288,384},{384,480},{480,576},{576,672},... | collective-permute-start | bytes 589832 | tf_op jit(solution)/shard_map/ppermute | solution.py:289
  123.4 9.2 %collective-permute-start.2 = (bf16[64,1536]{1,0:T(8,128)(2,1)S(1)}, bf16[64,1536]{1,0:T(8,128)(2,1)S(1)}, u32[]{:S(2)}, u32[]{:S(2)}) collective-permute-start(bf16[64,1536]{1,0:T(8,128)(2,1)S(1)} %get-tuple-element.95.refs_2_), channel_id=1, source_target_pairs={{0,96},{96,192},{192,288},{288,384},{384,480},{480,576},{576,672},... | collective-permute-start | bytes 589832 | tf_op jit(solution)/shard_map/ppermute | solution.py:289
  136.2 8.8 %collective-permute-start.3 = (bf16[64,1536]{1,0:T(8,128)(2,1)S(1)}, bf16[64,1536]{1,0:T(8,128)(2,1)S(1)}, u32[]{:S(2)}, u32[]{:S(2)}) collective-permute-start(bf16[64,1536]{1,0:T(8,128)(2,1)S(1)} %get-tuple-element.101.refs_2_), channel_id=1, source_target_pairs={{0,96},{96,192},{192,288},{288,384},{384,480},{480,576},{576,672},... | collective-permute-start | bytes 589832 | tf_op jit(solution)/shard_map/ppermute | solution.py:289
  148.7 8.8 %collective-permute-start.4 = (bf16[64,1536]{1,0:T(8,128)(2,1)S(1)}, bf16[64,1536]{1,0:T(8,128)(2,1)S(1)}, u32[]{:S(2)}, u32[]{:S(2)}) collective-permute-start(bf16[64,1536]{1,0:T(8,128)(2,1)S(1)} %get-tuple-element.107.refs_2_), channel_id=1, source_target_pairs={{0,96},{96,192},{192,288},{288,384},{384,480},{480,576},{576,672},... | collective-permute-start | bytes 589832 | tf_op jit(solution)/shard_map/ppermute | solution.py:289
  161.0 8.8 %collective-permute-start.5 = (bf16[64,1536]{1,0:T(8,128)(2,1)S(1)}, bf16[64,1536]{1,0:T(8,128)(2,1)S(1)}, u32[]{:S(2)}, u32[]{:S(2)}) collective-permute-start(bf16[64,1536]{1,0:T(8,128)(2,1)S(1)} %get-tuple-element.113.refs_2_), channel_id=1, source_target_pairs={{0,96},{96,192},{192,288},{288,384},{384,480},{480,576},{576,672},... | collective-permute-start | bytes 589832 | tf_op jit(solution)/shard_map/ppermute | solution.py:289
  173.4 8.9 %collective-permute-start.6 = (bf16[64,1536]{1,0:T(8,128)(2,1)S(1)}, bf16[64,1536]{1,0:T(8,128)(2,1)S(1)}, u32[]{:S(2)}, u32[]{:S(2)}) collective-permute-start(bf16[64,1536]{1,0:T(8,128)(2,1)S(1)} %get-tuple-element.119.refs_2_), channel_id=1, source_target_pairs={{0,96},{96,192},{192,288},{288,384},{384,480},{480,576},{576,672},... | collective-permute-start | bytes 589832 | tf_op jit(solution)/shard_map/ppermute | solution.py:289
  182.4 9.0 %copy-start.3 = (bf16[2,1,64,1536]{3,2,1,0:T(8,128)(2,1)S(1)}, bf16[2,1,64,1536]{3,2,1,0:T(8,128)(2,1)}, u32[]{:S(2)}) copy-start(bf16[2,1,64,1536]{3,2,1,0:T(8,128)(2,1)} %param.11) | copy-start | bytes 1179652
  186.0 9.3 %collective-permute-start.7 = (bf16[64,1536]{1,0:T(8,128)(2,1)S(1)}, bf16[64,1536]{1,0:T(8,128)(2,1)S(1)}, u32[]{:S(2)}, u32[]{:S(2)}) collective-permute-start(bf16[64,1536]{1,0:T(8,128)(2,1)S(1)} %get-tuple-element.125.refs_2_), channel_id=1, source_target_pairs={{0,96},{96,192},{192,288},{288,384},{384,480},{480,576},{576,672},... | collective-permute-start | bytes 589832 | tf_op jit(solution)/shard_map/ppermute | solution.py:289
  201.0 0.7 copy-start.2
  201.6 11.1 %collective-permute-start.9 = (bf16[64,1536]{1,0:T(8,128)(2,1)S(1)}, bf16[64,1536]{1,0:T(8,128)(2,1)S(1)}, u32[]{:S(2)}, u32[]{:S(2)}) collective-permute-start(bf16[64,1536]{1,0:T(8,128)(2,1)S(1)} %get-tuple-element.132.refs_2_), channel_id=1, source_target_pairs={{96,0},{192,96},{288,192},{384,288},{480,384},{576,480},{672,576},... | collective-permute-start | bytes 589832 | tf_op jit(solution)/shard_map/ppermute | solution.py:291
  203.7 9.1 %copy-start.4 = (bf16[2,1,64,1536]{3,2,1,0:T(8,128)(2,1)S(1)}, bf16[2,1,64,1536]{3,2,1,0:T(8,128)(2,1)}, u32[]{:S(2)}) copy-start(bf16[2,1,64,1536]{3,2,1,0:T(8,128)(2,1)} %param.11) | copy-start | bytes 1179652
  203.7 9.1 %collective-permute-start.8 = (bf16[64,1536]{1,0:T(8,128)(2,1)}, bf16[64,1536]{1,0:T(8,128)(2,1)S(1)}, u32[]{:S(2)}, u32[]{:S(2)}) collective-permute-start(bf16[64,1536]{1,0:T(8,128)(2,1)} %copy-done.2), channel_id=1, source_target_pairs={{0,96},{96,192},{192,288},{288,384},{384,480},{480,576},{576,672},... | collective-permute-start | bytes 589832 | tf_op jit(solution)/shard_map/ppermute | solution.py:289
  218.3 13.4 %collective-permute-start.12 = (bf16[64,1536]{1,0:T(8,128)(2,1)S(1)}, bf16[64,1536]{1,0:T(8,128)(2,1)S(1)}, u32[]{:S(2)}, u32[]{:S(2)}) collective-permute-start(bf16[64,1536]{1,0:T(8,128)(2,1)S(1)} %get-tuple-element.140.refs_2_), channel_id=1, source_target_pairs={{96,0},{192,96},{288,192},{384,288},{480,384},{576,480},{672,576},... | collective-permute-start | bytes 589832 | tf_op jit(solution)/shard_map/ppermute | solution.py:291
  221.0 28.9 %collective-permute-start.10 = (bf16[2,64,1536]{2,1,0:T(8,128)(2,1)}, bf16[2,64,1536]{2,1,0:T(8,128)(2,1)}, u32[]{:S(2)}, u32[]{:S(2)}) collective-permute-start(bf16[2,64,1536]{2,1,0:T(8,128)(2,1)} %slice.23), channel_id=1, source_target_pairs={{0,8},{8,16},{16,0},{1,9},{9,17},{17,1},{2,10},{10,18},{18,2},{3,1... | collective-permute-start | bytes 1179656 | tf_op jit(solution)/shard_map/ppermute | solution.py:299
  224.1 25.9 %collective-permute-start.11 = (bf16[2,64,1536]{2,1,0:T(8,128)(2,1)}, bf16[2,64,1536]{2,1,0:T(8,128)(2,1)}, u32[]{:S(2)}, u32[]{:S(2)}) collective-permute-start(bf16[2,64,1536]{2,1,0:T(8,128)(2,1)} %slice.23), channel_id=1, source_target_pairs={{0,16},{8,0},{16,8},{1,17},{9,1},{17,9},{2,18},{10,2},{18,10},{3,1... | collective-permute-start | bytes 1179656 | tf_op jit(solution)/shard_map/ppermute | solution.py:299
  235.3 8.8 %collective-permute-start.13 = (bf16[64,1536]{1,0:T(8,128)(2,1)S(1)}, bf16[64,1536]{1,0:T(8,128)(2,1)S(1)}, u32[]{:S(2)}, u32[]{:S(2)}) collective-permute-start(bf16[64,1536]{1,0:T(8,128)(2,1)S(1)} %get-tuple-element.146.refs_2_), channel_id=1, source_target_pairs={{96,0},{192,96},{288,192},{384,288},{480,384},{576,480},{672,576},... | collective-permute-start | bytes 589832 | tf_op jit(solution)/shard_map/ppermute | solution.py:291
  247.8 8.8 %collective-permute-start.14 = (bf16[64,1536]{1,0:T(8,128)(2,1)S(1)}, bf16[64,1536]{1,0:T(8,128)(2,1)S(1)}, u32[]{:S(2)}, u32[]{:S(2)}) collective-permute-start(bf16[64,1536]{1,0:T(8,128)(2,1)S(1)} %get-tuple-element.150.refs_2_), channel_id=1, source_target_pairs={{96,0},{192,96},{288,192},{384,288},{480,384},{576,480},{672,576},... | collective-permute-start | bytes 589832 | tf_op jit(solution)/shard_map/ppermute | solution.py:291
  264.1 10.6 %collective-permute-start.15 = (bf16[64,1536]{1,0:T(8,128)(2,1)S(1)}, bf16[64,1536]{1,0:T(8,128)(2,1)S(1)}, u32[]{:S(2)}, u32[]{:S(2)}) collective-permute-start(bf16[64,1536]{1,0:T(8,128)(2,1)S(1)} %get-tuple-element.155.refs_2_), channel_id=1, source_target_pairs={{96,0},{192,96},{288,192},{384,288},{480,384},{576,480},{672,576},... | collective-permute-start | bytes 589832 | tf_op jit(solution)/shard_map/ppermute | solution.py:291
  278.3 10.0 %collective-permute-start.16 = (bf16[64,1536]{1,0:T(8,128)(2,1)S(1)}, bf16[64,1536]{1,0:T(8,128)(2,1)S(1)}, u32[]{:S(2)}, u32[]{:S(2)}) collective-permute-start(bf16[64,1536]{1,0:T(8,128)(2,1)S(1)} %get-tuple-element.159.refs_2_), channel_id=1, source_target_pairs={{96,0},{192,96},{288,192},{384,288},{480,384},{576,480},{672,576},... | collective-permute-start | bytes 589832 | tf_op jit(solution)/shard_map/ppermute | solution.py:291
  292.0 9.3 %collective-permute-start.17 = (bf16[64,1536]{1,0:T(8,128)(2,1)S(1)}, bf16[64,1536]{1,0:T(8,128)(2,1)S(1)}, u32[]{:S(2)}, u32[]{:S(2)}) collective-permute-start(bf16[64,1536]{1,0:T(8,128)(2,1)S(1)} %get-tuple-element.163.refs_2_), channel_id=1, source_target_pairs={{96,0},{192,96},{288,192},{384,288},{480,384},{576,480},{672,576},... | collective-permute-start | bytes 589832 | tf_op jit(solution)/shard_map/ppermute | solution.py:291
  304.9 8.8 %collective-permute-start.18 = (bf16[64,1536]{1,0:T(8,128)(2,1)S(1)}, bf16[64,1536]{1,0:T(8,128)(2,1)S(1)}, u32[]{:S(2)}, u32[]{:S(2)}) collective-permute-start(bf16[64,1536]{1,0:T(8,128)(2,1)S(1)} %get-tuple-element.167.refs_2_), channel_id=1, source_target_pairs={{96,0},{192,96},{288,192},{384,288},{480,384},{576,480},{672,576},... | collective-permute-start | bytes 589832 | tf_op jit(solution)/shard_map/ppermute | solution.py:291
  334.6 44.7 %copy-start.1 = (bf16[128,1536]{1,0:T(8,128)(2,1)S(1)}, bf16[128,1536]{1,0:T(8,128)(2,1)}, u32[]{:S(2)}) copy-start(bf16[128,1536]{1,0:T(8,128)(2,1)} %param.8) | copy-start | bytes 1179652
Sparse Core Ops, SparseCore 0:
  20.8 74.1 all-gather.3
  256.7 61.2 all-gather.5

commit v2 on v0

--- a/solution.py
+++ b/solution.py
@@ -135,11 +135,10 @@
         lanes = slice(source * 2 * length, (source + 1) * 2 * length)
         sides[:piece, lanes] = current[span].astype(jnp.bfloat16)
         sides[piece:, lanes] = moved[span].astype(jnp.bfloat16)
-    chips = BLOCK // (CORES * OWN)
     for index in range(CHUNKS):
         copies[index].wait()
         span = slice(index * depth, (index + 1) * depth)
-        for block, start in enumerate(range(0, every.shape[1], BLOCK)):
+        for start in range(0, every.shape[1], BLOCK):
             cols = slice(start, start + BLOCK)
             part = jnp.dot(sides[:, span], every[span, cols], preferred_element_type=jnp.float32)
             if index > 0:
@@ -147,9 +146,7 @@
             if index < CHUNKS - 1:
                 total[:, cols] = part
                 continue
-            part = part.T.reshape(chips, CORES, OWN, 2 * piece).astype(jnp.bfloat16)
-            for core in range(CORES):
-                out[core, block * chips : (block + 1) * chips] = part[:, core]
+            out[cols, :] = part.T.astype(jnp.bfloat16)
 
 
 def weight_partials(meta, turned, every):
@@ -157,7 +154,7 @@
     piece = width * turned.shape[1] // tokens
     return pl.pallas_call(
         weights_body,
-        out_shape=jax.ShapeDtypeStruct((CORES, width // (CORES * OWN), OWN, 2 * piece), jnp.bfloat16),
+        out_shape=jax.ShapeDtypeStruct((width, 2 * piece), jnp.bfloat16),
         in_specs=[SMEM, VMEM, pl.BlockSpec(memory_space=pltpu.HBM)],
         out_specs=VMEM,
         scratch_shapes=[
@@ -258,33 +255,34 @@
         else:
             grad, dzs = run(backward_body, "layer_backward", meta, (grad,), near, (dzs,), (xs, zs), scratch)
             lead = grad
+        if tick == ticks + 1:
+            every = jnp.stack(
+                [
+                    jnp.where(depth == j, moved[0], jnp.where((depth - j) % LOW == 1, moved[1], moved[2]))
+                    for j in range(LOW)
+                ]
+            )
+            every, lead = lax.optimization_barrier((every, lead))
+            every = lax.all_gather(every, ROW, axis=0, tiled=False)
         if tick < ticks + SECTIONS - 2:
             near = settle((own, other), lead)
         if tick < ticks - 1:
             block = lax.ppermute(block, "section", upward)
         if 0 <= behind and tick < ticks + SECTIONS - 2:
             grad = lax.ppermute(grad, "section", downward)
-        if tick == ticks + 1:
-            every, grad = lax.optimization_barrier((every, grad))
-            every = lax.all_gather(every, ROW, axis=0, tiled=False)
+        if tick == ticks:
+            moved.append(lax.ppermute(done, "zl", turns[2]))
         if tick == ticks - 1:
             done = acts[:micro]
             depth = lax.axis_index("zl")
             turns = [[(i, (i + k) % LOW) for i in range(LOW)] for k in range(LOW)]
-            moved = [done] + [lax.ppermute(done, "zl", turns[k]) for k in range(1, LOW)]
-            every = jnp.stack(
-                [
-                    jnp.where(depth == j, moved[0], jnp.where((depth - j) % LOW == 1, moved[1], moved[2]))
-                    for j in range(LOW)
-                ]
-            )
+            moved = [done, lax.ppermute(done, "zl", turns[1])]
 
     members = LOW * ACROSS * CORES
     piece = width // members
     theirs = lax.all_to_all(turned, ROW + ("zl",), 0, 0, tiled=True)
     partial = weight_partials(meta, theirs, every.reshape(members * micro * length, width))
-    both = lax.all_to_all(partial, "core", 0, 0, tiled=True).transpose(1, 0, 2, 3)
-    spread = lax.all_to_all(both, DEEP + ("x",), 0, 0, tiled=True)
+    spread = lax.all_to_all(partial, SHARD, 0, 0, tiled=True)
     back = jnp.sum(spread.reshape(HIGH, members * OWN, 2 * piece).astype(jnp.float32), axis=0)
     back = back.reshape(LOW, ACROSS * CORES, OWN, 2, piece)
     owned = back.transpose(3, 2, 1, 0, 4).reshape(2, OWN, width)

time: 379 us -> 375 us (0.989)
    all_to_all x2 -> x1, blocking collectives: 37 us -> 33.8 us  [shards(): spread = lax.all_to_all(partial, SHARD, 0, 0, tiled=True)]
  transfers between devices with their start and end apart: 21 -> 21, of which waited for: 9 -> 9; matrix products, arithmetic and copies ran while one was open for 2% -> 1% of each run, Pallas kernels for 23% -> 23%
where the time goes in v2:
time: 375 us; the launch traced here: 374 us
  Pallas kernels  123 us (33%)
  waiting for transfers between devices  97.9 us (26%)
  starting transfers between devices  64.6 us (17%)
  blocking collectives  63 us (17%)
  between operations  14.9 us (4%)
  other arithmetic  5.86 us (2%)
  local copies, waits for them, and re-layouts  4.25 us (1%)
    all_gather x1, waiting for transfers between devices, shards(): own = lax.all_gather(row, DEEP, axis=0, tiled=True)  74.3 us
    pallas_call x17, Pallas kernels, settle(): pl.pallas_call(settle_body, out_shape=tuple((pltpu.VMEM(v.shape, v.dtype)...  63.2 us
    pallas_call x16, Pallas kernels, run(): pl.pallas_call(body, out_shape=tuple((jax.ShapeDtypeStruct(v.shape, v.dty...  54.6 us
    ppermute x8, starting transfers between devices, shards(): block = lax.ppermute(block, 'section', upward)  40.4 us
    all_to_all x1, blocking collectives, shards(): spread = lax.all_to_all(partial, SHARD, 0, 0, tiled=True)  33.8 us
    ppermute x8, waiting for transfers between devices, shards(): grad = lax.ppermute(grad, 'section', downward)  20.9 us
    all_to_all x1, blocking collectives, shards(): theirs = lax.all_to_all(turned, ROW + ('zl',), 0, 0, tiled=True)  16 us
    ppermute x8, starting transfers between devices, shards(): grad = lax.ppermute(grad, 'section', downward)  15.6 us
  transfers between devices with their start and end apart: 21, of which 9 were waited for; matrix products, arithmetic and copies ran while one was open for 1% of the time, Pallas kernels for 23%

profile of v2, /device:TPU:24, one launch (start us, length us, event | category | flops | bytes accessed | tf_op | source)
XLA Modules:
  0.0 374.2 jit_solution(7781003896610154934)
XLA Ops:
  7.5 13.1 %all_to_all.32 = bf16[8,16,1536]{2,1,0:T(8,128)(2,1)} all-to-all(bf16[8,16,1536]{2,1,0:T(8,128)(2,1)S(1)} %bitcast.72), channel_id=1, replica_groups=mesh['section'=8,'zh'=4,'zl'=3,'x'=4,'core'=2] {'x','core'}, dimensions={0} | all-to-all | bytes 786432 | tf_op jit(solution)/shard_map/all_to_all | solution.py:210
  20.7 74.3 %all-gather.4.cloned.1.call-done.refs_0_ = bf16[1536,1536]{1,0:T(8,128)(2,1)} async-done(((bf16[128,1536]{1,0:T(8,128)(2,1)}), bf16[1536,1536]{1,0:T(8,128)(2,1)}) %all-gather.4.cloned.1.call-update) | async-done | bytes 4718608 | tf_op jit(solution)/shard_map/all_gather | solution.py:211
  95.0 1.9 collective-permute-start
  100.7 2.3 settle.17.own_ref
  103.1 2.1 collective-permute-done.refs_0_.refs_1_
  105.2 2.3 settle.18.other_ref
  107.7 2.5 layer_forward.7
  110.2 4.6 %collective-permute-start.1 = (bf16[64,1536]{1,0:T(8,128)(2,1)S(1)}, bf16[64,1536]{1,0:T(8,128)(2,1)S(1)}, u32[]{:S(2)}, u32[]{:S(2)}) collective-permute-start(bf16[64,1536]{1,0:T(8,128)(2,1)S(1)} %get-tuple-element.89.refs_2_), channel_id=1, source_target_pairs={{0,96},{96,192},{192,288},{288,384},{384,480},{480,576},{576,672},... | collective-permute-start | bytes 589832 | tf_op jit(solution)/shard_map/ppermute | solution.py:270
  114.9 3.8 %settle.19 = (bf16[1536,1536]{1,0:T(8,128)(2,1)S(1)}, bf16[1536,1536]{1,0:T(8,128)(2,1)S(1)}) custom-call(bf16[1536,1536]{1,0:T(8,128)(2,1)} %all-gather.4.cloned.1.call-done.refs_0_, bf16[1536,1536]{1,0:T(8,128)(2,1)} %collective-permute-done.refs_0_.refs_1_, bf16[64,1536]{1,0:T(8,128)(2,1)S(1)} %get-tuple-element.89.refs_2_), custom_call_target="tpu_custom_call" | custom-call | bytes 37748736 | tf_op jit(solution)/shard_map/settle/pallas_call | solution.py:46
  119.3 2.5 layer_forward.8
  121.8 5.6 %collective-permute-start.2 = (bf16[64,1536]{1,0:T(8,128)(2,1)S(1)}, bf16[64,1536]{1,0:T(8,128)(2,1)S(1)}, u32[]{:S(2)}, u32[]{:S(2)}) collective-permute-start(bf16[64,1536]{1,0:T(8,128)(2,1)S(1)} %get-tuple-element.95.refs_2_), channel_id=1, source_target_pairs={{0,96},{96,192},{192,288},{288,384},{384,480},{480,576},{576,672},... | collective-permute-start | bytes 589832 | tf_op jit(solution)/shard_map/ppermute | solution.py:270
  127.5 3.8 %settle.20 = (bf16[1536,1536]{1,0:T(8,128)(2,1)S(1)}, bf16[1536,1536]{1,0:T(8,128)(2,1)S(1)}) custom-call(bf16[1536,1536]{1,0:T(8,128)(2,1)} %all-gather.4.cloned.1.call-done.refs_0_, bf16[1536,1536]{1,0:T(8,128)(2,1)} %collective-permute-done.refs_0_.refs_1_, bf16[64,1536]{1,0:T(8,128)(2,1)S(1)} %get-tuple-element.95.refs_2_), custom_call_target="tpu_custom_call" | custom-call | bytes 37748736 | tf_op jit(solution)/shard_map/settle/pallas_call | solution.py:46
  131.3 2.5 layer_forward.9
  133.8 5.3 %collective-permute-start.3 = (bf16[64,1536]{1,0:T(8,128)(2,1)S(1)}, bf16[64,1536]{1,0:T(8,128)(2,1)S(1)}, u32[]{:S(2)}, u32[]{:S(2)}) collective-permute-start(bf16[64,1536]{1,0:T(8,128)(2,1)S(1)} %get-tuple-element.101.refs_2_), channel_id=1, source_target_pairs={{0,96},{96,192},{192,288},{288,384},{384,480},{480,576},{576,672},... | collective-permute-start | bytes 589832 | tf_op jit(solution)/shard_map/ppermute | solution.py:270
  139.2 3.8 %settle.21 = (bf16[1536,1536]{1,0:T(8,128)(2,1)S(1)}, bf16[1536,1536]{1,0:T(8,128)(2,1)S(1)}) custom-call(bf16[1536,1536]{1,0:T(8,128)(2,1)} %all-gather.4.cloned.1.call-done.refs_0_, bf16[1536,1536]{1,0:T(8,128)(2,1)} %collective-permute-done.refs_0_.refs_1_, bf16[64,1536]{1,0:T(8,128)(2,1)S(1)} %get-tuple-element.101.refs_2_), custom_call_target="tpu_custom_call" | custom-call | bytes 37748736 | tf_op jit(solution)/shard_map/settle/pallas_call | solution.py:46
  143.0 2.5 layer_forward.10
  145.5 4.9 %collective-permute-start.4 = (bf16[64,1536]{1,0:T(8,128)(2,1)S(1)}, bf16[64,1536]{1,0:T(8,128)(2,1)S(1)}, u32[]{:S(2)}, u32[]{:S(2)}) collective-permute-start(bf16[64,1536]{1,0:T(8,128)(2,1)S(1)} %get-tuple-element.107.refs_2_), channel_id=1, source_target_pairs={{0,96},{96,192},{192,288},{288,384},{384,480},{480,576},{576,672},... | collective-permute-start | bytes 589832 | tf_op jit(solution)/shard_map/ppermute | solution.py:270
  150.5 3.8 %settle.22 = (bf16[1536,1536]{1,0:T(8,128)(2,1)S(1)}, bf16[1536,1536]{1,0:T(8,128)(2,1)S(1)}) custom-call(bf16[1536,1536]{1,0:T(8,128)(2,1)} %all-gather.4.cloned.1.call-done.refs_0_, bf16[1536,1536]{1,0:T(8,128)(2,1)} %collective-permute-done.refs_0_.refs_1_, bf16[64,1536]{1,0:T(8,128)(2,1)S(1)} %get-tuple-element.107.refs_2_), custom_call_target="tpu_custom_call" | custom-call | bytes 37748736 | tf_op jit(solution)/shard_map/settle/pallas_call | solution.py:46
  154.3 2.5 layer_forward.11
  156.7 4.9 %collective-permute-start.5 = (bf16[64,1536]{1,0:T(8,128)(2,1)S(1)}, bf16[64,1536]{1,0:T(8,128)(2,1)S(1)}, u32[]{:S(2)}, u32[]{:S(2)}) collective-permute-start(bf16[64,1536]{1,0:T(8,128)(2,1)S(1)} %get-tuple-element.113.refs_2_), channel_id=1, source_target_pairs={{0,96},{96,192},{192,288},{288,384},{384,480},{480,576},{576,672},... | collective-permute-start | bytes 589832 | tf_op jit(solution)/shard_map/ppermute | solution.py:270
  161.7 3.8 %settle.23 = (bf16[1536,1536]{1,0:T(8,128)(2,1)S(1)}, bf16[1536,1536]{1,0:T(8,128)(2,1)S(1)}) custom-call(bf16[1536,1536]{1,0:T(8,128)(2,1)} %all-gather.4.cloned.1.call-done.refs_0_, bf16[1536,1536]{1,0:T(8,128)(2,1)} %collective-permute-done.refs_0_.refs_1_, bf16[64,1536]{1,0:T(8,128)(2,1)S(1)} %get-tuple-element.113.refs_2_), custom_call_target="tpu_custom_call" | custom-call | bytes 37748736 | tf_op jit(solution)/shard_map/settle/pallas_call | solution.py:46
  165.5 2.5 layer_forward.12
  168.0 4.9 %collective-permute-start.6 = (bf16[64,1536]{1,0:T(8,128)(2,1)S(1)}, bf16[64,1536]{1,0:T(8,128)(2,1)S(1)}, u32[]{:S(2)}, u32[]{:S(2)}) collective-permute-start(bf16[64,1536]{1,0:T(8,128)(2,1)S(1)} %get-tuple-element.119.refs_2_), channel_id=1, source_target_pairs={{0,96},{96,192},{192,288},{288,384},{384,480},{480,576},{576,672},... | collective-permute-start | bytes 589832 | tf_op jit(solution)/shard_map/ppermute | solution.py:270
  173.0 3.8 %settle.24 = (bf16[1536,1536]{1,0:T(8,128)(2,1)S(1)}, bf16[1536,1536]{1,0:T(8,128)(2,1)S(1)}) custom-call(bf16[1536,1536]{1,0:T(8,128)(2,1)} %all-gather.4.cloned.1.call-done.refs_0_, bf16[1536,1536]{1,0:T(8,128)(2,1)} %collective-permute-done.refs_0_.refs_1_, bf16[64,1536]{1,0:T(8,128)(2,1)S(1)} %get-tuple-element.119.refs_2_), custom_call_target="tpu_custom_call" | custom-call | bytes 37748736 | tf_op jit(solution)/shard_map/settle/pallas_call | solution.py:46
  176.8 2.5 layer_forward.13
  179.3 5.0 %collective-permute-start.7 = (bf16[64,1536]{1,0:T(8,128)(2,1)S(1)}, bf16[64,1536]{1,0:T(8,128)(2,1)S(1)}, u32[]{:S(2)}, u32[]{:S(2)}) collective-permute-start(bf16[64,1536]{1,0:T(8,128)(2,1)S(1)} %get-tuple-element.125.refs_2_), channel_id=1, source_target_pairs={{0,96},{96,192},{192,288},{288,384},{384,480},{480,576},{576,672},... | collective-permute-start | bytes 589832 | tf_op jit(solution)/shard_map/ppermute | solution.py:270
  184.4 3.8 %settle.25 = (bf16[1536,1536]{1,0:T(8,128)(2,1)S(1)}, bf16[1536,1536]{1,0:T(8,128)(2,1)S(1)}) custom-call(bf16[1536,1536]{1,0:T(8,128)(2,1)} %all-gather.4.cloned.1.call-done.refs_0_, bf16[1536,1536]{1,0:T(8,128)(2,1)} %collective-permute-done.refs_0_.refs_1_, bf16[64,1536]{1,0:T(8,128)(2,1)S(1)} %get-tuple-element.125.refs_2_), custom_call_target="tpu_custom_call" | custom-call | bytes 37748736 | tf_op jit(solution)/shard_map/settle/pallas_call | solution.py:46
  188.3 5.6 %layer_turn.2 = (bf16[64,1536]{1,0:T(8,128)(2,1)S(1)}, bf16[64,1536]{1,0:T(8,128)(2,1)S(1)}, bf16[3,64,1536]{2,1,0:T(8,128)(2,1)S(1)}, f32[3,64,1536]{2,1,0:T(8,...) custom-call(s32[4]{0:T(128)S(1)} %pad_add_fusion.8.meta, ...), custom_call_target="tpu_custom_call", output_to_operand_aliasing={{2}: (5, {}), {3}: (6, {}), {4}: (7, {}), {5}: (8, {})} | custom-call | tf_op jit(solution)/shard_map/layer_turn/pallas_call | solution.py:186
  194.6 1.9 collective-permute-start.9
  196.6 5.3 %collective-permute-start.8 = (bf16[64,1536]{1,0:T(8,128)(2,1)}, bf16[64,1536]{1,0:T(8,128)(2,1)S(1)}, u32[]{:S(2)}, u32[]{:S(2)}) collective-permute-start(bf16[64,1536]{1,0:T(8,128)(2,1)} %copy-done.2), channel_id=1, source_target_pairs={{0,96},{96,192},{192,288},{288,384},{384,480},{480,576},{576,672},... | collective-permute-start | bytes 589832 | tf_op jit(solution)/shard_map/ppermute | solution.py:270
  201.9 3.8 %settle.26 = (bf16[1536,1536]{1,0:T(8,128)(2,1)S(1)}, bf16[1536,1536]{1,0:T(8,128)(2,1)S(1)}) custom-call(bf16[1536,1536]{1,0:T(8,128)(2,1)} %all-gather.4.cloned.1.call-done.refs_0_, bf16[1536,1536]{1,0:T(8,128)(2,1)} %collective-permute-done.refs_0_.refs_1_, bf16[64,1536]{1,0:T(8,128)(2,1)S(1)} %get-tuple-element.132.refs_2_), custom_call_target="tpu_custom_call" | custom-call | bytes 37748736 | tf_op jit(solution)/shard_map/settle/pallas_call | solution.py:46
  205.7 5.5 %layer_turn.3 = (bf16[64,1536]{1,0:T(8,128)(2,1)}, bf16[64,1536]{1,0:T(8,128)(2,1)S(1)}, bf16[3,64,1536]{2,1,0:T(8,128)(2,1)S(1)}, f32[3,64,1536]{2,1,0:T(8,128)...) custom-call(s32[4]{0:T(128)S(1)} %pad_add_fusion.7.meta, ...), custom_call_target="tpu_custom_call", output_to_operand_aliasing={{2}: (5, {}), {3}: (6, {}), {4}: (7, {}), {5}: (8, {})} | custom-call | tf_op jit(solution)/shard_map/layer_turn/pallas_call | solution.py:186
  211.3 1.9 collective-permute-start.10
  214.0 3.0 collective-permute-start.13
  217.0 3.7 %collective-permute-start.14 = (bf16[2,64,1536]{2,1,0:T(8,128)(2,1)}, bf16[2,64,1536]{2,1,0:T(8,128)(2,1)}, u32[]{:S(2)}, u32[]{:S(2)}) collective-permute-start(bf16[2,64,1536]{2,1,0:T(8,128)(2,1)} %slice.23), channel_id=1, source_target_pairs={{0,16},{8,0},{16,8},{1,17},{9,1},{17,9},{2,18},{10,2},{18,10},{3,1... | collective-permute-start | bytes 1179656 | tf_op jit(solution)/shard_map/ppermute | solution.py:274
  220.8 3.8 %settle.27 = (bf16[1536,1536]{1,0:T(8,128)(2,1)S(1)}, bf16[1536,1536]{1,0:T(8,128)(2,1)S(1)}) custom-call(bf16[1536,1536]{1,0:T(8,128)(2,1)} %all-gather.4.cloned.1.call-done.refs_0_, bf16[1536,1536]{1,0:T(8,128)(2,1)} %collective-permute-done.refs_0_.refs_1_, bf16[64,1536]{1,0:T(8,128)(2,1)S(1)} %get-tuple-element.139.refs_2_), custom_call_target="tpu_custom_call" | custom-call | bytes 37748736 | tf_op jit(solution)/shard_map/settle/pallas_call | solution.py:46
  224.6 3.7 layer_backward.6
  228.3 1.9 collective-permute-start.11
  230.4 3.8 %settle.28 = (bf16[1536,1536]{1,0:T(8,128)(2,1)S(1)}, bf16[1536,1536]{1,0:T(8,128)(2,1)S(1)}) custom-call(bf16[1536,1536]{1,0:T(8,128)(2,1)} %all-gather.4.cloned.1.call-done.refs_0_, bf16[1536,1536]{1,0:T(8,128)(2,1)} %collective-permute-done.refs_0_.refs_1_, bf16[64,1536]{1,0:T(8,128)(2,1)S(1)} %get-tuple-element.145.refs_2_), custom_call_target="tpu_custom_call" | custom-call | bytes 37748736 | tf_op jit(solution)/shard_map/settle/pallas_call | solution.py:46
  234.2 2.9 collective-permute-done.11.g_ref
  237.1 3.7 layer_backward.7
  243.2 1.9 collective-permute-start.12
  245.2 3.8 %settle.29 = (bf16[1536,1536]{1,0:T(8,128)(2,1)S(1)}, bf16[1536,1536]{1,0:T(8,128)(2,1)S(1)}) custom-call(bf16[1536,1536]{1,0:T(8,128)(2,1)} %all-gather.4.cloned.1.call-done.refs_0_, bf16[1536,1536]{1,0:T(8,128)(2,1)} %collective-permute-done.refs_0_.refs_1_, bf16[64,1536]{1,0:T(8,128)(2,1)S(1)} %get-tuple-element.151.refs_2_), custom_call_target="tpu_custom_call" | custom-call | bytes 37748736 | tf_op jit(solution)/shard_map/settle/pallas_call | solution.py:46
  249.0 3.5 collective-permute-done.12.g_ref
  252.5 3.6 layer_backward.8
  256.1 2.1 collective-permute-start.15
  258.4 4.9 %settle.30 = (bf16[1536,1536]{1,0:T(8,128)(2,1)S(1)}, bf16[1536,1536]{1,0:T(8,128)(2,1)S(1)}) custom-call(bf16[1536,1536]{1,0:T(8,128)(2,1)} %all-gather.4.cloned.1.call-done.refs_0_, bf16[1536,1536]{1,0:T(8,128)(2,1)} %collective-permute-done.refs_0_.refs_1_, bf16[64,1536]{1,0:T(8,128)(2,1)S(1)} %get-tuple-element.155.refs_2_), custom_call_target="tpu_custom_call" | custom-call | bytes 37748736 | tf_op jit(solution)/shard_map/settle/pallas_call | solution.py:46
  263.3 3.4 collective-permute-done.15.g_ref
  266.7 3.6 layer_backward.9
  270.3 1.9 collective-permute-start.16
  272.3 4.0 %settle.31 = (bf16[1536,1536]{1,0:T(8,128)(2,1)S(1)}, bf16[1536,1536]{1,0:T(8,128)(2,1)S(1)}) custom-call(bf16[1536,1536]{1,0:T(8,128)(2,1)} %all-gather.4.cloned.1.call-done.refs_0_, bf16[1536,1536]{1,0:T(8,128)(2,1)} %collective-permute-done.refs_0_.refs_1_, bf16[64,1536]{1,0:T(8,128)(2,1)S(1)} %get-tuple-element.159.refs_2_), custom_call_target="tpu_custom_call" | custom-call | bytes 37748736 | tf_op jit(solution)/shard_map/settle/pallas_call | solution.py:46
  276.3 4.5 %collective-permute-done.16.g_ref = bf16[64,1536]{1,0:T(8,128)(2,1)S(1)} collective-permute-done((bf16[64,1536]{1,0:T(8,128)(2,1)S(1)}, bf16[64,1536]{1,0:T(8,128)(2,1)S(1)}, u32[]{:S(2)}, u32[]{:S(2)}) %collective-permute-start.16) | collective-permute-done | bytes 196640 | tf_op jit(solution)/shard_map/ppermute | solution.py:272
  280.8 3.6 layer_backward.10
  284.4 1.9 collective-permute-start.17
  286.4 4.0 %settle.32 = (bf16[1536,1536]{1,0:T(8,128)(2,1)S(1)}, bf16[1536,1536]{1,0:T(8,128)(2,1)S(1)}) custom-call(bf16[1536,1536]{1,0:T(8,128)(2,1)} %all-gather.4.cloned.1.call-done.refs_0_, bf16[1536,1536]{1,0:T(8,128)(2,1)} %collective-permute-done.refs_0_.refs_1_, bf16[64,1536]{1,0:T(8,128)(2,1)S(1)} %get-tuple-element.163.refs_2_), custom_call_target="tpu_custom_call" | custom-call | bytes 37748736 | tf_op jit(solution)/shard_map/settle/pallas_call | solution.py:46
  290.4 3.8 %collective-permute-done.17.g_ref = bf16[64,1536]{1,0:T(8,128)(2,1)S(1)} collective-permute-done((bf16[64,1536]{1,0:T(8,128)(2,1)S(1)}, bf16[64,1536]{1,0:T(8,128)(2,1)S(1)}, u32[]{:S(2)}, u32[]{:S(2)}) %collective-permute-start.17) | collective-permute-done | bytes 196640 | tf_op jit(solution)/shard_map/ppermute | solution.py:272
  294.2 3.6 layer_backward.11
  297.8 1.9 collective-permute-start.18
  299.9 3.9 %settle.33 = (bf16[1536,1536]{1,0:T(8,128)(2,1)S(1)}, bf16[1536,1536]{1,0:T(8,128)(2,1)S(1)}) custom-call(bf16[1536,1536]{1,0:T(8,128)(2,1)} %all-gather.4.cloned.1.call-done.refs_0_, bf16[1536,1536]{1,0:T(8,128)(2,1)} %collective-permute-done.refs_0_.refs_1_, bf16[64,1536]{1,0:T(8,128)(2,1)S(1)} %get-tuple-element.167.refs_2_), custom_call_target="tpu_custom_call" | custom-call | bytes 37748736 | tf_op jit(solution)/shard_map/settle/pallas_call | solution.py:46
  303.7 2.9 collective-permute-done.18.g_ref
  306.6 4.3 %layer_last.1 = (bf16[64,1536]{1,0:T(8,128)(2,1)}, bf16[1536,128]{1,0:T(8,128)(2,1)S(1)}, bf16[3,64,1536]{2,1,0:T(8,128)(2,1)S(1)}) custom-call(s32[4]{0:T(128)S(1)} %pad_add_fusion.meta, bf16[64,1536]{1,0:T(8,128)(2,1)S(1)} %collective-permute-done.18.g_ref, bf16[1536,1536]{1,0:T(8,128)(2,1)S(1)} %get-tuple-element.168.own_ref, ...), custom_call_target="tpu_custom_call", output_to_operand_aliasing={{2}: (6, {})} | custom-call | tf_op jit(solution)/shard_map/layer_last/pallas_call | solution.py:186
  310.9 16.0 %all_to_all.33 = bf16[24,64,128]{2,1,0:T(8,128)(2,1)S(1)} all-to-all(bf16[24,64,128]{2,1,0:T(8,128)(2,1)S(1)} %bitcast.67), channel_id=1, replica_groups=mesh['section'=8,'zh'=4,'zl'=3,'x'=4,'core'=2] {'x','core','zl'}, dimensions={0} | all-to-all | bytes 786432 | tf_op jit(solution)/shard_map/all_to_all | solution.py:283
  327.0 5.0 %weight_partials.1 = bf16[1536,128]{1,0:T(8,128)(2,1)S(1)} custom-call(s32[4]{0:T(128)S(1)} %pad_add_fusion.meta, bf16[1536,128]{1,0:T(8,128)(2,1)S(1)} %bitcast.65, bf16[3072,1536]{1,0:T(8,128)(2,1)} %bitcast.68), custom_call_target="tpu_custom_call" | custom-call | tf_op jit(solution)/shard_map/weight_partials/pallas_call | solution.py:155
  332.0 33.8 %all_to_all.34 = bf16[96,16,128]{2,1,0:T(8,128)(2,1)S(1)} all-to-all(bf16[96,16,128]{2,1,0:T(8,128)(2,1)S(1)} %bitcast.66), channel_id=1, replica_groups=mesh['section'=8,'zh'=4,'zl'=3,'x'=4,'core'=2] {'zh','zl','x','core'}, dimensions={0} | all-to-all | bytes 786432 | tf_op jit(solution)/shard_map/all_to_all | solution.py:285
  (62 shorter events, 11.6 us)
Async XLA Ops:
  6.5 91.1 %copy-start = (bf16[128,1536]{1,0:T(8,128)(2,1)S(1)}, bf16[128,1536]{1,0:T(8,128)(2,1)}, u32[]{:S(2)}) copy-start(bf16[128,1536]{1,0:T(8,128)(2,1)} %param.8) | copy-start | bytes 1179652
  6.5 88.5 %all-gather.4.cloned.1.call-start = ((), (), s32[]{:S(2)}) async-start(), calls=%async_computation.3 | async-start | bytes 5111808 | tf_op jit(solution)/shard_map/all_gather | solution.py:211
  20.7 306.3 %all-gather.6.cloned.1.call-start = ((), (), s32[]{:S(2)}) async-start(), calls=%async_computation.4 | async-start | bytes 10616832 | tf_op jit(solution)/shard_map/all_gather | solution.py:266
  95.0 10.1 %collective-permute-start = (bf16[1536,1536]{1,0:T(8,128)(2,1)}, bf16[1536,1536]{1,0:T(8,128)(2,1)}, u32[]{:S(2)}, u32[]{:S(2)}) collective-permute-start(bf16[1536,1536]{1,0:T(8,128)(2,1)} %all-gather.4.cloned.1.call-done.refs_0_), channel_id=1, source_target_pairs={{0,1},{1,0},{2,3},{3,2},{4,5},{5,4},{6,7},{7,6},{8,9},{9,8},{10,11... | collective-permute-start | bytes 14155784 | tf_op jit(solution)/shard_map/ppermute | solution.py:212
  110.2 9.1 %collective-permute-start.1 = (bf16[64,1536]{1,0:T(8,128)(2,1)S(1)}, bf16[64,1536]{1,0:T(8,128)(2,1)S(1)}, u32[]{:S(2)}, u32[]{:S(2)}) collective-permute-start(bf16[64,1536]{1,0:T(8,128)(2,1)S(1)} %get-tuple-element.89.refs_2_), channel_id=1, source_target_pairs={{0,96},{96,192},{192,288},{288,384},{384,480},{480,576},{576,672},... | collective-permute-start | bytes 589832 | tf_op jit(solution)/shard_map/ppermute | solution.py:270
  121.8 9.5 %collective-permute-start.2 = (bf16[64,1536]{1,0:T(8,128)(2,1)S(1)}, bf16[64,1536]{1,0:T(8,128)(2,1)S(1)}, u32[]{:S(2)}, u32[]{:S(2)}) collective-permute-start(bf16[64,1536]{1,0:T(8,128)(2,1)S(1)} %get-tuple-element.95.refs_2_), channel_id=1, source_target_pairs={{0,96},{96,192},{192,288},{288,384},{384,480},{480,576},{576,672},... | collective-permute-start | bytes 589832 | tf_op jit(solution)/shard_map/ppermute | solution.py:270
  133.8 9.2 %collective-permute-start.3 = (bf16[64,1536]{1,0:T(8,128)(2,1)S(1)}, bf16[64,1536]{1,0:T(8,128)(2,1)S(1)}, u32[]{:S(2)}, u32[]{:S(2)}) collective-permute-start(bf16[64,1536]{1,0:T(8,128)(2,1)S(1)} %get-tuple-element.101.refs_2_), channel_id=1, source_target_pairs={{0,96},{96,192},{192,288},{288,384},{384,480},{480,576},{576,672},... | collective-permute-start | bytes 589832 | tf_op jit(solution)/shard_map/ppermute | solution.py:270
  145.5 8.8 %collective-permute-start.4 = (bf16[64,1536]{1,0:T(8,128)(2,1)S(1)}, bf16[64,1536]{1,0:T(8,128)(2,1)S(1)}, u32[]{:S(2)}, u32[]{:S(2)}) collective-permute-start(bf16[64,1536]{1,0:T(8,128)(2,1)S(1)} %get-tuple-element.107.refs_2_), channel_id=1, source_target_pairs={{0,96},{96,192},{192,288},{288,384},{384,480},{480,576},{576,672},... | collective-permute-start | bytes 589832 | tf_op jit(solution)/shard_map/ppermute | solution.py:270
  156.7 8.8 %collective-permute-start.5 = (bf16[64,1536]{1,0:T(8,128)(2,1)S(1)}, bf16[64,1536]{1,0:T(8,128)(2,1)S(1)}, u32[]{:S(2)}, u32[]{:S(2)}) collective-permute-start(bf16[64,1536]{1,0:T(8,128)(2,1)S(1)} %get-tuple-element.113.refs_2_), channel_id=1, source_target_pairs={{0,96},{96,192},{192,288},{288,384},{384,480},{480,576},{576,672},... | collective-permute-start | bytes 589832 | tf_op jit(solution)/shard_map/ppermute | solution.py:270
  168.0 8.8 %collective-permute-start.6 = (bf16[64,1536]{1,0:T(8,128)(2,1)S(1)}, bf16[64,1536]{1,0:T(8,128)(2,1)S(1)}, u32[]{:S(2)}, u32[]{:S(2)}) collective-permute-start(bf16[64,1536]{1,0:T(8,128)(2,1)S(1)} %get-tuple-element.119.refs_2_), channel_id=1, source_target_pairs={{0,96},{96,192},{192,288},{288,384},{384,480},{480,576},{576,672},... | collective-permute-start | bytes 589832 | tf_op jit(solution)/shard_map/ppermute | solution.py:270
  176.8 7.5 %copy-start.3 = (bf16[2,1,64,1536]{3,2,1,0:T(8,128)(2,1)S(1)}, bf16[2,1,64,1536]{3,2,1,0:T(8,128)(2,1)}, u32[]{:S(2)}) copy-start(bf16[2,1,64,1536]{3,2,1,0:T(8,128)(2,1)} %param.11) | copy-start | bytes 1179652
  179.3 9.0 %collective-permute-start.7 = (bf16[64,1536]{1,0:T(8,128)(2,1)S(1)}, bf16[64,1536]{1,0:T(8,128)(2,1)S(1)}, u32[]{:S(2)}, u32[]{:S(2)}) collective-permute-start(bf16[64,1536]{1,0:T(8,128)(2,1)S(1)} %get-tuple-element.125.refs_2_), channel_id=1, source_target_pairs={{0,96},{96,192},{192,288},{288,384},{384,480},{480,576},{576,672},... | collective-permute-start | bytes 589832 | tf_op jit(solution)/shard_map/ppermute | solution.py:270
  193.9 0.7 copy-start.2
  194.6 11.1 %collective-permute-start.9 = (bf16[64,1536]{1,0:T(8,128)(2,1)S(1)}, bf16[64,1536]{1,0:T(8,128)(2,1)S(1)}, u32[]{:S(2)}, u32[]{:S(2)}) collective-permute-start(bf16[64,1536]{1,0:T(8,128)(2,1)S(1)} %get-tuple-element.132.refs_2_), channel_id=1, source_target_pairs={{96,0},{192,96},{288,192},{384,288},{480,384},{576,480},{672,576},... | collective-permute-start | bytes 589832 | tf_op jit(solution)/shard_map/ppermute | solution.py:272
  196.6 9.1 %copy-start.4 = (bf16[2,1,64,1536]{3,2,1,0:T(8,128)(2,1)S(1)}, bf16[2,1,64,1536]{3,2,1,0:T(8,128)(2,1)}, u32[]{:S(2)}) copy-start(bf16[2,1,64,1536]{3,2,1,0:T(8,128)(2,1)} %param.11) | copy-start | bytes 1179652
  196.6 9.1 %collective-permute-start.8 = (bf16[64,1536]{1,0:T(8,128)(2,1)}, bf16[64,1536]{1,0:T(8,128)(2,1)S(1)}, u32[]{:S(2)}, u32[]{:S(2)}) collective-permute-start(bf16[64,1536]{1,0:T(8,128)(2,1)} %copy-done.2), channel_id=1, source_target_pairs={{0,96},{96,192},{192,288},{288,384},{384,480},{480,576},{576,672},... | collective-permute-start | bytes 589832 | tf_op jit(solution)/shard_map/ppermute | solution.py:270
  211.3 13.4 %collective-permute-start.10 = (bf16[64,1536]{1,0:T(8,128)(2,1)S(1)}, bf16[64,1536]{1,0:T(8,128)(2,1)S(1)}, u32[]{:S(2)}, u32[]{:S(2)}) collective-permute-start(bf16[64,1536]{1,0:T(8,128)(2,1)S(1)} %get-tuple-element.139.refs_2_), channel_id=1, source_target_pairs={{96,0},{192,96},{288,192},{384,288},{480,384},{576,480},{672,576},... | collective-permute-start | bytes 589832 | tf_op jit(solution)/shard_map/ppermute | solution.py:272
  214.0 26.8 %collective-permute-start.13 = (bf16[2,64,1536]{2,1,0:T(8,128)(2,1)}, bf16[2,64,1536]{2,1,0:T(8,128)(2,1)}, u32[]{:S(2)}, u32[]{:S(2)}) collective-permute-start(bf16[2,64,1536]{2,1,0:T(8,128)(2,1)} %slice.23), channel_id=1, source_target_pairs={{0,8},{8,16},{16,0},{1,9},{9,17},{17,1},{2,10},{10,18},{18,2},{3,1... | collective-permute-start | bytes 1179656 | tf_op jit(solution)/shard_map/ppermute | solution.py:279
  217.0 23.8 %collective-permute-start.14 = (bf16[2,64,1536]{2,1,0:T(8,128)(2,1)}, bf16[2,64,1536]{2,1,0:T(8,128)(2,1)}, u32[]{:S(2)}, u32[]{:S(2)}) collective-permute-start(bf16[2,64,1536]{2,1,0:T(8,128)(2,1)} %slice.23), channel_id=1, source_target_pairs={{0,16},{8,0},{16,8},{1,17},{9,1},{17,9},{2,18},{10,2},{18,10},{3,1... | collective-permute-start | bytes 1179656 | tf_op jit(solution)/shard_map/ppermute | solution.py:274
  228.3 8.8 %collective-permute-start.11 = (bf16[64,1536]{1,0:T(8,128)(2,1)S(1)}, bf16[64,1536]{1,0:T(8,128)(2,1)S(1)}, u32[]{:S(2)}, u32[]{:S(2)}) collective-permute-start(bf16[64,1536]{1,0:T(8,128)(2,1)S(1)} %get-tuple-element.145.refs_2_), channel_id=1, source_target_pairs={{96,0},{192,96},{288,192},{384,288},{480,384},{576,480},{672,576},... | collective-permute-start | bytes 589832 | tf_op jit(solution)/shard_map/ppermute | solution.py:272
  243.2 9.3 %collective-permute-start.12 = (bf16[64,1536]{1,0:T(8,128)(2,1)S(1)}, bf16[64,1536]{1,0:T(8,128)(2,1)S(1)}, u32[]{:S(2)}, u32[]{:S(2)}) collective-permute-start(bf16[64,1536]{1,0:T(8,128)(2,1)S(1)} %get-tuple-element.151.refs_2_), channel_id=1, source_target_pairs={{96,0},{192,96},{288,192},{384,288},{480,384},{576,480},{672,576},... | collective-permute-start | bytes 589832 | tf_op jit(solution)/shard_map/ppermute | solution.py:272
  256.1 10.5 %collective-permute-start.15 = (bf16[64,1536]{1,0:T(8,128)(2,1)S(1)}, bf16[64,1536]{1,0:T(8,128)(2,1)S(1)}, u32[]{:S(2)}, u32[]{:S(2)}) collective-permute-start(bf16[64,1536]{1,0:T(8,128)(2,1)S(1)} %get-tuple-element.155.refs_2_), channel_id=1, source_target_pairs={{96,0},{192,96},{288,192},{384,288},{480,384},{576,480},{672,576},... | collective-permute-start | bytes 589832 | tf_op jit(solution)/shard_map/ppermute | solution.py:272
  270.3 10.5 %collective-permute-start.16 = (bf16[64,1536]{1,0:T(8,128)(2,1)S(1)}, bf16[64,1536]{1,0:T(8,128)(2,1)S(1)}, u32[]{:S(2)}, u32[]{:S(2)}) collective-permute-start(bf16[64,1536]{1,0:T(8,128)(2,1)S(1)} %get-tuple-element.159.refs_2_), channel_id=1, source_target_pairs={{96,0},{192,96},{288,192},{384,288},{480,384},{576,480},{672,576},... | collective-permute-start | bytes 589832 | tf_op jit(solution)/shard_map/ppermute | solution.py:272
  284.4 9.8 %collective-permute-start.17 = (bf16[64,1536]{1,0:T(8,128)(2,1)S(1)}, bf16[64,1536]{1,0:T(8,128)(2,1)S(1)}, u32[]{:S(2)}, u32[]{:S(2)}) collective-permute-start(bf16[64,1536]{1,0:T(8,128)(2,1)S(1)} %get-tuple-element.163.refs_2_), channel_id=1, source_target_pairs={{96,0},{192,96},{288,192},{384,288},{480,384},{576,480},{672,576},... | collective-permute-start | bytes 589832 | tf_op jit(solution)/shard_map/ppermute | solution.py:272
  297.8 8.8 %collective-permute-start.18 = (bf16[64,1536]{1,0:T(8,128)(2,1)S(1)}, bf16[64,1536]{1,0:T(8,128)(2,1)S(1)}, u32[]{:S(2)}, u32[]{:S(2)}) collective-permute-start(bf16[64,1536]{1,0:T(8,128)(2,1)S(1)} %get-tuple-element.167.refs_2_), channel_id=1, source_target_pairs={{96,0},{192,96},{288,192},{384,288},{480,384},{576,480},{672,576},... | collective-permute-start | bytes 589832 | tf_op jit(solution)/shard_map/ppermute | solution.py:272
  327.0 40.4 %copy-start.1 = (bf16[128,1536]{1,0:T(8,128)(2,1)S(1)}, bf16[128,1536]{1,0:T(8,128)(2,1)}, u32[]{:S(2)}) copy-start(bf16[128,1536]{1,0:T(8,128)(2,1)} %param.8) | copy-start | bytes 1179652
Sparse Core Ops, SparseCore 0:
  20.8 74.1 all-gather.3
  243.3 61.0 all-gather.5

commit v3 on v2

--- a/solution.py
+++ b/solution.py
@@ -110,8 +110,13 @@
     backward_part(meta, g_ref, own_ref, other_ref, xs, zs, g_out, dzs, da)
 
 
-def last_body(meta, g_ref, own_ref, other_ref, xs, zs, keep_d, g_out, turned, dzs, da):
-    backward_body(meta, g_ref, own_ref, other_ref, xs, zs, keep_d, g_out, dzs, da)
+def last_body(meta, g_ref, xs, zs, keep_d, turned, dzs):
+    del xs, keep_d
+    slot = meta[3]
+    pre = zs[slot]
+    sigma = jax.nn.sigmoid(pre)
+    d_pre = g_ref[...].astype(jnp.float32) * sigma * (1.0 + pre * (1.0 - sigma))
+    dzs[slot] = d_pre.astype(jnp.bfloat16)
     hours_all = jnp.concatenate([dzs[i].astype(jnp.float32) for i in range(dzs.shape[0] - 1)], axis=0)
     turned[...] = hours_all.T.astype(jnp.bfloat16)
 
@@ -127,14 +132,15 @@
     piece = turned.shape[0] // members
     length = turned.shape[1] // 2
     hours = meta[1]
-    current = turned[...].astype(jnp.float32)
-    lane = lax.broadcasted_iota(jnp.int32, current.shape, 1) % length
-    moved = jnp.where(lane < length - hours, pltpu.roll(current, 2 * length - hours, 1), 0.0)
+    lane = lax.broadcasted_iota(jnp.int32, (piece, 2 * length), 1) % length
     for source in range(members):
-        span = slice(source * piece, (source + 1) * piece)
+        behind = meta[4] - source % LOW
+        origin = source - source % LOW + jnp.where(behind < 0, behind + LOW, behind)
+        current = turned[pl.ds(pl.multiple_of(origin * piece, piece), piece), :].astype(jnp.float32)
+        moved = jnp.where(lane < length - hours, pltpu.roll(current, 2 * length - hours, 1), 0.0)
         lanes = slice(source * 2 * length, (source + 1) * 2 * length)
-        sides[:piece, lanes] = current[span].astype(jnp.bfloat16)
-        sides[piece:, lanes] = moved[span].astype(jnp.bfloat16)
+        sides[:piece, lanes] = current.astype(jnp.bfloat16)
+        sides[piece:, lanes] = moved.astype(jnp.bfloat16)
     for index in range(CHUNKS):
         copies[index].wait()
         span = slice(index * depth, (index + 1) * depth)
@@ -205,6 +211,7 @@
     inputs = (features.astype(jnp.float32) + bias[:, :, None, :]).astype(jnp.bfloat16)[:, 0]
     upstream = cotangent[:, 0]
     core = lax.axis_index("core")
+    depth = lax.axis_index("zl")
     tap = weights[0]
     copies = jnp.broadcast_to(tap[None], (ACROSS,) + tap.shape).reshape(ACROSS * CORES * OWN, width)
     row = lax.all_to_all(copies, ROW, 0, 0, tiled=True)
@@ -223,7 +230,7 @@
         return jnp.where(jnp.logical_and(order >= 0, order < micro), order, micro)
 
     def meta_of(ahead, behind):
-        parts = [slot_of(ahead - here), hours, core, slot_of(behind - (SECTIONS - 1 - here))]
+        parts = [slot_of(ahead - here), hours, core, slot_of(behind - (SECTIONS - 1 - here)), depth]
         return jnp.stack(parts).astype(jnp.int32)
 
     upward = [(i, i + 1) for i in range(SECTIONS - 1)]
@@ -249,22 +256,15 @@
             lead = grad
         elif tick == ticks + SECTIONS - 2:
             turned = jax.ShapeDtypeStruct((width, micro * length), jnp.bfloat16)
-            grad, turned, dzs = run(
-                last_body, "layer_last", meta, (grad,), near, (dzs,), (xs, zs), scratch, (turned,)
-            )
+            turned, dzs = run(last_body, "layer_last", meta, (), (), (dzs,), (grad, xs, zs), [], (turned,))
         else:
             grad, dzs = run(backward_body, "layer_backward", meta, (grad,), near, (dzs,), (xs, zs), scratch)
             lead = grad
         if tick == ticks + 1:
-            every = jnp.stack(
-                [
-                    jnp.where(depth == j, moved[0], jnp.where((depth - j) % LOW == 1, moved[1], moved[2]))
-                    for j in range(LOW)
-                ]
-            )
+            every = jnp.stack(moved)
             every, lead = lax.optimization_barrier((every, lead))
             every = lax.all_gather(every, ROW, axis=0, tiled=False)
-        if tick < ticks + SECTIONS - 2:
+        if tick < ticks + SECTIONS - 3:
             near = settle((own, other), lead)
         if tick < ticks - 1:
             block = lax.ppermute(block, "section", upward)
@@ -274,7 +274,6 @@
             moved.append(lax.ppermute(done, "zl", turns[2]))
         if tick == ticks - 1:
             done = acts[:micro]
-            depth = lax.axis_index("zl")
             turns = [[(i, (i + k) % LOW) for i in range(LOW)] for k in range(LOW)]
             moved = [done, lax.ppermute(done, "zl", turns[1])]
 

time: 375 us -> 371 us (0.989)
  Pallas kernels: 123 us -> 115 us
  waiting for transfers between devices: 97.9 us -> 102 us
    ppermute x8, waiting for transfers between devices: 20.9 us -> 24.9 us  [shards(): grad = lax.ppermute(grad, 'section', downward)]
    pallas_call x17 -> x16, Pallas kernels: 63.2 us -> 59.3 us  [settle(): pl.pallas_call(settle_body, out_shape=tuple((pltpu.VMEM(v.shape, v.dtype)...]
    pallas_call x16, Pallas kernels: 54.6 us -> 50.8 us  [run(): pl.pallas_call(body, out_shape=tuple((jax.ShapeDtypeStruct(v.shape, v.dty...]
  transfers between devices with their start and end apart: 21 -> 21, of which waited for: 9 -> 9; matrix products, arithmetic and copies ran while one was open for 1% -> 1% of each run, Pallas kernels for 23% -> 21%
where the time goes in v3:
time: 371 us; the launch traced here: 370 us
  Pallas kernels  115 us (31%)
  waiting for transfers between devices  102 us (27%)
  starting transfers between devices  64.6 us (17%)
  blocking collectives  63 us (17%)
  between operations  14.9 us (4%)
  local copies, waits for them, and re-layouts  5.76 us (2%)
  other arithmetic  4.52 us (1%)
    all_gather x1, waiting for transfers between devices, shards(): own = lax.all_gather(row, DEEP, axis=0, tiled=True)  74.3 us
    pallas_call x16, Pallas kernels, settle(): pl.pallas_call(settle_body, out_shape=tuple((pltpu.VMEM(v.shape, v.dtype)...  59.3 us
    pallas_call x16, Pallas kernels, run(): pl.pallas_call(body, out_shape=tuple((jax.ShapeDtypeStruct(v.shape, v.dty...  50.8 us
    ppermute x8, starting transfers between devices, shards(): block = lax.ppermute(block, 'section', upward)  40.4 us
    all_to_all x1, blocking collectives, shards(): spread = lax.all_to_all(partial, SHARD, 0, 0, tiled=True)  33.8 us
    ppermute x8, waiting for transfers between devices, shards(): grad = lax.ppermute(grad, 'section', downward)  24.9 us
    all_to_all x1, blocking collectives, shards(): theirs = lax.all_to_all(turned, ROW + ('zl',), 0, 0, tiled=True)  16.1 us
    ppermute x8, starting transfers between devices, shards(): grad = lax.ppermute(grad, 'section', downward)  15.6 us
  transfers between devices with their start and end apart: 21, of which 9 were waited for; matrix products, arithmetic and copies ran while one was open for 1% of the time, Pallas kernels for 21%

profile of v3, /device:TPU:24, one launch (start us, length us, event | category | flops | bytes accessed | tf_op | source)
XLA Modules:
  0.0 370.4 jit_solution(8230196109670712503)
XLA Ops:
  7.5 13.1 %all_to_all.32 = bf16[8,16,1536]{2,1,0:T(8,128)(2,1)} all-to-all(bf16[8,16,1536]{2,1,0:T(8,128)(2,1)S(1)} %bitcast.71), channel_id=1, replica_groups=mesh['section'=8,'zh'=4,'zl'=3,'x'=4,'core'=2] {'x','core'}, dimensions={0} | all-to-all | bytes 786432 | tf_op jit(solution)/shard_map/all_to_all | solution.py:217
  20.7 74.3 %all-gather.4.cloned.1.call-done.refs_0_ = bf16[1536,1536]{1,0:T(8,128)(2,1)} async-done(((bf16[128,1536]{1,0:T(8,128)(2,1)}), bf16[1536,1536]{1,0:T(8,128)(2,1)}) %all-gather.4.cloned.1.call-update) | async-done | bytes 4718608 | tf_op jit(solution)/shard_map/all_gather | solution.py:218
  95.0 1.9 collective-permute-start
  98.6 1.1 add_convert_fusion
  100.7 2.3 settle.16.own_ref
  103.1 2.1 collective-permute-done.refs_0_.refs_1_
  105.2 2.3 settle.17.other_ref
  107.7 2.4 layer_forward.7
  110.2 4.6 %collective-permute-start.1 = (bf16[64,1536]{1,0:T(8,128)(2,1)S(1)}, bf16[64,1536]{1,0:T(8,128)(2,1)S(1)}, u32[]{:S(2)}, u32[]{:S(2)}) collective-permute-start(bf16[64,1536]{1,0:T(8,128)(2,1)S(1)} %get-tuple-element.87.refs_2_), channel_id=1, source_target_pairs={{0,96},{96,192},{192,288},{288,384},{384,480},{480,576},{576,672},... | collective-permute-start | bytes 589832 | tf_op jit(solution)/shard_map/ppermute | solution.py:270
  114.9 3.8 %settle.18 = (bf16[1536,1536]{1,0:T(8,128)(2,1)S(1)}, bf16[1536,1536]{1,0:T(8,128)(2,1)S(1)}) custom-call(bf16[1536,1536]{1,0:T(8,128)(2,1)} %all-gather.4.cloned.1.call-done.refs_0_, bf16[1536,1536]{1,0:T(8,128)(2,1)} %collective-permute-done.refs_0_.refs_1_, bf16[64,1536]{1,0:T(8,128)(2,1)S(1)} %get-tuple-element.87.refs_2_), custom_call_target="tpu_custom_call" | custom-call | bytes 37748736 | tf_op jit(solution)/shard_map/settle/pallas_call | solution.py:46
  119.3 2.4 layer_forward.8
  121.7 5.6 %collective-permute-start.2 = (bf16[64,1536]{1,0:T(8,128)(2,1)S(1)}, bf16[64,1536]{1,0:T(8,128)(2,1)S(1)}, u32[]{:S(2)}, u32[]{:S(2)}) collective-permute-start(bf16[64,1536]{1,0:T(8,128)(2,1)S(1)} %get-tuple-element.93.refs_2_), channel_id=1, source_target_pairs={{0,96},{96,192},{192,288},{288,384},{384,480},{480,576},{576,672},... | collective-permute-start | bytes 589832 | tf_op jit(solution)/shard_map/ppermute | solution.py:270
  127.4 3.8 %settle.19 = (bf16[1536,1536]{1,0:T(8,128)(2,1)S(1)}, bf16[1536,1536]{1,0:T(8,128)(2,1)S(1)}) custom-call(bf16[1536,1536]{1,0:T(8,128)(2,1)} %all-gather.4.cloned.1.call-done.refs_0_, bf16[1536,1536]{1,0:T(8,128)(2,1)} %collective-permute-done.refs_0_.refs_1_, bf16[64,1536]{1,0:T(8,128)(2,1)S(1)} %get-tuple-element.93.refs_2_), custom_call_target="tpu_custom_call" | custom-call | bytes 37748736 | tf_op jit(solution)/shard_map/settle/pallas_call | solution.py:46
  131.2 2.4 layer_forward.9
  133.7 5.3 %collective-permute-start.3 = (bf16[64,1536]{1,0:T(8,128)(2,1)S(1)}, bf16[64,1536]{1,0:T(8,128)(2,1)S(1)}, u32[]{:S(2)}, u32[]{:S(2)}) collective-permute-start(bf16[64,1536]{1,0:T(8,128)(2,1)S(1)} %get-tuple-element.99.refs_2_), channel_id=1, source_target_pairs={{0,96},{96,192},{192,288},{288,384},{384,480},{480,576},{576,672},... | collective-permute-start | bytes 589832 | tf_op jit(solution)/shard_map/ppermute | solution.py:270
  139.1 3.8 %settle.20 = (bf16[1536,1536]{1,0:T(8,128)(2,1)S(1)}, bf16[1536,1536]{1,0:T(8,128)(2,1)S(1)}) custom-call(bf16[1536,1536]{1,0:T(8,128)(2,1)} %all-gather.4.cloned.1.call-done.refs_0_, bf16[1536,1536]{1,0:T(8,128)(2,1)} %collective-permute-done.refs_0_.refs_1_, bf16[64,1536]{1,0:T(8,128)(2,1)S(1)} %get-tuple-element.99.refs_2_), custom_call_target="tpu_custom_call" | custom-call | bytes 37748736 | tf_op jit(solution)/shard_map/settle/pallas_call | solution.py:46
  142.9 2.4 layer_forward.10
  145.4 4.9 %collective-permute-start.4 = (bf16[64,1536]{1,0:T(8,128)(2,1)S(1)}, bf16[64,1536]{1,0:T(8,128)(2,1)S(1)}, u32[]{:S(2)}, u32[]{:S(2)}) collective-permute-start(bf16[64,1536]{1,0:T(8,128)(2,1)S(1)} %get-tuple-element.105.refs_2_), channel_id=1, source_target_pairs={{0,96},{96,192},{192,288},{288,384},{384,480},{480,576},{576,672},... | collective-permute-start | bytes 589832 | tf_op jit(solution)/shard_map/ppermute | solution.py:270
  150.3 3.8 %settle.21 = (bf16[1536,1536]{1,0:T(8,128)(2,1)S(1)}, bf16[1536,1536]{1,0:T(8,128)(2,1)S(1)}) custom-call(bf16[1536,1536]{1,0:T(8,128)(2,1)} %all-gather.4.cloned.1.call-done.refs_0_, bf16[1536,1536]{1,0:T(8,128)(2,1)} %collective-permute-done.refs_0_.refs_1_, bf16[64,1536]{1,0:T(8,128)(2,1)S(1)} %get-tuple-element.105.refs_2_), custom_call_target="tpu_custom_call" | custom-call | bytes 37748736 | tf_op jit(solution)/shard_map/settle/pallas_call | solution.py:46
  154.1 2.4 layer_forward.11
  156.6 4.9 %collective-permute-start.5 = (bf16[64,1536]{1,0:T(8,128)(2,1)S(1)}, bf16[64,1536]{1,0:T(8,128)(2,1)S(1)}, u32[]{:S(2)}, u32[]{:S(2)}) collective-permute-start(bf16[64,1536]{1,0:T(8,128)(2,1)S(1)} %get-tuple-element.111.refs_2_), channel_id=1, source_target_pairs={{0,96},{96,192},{192,288},{288,384},{384,480},{480,576},{576,672},... | collective-permute-start | bytes 589832 | tf_op jit(solution)/shard_map/ppermute | solution.py:270
  161.5 3.8 %settle.22 = (bf16[1536,1536]{1,0:T(8,128)(2,1)S(1)}, bf16[1536,1536]{1,0:T(8,128)(2,1)S(1)}) custom-call(bf16[1536,1536]{1,0:T(8,128)(2,1)} %all-gather.4.cloned.1.call-done.refs_0_, bf16[1536,1536]{1,0:T(8,128)(2,1)} %collective-permute-done.refs_0_.refs_1_, bf16[64,1536]{1,0:T(8,128)(2,1)S(1)} %get-tuple-element.111.refs_2_), custom_call_target="tpu_custom_call" | custom-call | bytes 37748736 | tf_op jit(solution)/shard_map/settle/pallas_call | solution.py:46
  165.4 2.4 layer_forward.12
  167.8 4.9 %collective-permute-start.6 = (bf16[64,1536]{1,0:T(8,128)(2,1)S(1)}, bf16[64,1536]{1,0:T(8,128)(2,1)S(1)}, u32[]{:S(2)}, u32[]{:S(2)}) collective-permute-start(bf16[64,1536]{1,0:T(8,128)(2,1)S(1)} %get-tuple-element.117.refs_2_), channel_id=1, source_target_pairs={{0,96},{96,192},{192,288},{288,384},{384,480},{480,576},{576,672},... | collective-permute-start | bytes 589832 | tf_op jit(solution)/shard_map/ppermute | solution.py:270
  172.8 3.8 %settle.23 = (bf16[1536,1536]{1,0:T(8,128)(2,1)S(1)}, bf16[1536,1536]{1,0:T(8,128)(2,1)S(1)}) custom-call(bf16[1536,1536]{1,0:T(8,128)(2,1)} %all-gather.4.cloned.1.call-done.refs_0_, bf16[1536,1536]{1,0:T(8,128)(2,1)} %collective-permute-done.refs_0_.refs_1_, bf16[64,1536]{1,0:T(8,128)(2,1)S(1)} %get-tuple-element.117.refs_2_), custom_call_target="tpu_custom_call" | custom-call | bytes 37748736 | tf_op jit(solution)/shard_map/settle/pallas_call | solution.py:46
  176.6 2.4 layer_forward.13
  179.0 5.0 %collective-permute-start.7 = (bf16[64,1536]{1,0:T(8,128)(2,1)S(1)}, bf16[64,1536]{1,0:T(8,128)(2,1)S(1)}, u32[]{:S(2)}, u32[]{:S(2)}) collective-permute-start(bf16[64,1536]{1,0:T(8,128)(2,1)S(1)} %get-tuple-element.123.refs_2_), channel_id=1, source_target_pairs={{0,96},{96,192},{192,288},{288,384},{384,480},{480,576},{576,672},... | collective-permute-start | bytes 589832 | tf_op jit(solution)/shard_map/ppermute | solution.py:270
  184.2 3.8 %settle.24 = (bf16[1536,1536]{1,0:T(8,128)(2,1)S(1)}, bf16[1536,1536]{1,0:T(8,128)(2,1)S(1)}) custom-call(bf16[1536,1536]{1,0:T(8,128)(2,1)} %all-gather.4.cloned.1.call-done.refs_0_, bf16[1536,1536]{1,0:T(8,128)(2,1)} %collective-permute-done.refs_0_.refs_1_, bf16[64,1536]{1,0:T(8,128)(2,1)S(1)} %get-tuple-element.123.refs_2_), custom_call_target="tpu_custom_call" | custom-call | bytes 37748736 | tf_op jit(solution)/shard_map/settle/pallas_call | solution.py:46
  188.1 5.5 %layer_turn.2 = (bf16[64,1536]{1,0:T(8,128)(2,1)S(1)}, bf16[64,1536]{1,0:T(8,128)(2,1)S(1)}, bf16[3,64,1536]{2,1,0:T(8,128)(2,1)S(1)}, f32[3,64,1536]{2,1,0:T(8,...) custom-call(s32[5]{0:T(128)S(1)} %stack.236.meta, ...), custom_call_target="tpu_custom_call", output_to_operand_aliasing={{2}: (5, {}), {3}: (6, {}), {4}: (7, {}), {5}: (8, {})} | custom-call | tf_op jit(solution)/shard_map/layer_turn/pallas_call | solution.py:192
  194.3 1.9 collective-permute-start.9
  196.3 5.3 %collective-permute-start.8 = (bf16[64,1536]{1,0:T(8,128)(2,1)}, bf16[64,1536]{1,0:T(8,128)(2,1)S(1)}, u32[]{:S(2)}, u32[]{:S(2)}) collective-permute-start(bf16[64,1536]{1,0:T(8,128)(2,1)} %copy-done.2), channel_id=1, source_target_pairs={{0,96},{96,192},{192,288},{288,384},{384,480},{480,576},{576,672},... | collective-permute-start | bytes 589832 | tf_op jit(solution)/shard_map/ppermute | solution.py:270
  201.6 3.8 %settle.25 = (bf16[1536,1536]{1,0:T(8,128)(2,1)S(1)}, bf16[1536,1536]{1,0:T(8,128)(2,1)S(1)}) custom-call(bf16[1536,1536]{1,0:T(8,128)(2,1)} %all-gather.4.cloned.1.call-done.refs_0_, bf16[1536,1536]{1,0:T(8,128)(2,1)} %collective-permute-done.refs_0_.refs_1_, bf16[64,1536]{1,0:T(8,128)(2,1)S(1)} %get-tuple-element.130.refs_2_), custom_call_target="tpu_custom_call" | custom-call | bytes 37748736 | tf_op jit(solution)/shard_map/settle/pallas_call | solution.py:46
  205.4 5.5 %layer_turn.3 = (bf16[64,1536]{1,0:T(8,128)(2,1)}, bf16[64,1536]{1,0:T(8,128)(2,1)S(1)}, bf16[3,64,1536]{2,1,0:T(8,128)(2,1)S(1)}, f32[3,64,1536]{2,1,0:T(8,128)...) custom-call(s32[5]{0:T(128)S(1)} %stack.233.meta, ...), custom_call_target="tpu_custom_call", output_to_operand_aliasing={{2}: (5, {}), {3}: (6, {}), {4}: (7, {}), {5}: (8, {})} | custom-call | tf_op jit(solution)/shard_map/layer_turn/pallas_call | solution.py:192
  210.9 1.9 collective-permute-start.10
  213.8 3.0 collective-permute-start.13
  216.8 3.7 %collective-permute-start.14 = (bf16[2,64,1536]{2,1,0:T(8,128)(2,1)}, bf16[2,64,1536]{2,1,0:T(8,128)(2,1)}, u32[]{:S(2)}, u32[]{:S(2)}) collective-permute-start(bf16[2,64,1536]{2,1,0:T(8,128)(2,1)} %get-tuple-element.170), channel_id=1, source_target_pairs={{0,16},{8,0},{16,8},{1,17},{9,1},{17,9},{2,18},{10,2},{18,10},{3,1... | collective-permute-start | bytes 1179656 | tf_op jit(solution)/shard_map/ppermute | solution.py:274
  220.6 3.8 %settle.26 = (bf16[1536,1536]{1,0:T(8,128)(2,1)S(1)}, bf16[1536,1536]{1,0:T(8,128)(2,1)S(1)}) custom-call(bf16[1536,1536]{1,0:T(8,128)(2,1)} %all-gather.4.cloned.1.call-done.refs_0_, bf16[1536,1536]{1,0:T(8,128)(2,1)} %collective-permute-done.refs_0_.refs_1_, bf16[64,1536]{1,0:T(8,128)(2,1)S(1)} %get-tuple-element.137.refs_2_), custom_call_target="tpu_custom_call" | custom-call | bytes 37748736 | tf_op jit(solution)/shard_map/settle/pallas_call | solution.py:46
  224.5 3.6 layer_backward.6
  228.1 1.9 collective-permute-start.11
  230.1 3.8 %settle.27 = (bf16[1536,1536]{1,0:T(8,128)(2,1)S(1)}, bf16[1536,1536]{1,0:T(8,128)(2,1)S(1)}) custom-call(bf16[1536,1536]{1,0:T(8,128)(2,1)} %all-gather.4.cloned.1.call-done.refs_0_, bf16[1536,1536]{1,0:T(8,128)(2,1)} %collective-permute-done.refs_0_.refs_1_, bf16[64,1536]{1,0:T(8,128)(2,1)S(1)} %get-tuple-element.143.refs_2_), custom_call_target="tpu_custom_call" | custom-call | bytes 37748736 | tf_op jit(solution)/shard_map/settle/pallas_call | solution.py:46
  233.9 3.0 collective-permute-done.11.g_ref
  236.9 3.6 layer_backward.7
  240.5 2.3 pad_maximum_fusion
  242.8 1.9 collective-permute-start.12
  244.9 3.8 %settle.28 = (bf16[1536,1536]{1,0:T(8,128)(2,1)S(1)}, bf16[1536,1536]{1,0:T(8,128)(2,1)S(1)}) custom-call(bf16[1536,1536]{1,0:T(8,128)(2,1)} %all-gather.4.cloned.1.call-done.refs_0_, bf16[1536,1536]{1,0:T(8,128)(2,1)} %collective-permute-done.refs_0_.refs_1_, bf16[64,1536]{1,0:T(8,128)(2,1)S(1)} %get-tuple-element.149.refs_2_), custom_call_target="tpu_custom_call" | custom-call | bytes 37748736 | tf_op jit(solution)/shard_map/settle/pallas_call | solution.py:46
  248.7 3.5 collective-permute-done.12.g_ref
  252.1 3.6 layer_backward.8
  255.8 2.1 collective-permute-start.15
  258.0 4.9 %settle.29 = (bf16[1536,1536]{1,0:T(8,128)(2,1)S(1)}, bf16[1536,1536]{1,0:T(8,128)(2,1)S(1)}) custom-call(bf16[1536,1536]{1,0:T(8,128)(2,1)} %all-gather.4.cloned.1.call-done.refs_0_, bf16[1536,1536]{1,0:T(8,128)(2,1)} %collective-permute-done.refs_0_.refs_1_, bf16[64,1536]{1,0:T(8,128)(2,1)S(1)} %get-tuple-element.153.refs_2_), custom_call_target="tpu_custom_call" | custom-call | bytes 37748736 | tf_op jit(solution)/shard_map/settle/pallas_call | solution.py:46
  262.9 3.4 collective-permute-done.15.g_ref
  266.3 3.6 layer_backward.9
  269.9 1.9 collective-permute-start.16
  272.0 4.0 %settle.30 = (bf16[1536,1536]{1,0:T(8,128)(2,1)S(1)}, bf16[1536,1536]{1,0:T(8,128)(2,1)S(1)}) custom-call(bf16[1536,1536]{1,0:T(8,128)(2,1)} %all-gather.4.cloned.1.call-done.refs_0_, bf16[1536,1536]{1,0:T(8,128)(2,1)} %collective-permute-done.refs_0_.refs_1_, bf16[64,1536]{1,0:T(8,128)(2,1)S(1)} %get-tuple-element.157.refs_2_), custom_call_target="tpu_custom_call" | custom-call | bytes 37748736 | tf_op jit(solution)/shard_map/settle/pallas_call | solution.py:46
  275.9 4.5 %collective-permute-done.16.g_ref = bf16[64,1536]{1,0:T(8,128)(2,1)S(1)} collective-permute-done((bf16[64,1536]{1,0:T(8,128)(2,1)S(1)}, bf16[64,1536]{1,0:T(8,128)(2,1)S(1)}, u32[]{:S(2)}, u32[]{:S(2)}) %collective-permute-start.16) | collective-permute-done | bytes 196640 | tf_op jit(solution)/shard_map/ppermute | solution.py:272
  280.4 3.6 layer_backward.10
  284.0 1.9 collective-permute-start.17
  286.1 4.0 %settle.31 = (bf16[1536,1536]{1,0:T(8,128)(2,1)S(1)}, bf16[1536,1536]{1,0:T(8,128)(2,1)S(1)}) custom-call(bf16[1536,1536]{1,0:T(8,128)(2,1)} %all-gather.4.cloned.1.call-done.refs_0_, bf16[1536,1536]{1,0:T(8,128)(2,1)} %collective-permute-done.refs_0_.refs_1_, bf16[64,1536]{1,0:T(8,128)(2,1)S(1)} %get-tuple-element.161.refs_2_), custom_call_target="tpu_custom_call" | custom-call | bytes 37748736 | tf_op jit(solution)/shard_map/settle/pallas_call | solution.py:46
  290.1 3.8 %collective-permute-done.17.g_ref = bf16[64,1536]{1,0:T(8,128)(2,1)S(1)} collective-permute-done((bf16[64,1536]{1,0:T(8,128)(2,1)S(1)}, bf16[64,1536]{1,0:T(8,128)(2,1)S(1)}, u32[]{:S(2)}, u32[]{:S(2)}) %collective-permute-start.17) | collective-permute-done | bytes 196640 | tf_op jit(solution)/shard_map/ppermute | solution.py:272
  293.9 3.6 layer_backward.11
  297.5 1.9 collective-permute-start.18
  299.5 6.8 %collective-permute-done.18.g_ref = bf16[64,1536]{1,0:T(8,128)(2,1)S(1)} collective-permute-done((bf16[64,1536]{1,0:T(8,128)(2,1)S(1)}, bf16[64,1536]{1,0:T(8,128)(2,1)S(1)}, u32[]{:S(2)}, u32[]{:S(2)}) %collective-permute-start.18) | collective-permute-done | bytes 196640 | tf_op jit(solution)/shard_map/ppermute | solution.py:272
  307.2 16.1 %all_to_all.33 = bf16[24,64,128]{2,1,0:T(8,128)(2,1)S(1)} all-to-all(bf16[24,64,128]{2,1,0:T(8,128)(2,1)S(1)} %bitcast.66), channel_id=1, replica_groups=mesh['section'=8,'zh'=4,'zl'=3,'x'=4,'core'=2] {'x','core','zl'}, dimensions={0} | all-to-all | bytes 786432 | tf_op jit(solution)/shard_map/all_to_all | solution.py:282
  323.2 5.0 %weight_partials.1 = bf16[1536,128]{1,0:T(8,128)(2,1)S(1)} custom-call(s32[5]{0:T(128)S(1)} %stack.212.meta, bf16[1536,128]{1,0:T(8,128)(2,1)S(1)} %bitcast.64, bf16[3072,1536]{1,0:T(8,128)(2,1)} %bitcast.67), custom_call_target="tpu_custom_call" | custom-call | tf_op jit(solution)/shard_map/weight_partials/pallas_call | solution.py:161
  328.2 33.8 %all_to_all.34 = bf16[96,16,128]{2,1,0:T(8,128)(2,1)S(1)} all-to-all(bf16[96,16,128]{2,1,0:T(8,128)(2,1)S(1)} %bitcast.65), channel_id=1, replica_groups=mesh['section'=8,'zh'=4,'zl'=3,'x'=4,'core'=2] {'zh','zl','x','core'}, dimensions={0} | all-to-all | bytes 786432 | tf_op jit(solution)/shard_map/all_to_all | solution.py:284
  (62 shorter events, 9.3 us)
Async XLA Ops:
  6.5 91.2 %copy-start = (bf16[128,1536]{1,0:T(8,128)(2,1)S(1)}, bf16[128,1536]{1,0:T(8,128)(2,1)}, u32[]{:S(2)}) copy-start(bf16[128,1536]{1,0:T(8,128)(2,1)} %param.8) | copy-start | bytes 1179652
  6.5 88.5 %all-gather.4.cloned.1.call-start = ((), (), s32[]{:S(2)}) async-start(), calls=%async_computation.3 | async-start | bytes 5111808 | tf_op jit(solution)/shard_map/all_gather | solution.py:218
  20.7 302.5 %all-gather.6.cloned.1.call-start = ((), (), s32[]{:S(2)}) async-start(), calls=%async_computation.4 | async-start | bytes 10616832 | tf_op jit(solution)/shard_map/all_gather | solution.py:266
  95.0 10.1 %collective-permute-start = (bf16[1536,1536]{1,0:T(8,128)(2,1)}, bf16[1536,1536]{1,0:T(8,128)(2,1)}, u32[]{:S(2)}, u32[]{:S(2)}) collective-permute-start(bf16[1536,1536]{1,0:T(8,128)(2,1)} %all-gather.4.cloned.1.call-done.refs_0_), channel_id=1, source_target_pairs={{0,1},{1,0},{2,3},{3,2},{4,5},{5,4},{6,7},{7,6},{8,9},{9,8},{10,11... | collective-permute-start | bytes 14155784 | tf_op jit(solution)/shard_map/ppermute | solution.py:219
  110.2 9.1 %collective-permute-start.1 = (bf16[64,1536]{1,0:T(8,128)(2,1)S(1)}, bf16[64,1536]{1,0:T(8,128)(2,1)S(1)}, u32[]{:S(2)}, u32[]{:S(2)}) collective-permute-start(bf16[64,1536]{1,0:T(8,128)(2,1)S(1)} %get-tuple-element.87.refs_2_), channel_id=1, source_target_pairs={{0,96},{96,192},{192,288},{288,384},{384,480},{480,576},{576,672},... | collective-permute-start | bytes 589832 | tf_op jit(solution)/shard_map/ppermute | solution.py:270
  121.7 9.5 %collective-permute-start.2 = (bf16[64,1536]{1,0:T(8,128)(2,1)S(1)}, bf16[64,1536]{1,0:T(8,128)(2,1)S(1)}, u32[]{:S(2)}, u32[]{:S(2)}) collective-permute-start(bf16[64,1536]{1,0:T(8,128)(2,1)S(1)} %get-tuple-element.93.refs_2_), channel_id=1, source_target_pairs={{0,96},{96,192},{192,288},{288,384},{384,480},{480,576},{576,672},... | collective-permute-start | bytes 589832 | tf_op jit(solution)/shard_map/ppermute | solution.py:270
  133.7 9.2 %collective-permute-start.3 = (bf16[64,1536]{1,0:T(8,128)(2,1)S(1)}, bf16[64,1536]{1,0:T(8,128)(2,1)S(1)}, u32[]{:S(2)}, u32[]{:S(2)}) collective-permute-start(bf16[64,1536]{1,0:T(8,128)(2,1)S(1)} %get-tuple-element.99.refs_2_), channel_id=1, source_target_pairs={{0,96},{96,192},{192,288},{288,384},{384,480},{480,576},{576,672},... | collective-permute-start | bytes 589832 | tf_op jit(solution)/shard_map/ppermute | solution.py:270
  145.4 8.8 %collective-permute-start.4 = (bf16[64,1536]{1,0:T(8,128)(2,1)S(1)}, bf16[64,1536]{1,0:T(8,128)(2,1)S(1)}, u32[]{:S(2)}, u32[]{:S(2)}) collective-permute-start(bf16[64,1536]{1,0:T(8,128)(2,1)S(1)} %get-tuple-element.105.refs_2_), channel_id=1, source_target_pairs={{0,96},{96,192},{192,288},{288,384},{384,480},{480,576},{576,672},... | collective-permute-start | bytes 589832 | tf_op jit(solution)/shard_map/ppermute | solution.py:270
  156.6 8.8 %collective-permute-start.5 = (bf16[64,1536]{1,0:T(8,128)(2,1)S(1)}, bf16[64,1536]{1,0:T(8,128)(2,1)S(1)}, u32[]{:S(2)}, u32[]{:S(2)}) collective-permute-start(bf16[64,1536]{1,0:T(8,128)(2,1)S(1)} %get-tuple-element.111.refs_2_), channel_id=1, source_target_pairs={{0,96},{96,192},{192,288},{288,384},{384,480},{480,576},{576,672},... | collective-permute-start | bytes 589832 | tf_op jit(solution)/shard_map/ppermute | solution.py:270
  167.8 8.8 %collective-permute-start.6 = (bf16[64,1536]{1,0:T(8,128)(2,1)S(1)}, bf16[64,1536]{1,0:T(8,128)(2,1)S(1)}, u32[]{:S(2)}, u32[]{:S(2)}) collective-permute-start(bf16[64,1536]{1,0:T(8,128)(2,1)S(1)} %get-tuple-element.117.refs_2_), channel_id=1, source_target_pairs={{0,96},{96,192},{192,288},{288,384},{384,480},{480,576},{576,672},... | collective-permute-start | bytes 589832 | tf_op jit(solution)/shard_map/ppermute | solution.py:270
  176.6 7.5 %copy-start.4 = (bf16[2,1,64,1536]{3,2,1,0:T(8,128)(2,1)S(1)}, bf16[2,1,64,1536]{3,2,1,0:T(8,128)(2,1)}, u32[]{:S(2)}) copy-start(bf16[2,1,64,1536]{3,2,1,0:T(8,128)(2,1)} %param.11) | copy-start | bytes 1179652
  179.0 9.0 %collective-permute-start.7 = (bf16[64,1536]{1,0:T(8,128)(2,1)S(1)}, bf16[64,1536]{1,0:T(8,128)(2,1)S(1)}, u32[]{:S(2)}, u32[]{:S(2)}) collective-permute-start(bf16[64,1536]{1,0:T(8,128)(2,1)S(1)} %get-tuple-element.123.refs_2_), channel_id=1, source_target_pairs={{0,96},{96,192},{192,288},{288,384},{384,480},{480,576},{576,672},... | collective-permute-start | bytes 589832 | tf_op jit(solution)/shard_map/ppermute | solution.py:270
  193.6 0.7 copy-start.2
  194.3 11.1 %collective-permute-start.9 = (bf16[64,1536]{1,0:T(8,128)(2,1)S(1)}, bf16[64,1536]{1,0:T(8,128)(2,1)S(1)}, u32[]{:S(2)}, u32[]{:S(2)}) collective-permute-start(bf16[64,1536]{1,0:T(8,128)(2,1)S(1)} %get-tuple-element.130.refs_2_), channel_id=1, source_target_pairs={{96,0},{192,96},{288,192},{384,288},{480,384},{576,480},{672,576},... | collective-permute-start | bytes 589832 | tf_op jit(solution)/shard_map/ppermute | solution.py:272
  196.3 9.1 %copy-start.5 = (bf16[2,1,64,1536]{3,2,1,0:T(8,128)(2,1)S(1)}, bf16[2,1,64,1536]{3,2,1,0:T(8,128)(2,1)}, u32[]{:S(2)}) copy-start(bf16[2,1,64,1536]{3,2,1,0:T(8,128)(2,1)} %param.11) | copy-start | bytes 1179652
  196.3 9.1 %collective-permute-start.8 = (bf16[64,1536]{1,0:T(8,128)(2,1)}, bf16[64,1536]{1,0:T(8,128)(2,1)S(1)}, u32[]{:S(2)}, u32[]{:S(2)}) collective-permute-start(bf16[64,1536]{1,0:T(8,128)(2,1)} %copy-done.2), channel_id=1, source_target_pairs={{0,96},{96,192},{192,288},{288,384},{384,480},{480,576},{576,672},... | collective-permute-start | bytes 589832 | tf_op jit(solution)/shard_map/ppermute | solution.py:270
  210.9 13.5 %collective-permute-start.10 = (bf16[64,1536]{1,0:T(8,128)(2,1)S(1)}, bf16[64,1536]{1,0:T(8,128)(2,1)S(1)}, u32[]{:S(2)}, u32[]{:S(2)}) collective-permute-start(bf16[64,1536]{1,0:T(8,128)(2,1)S(1)} %get-tuple-element.137.refs_2_), channel_id=1, source_target_pairs={{96,0},{192,96},{288,192},{384,288},{480,384},{576,480},{672,576},... | collective-permute-start | bytes 589832 | tf_op jit(solution)/shard_map/ppermute | solution.py:272
  213.8 26.7 %collective-permute-start.13 = (bf16[2,64,1536]{2,1,0:T(8,128)(2,1)}, bf16[2,64,1536]{2,1,0:T(8,128)(2,1)}, u32[]{:S(2)}, u32[]{:S(2)}) collective-permute-start(bf16[2,64,1536]{2,1,0:T(8,128)(2,1)} %get-tuple-element.170), channel_id=1, source_target_pairs={{0,8},{8,16},{16,0},{1,9},{9,17},{17,1},{2,10},{10,18},{18,2},{3,1... | collective-permute-start | bytes 1179656 | tf_op jit(solution)/shard_map/ppermute | solution.py:278
  216.8 23.7 %collective-permute-start.14 = (bf16[2,64,1536]{2,1,0:T(8,128)(2,1)}, bf16[2,64,1536]{2,1,0:T(8,128)(2,1)}, u32[]{:S(2)}, u32[]{:S(2)}) collective-permute-start(bf16[2,64,1536]{2,1,0:T(8,128)(2,1)} %get-tuple-element.170), channel_id=1, source_target_pairs={{0,16},{8,0},{16,8},{1,17},{9,1},{17,9},{2,18},{10,2},{18,10},{3,1... | collective-permute-start | bytes 1179656 | tf_op jit(solution)/shard_map/ppermute | solution.py:274
  228.1 8.8 %collective-permute-start.11 = (bf16[64,1536]{1,0:T(8,128)(2,1)S(1)}, bf16[64,1536]{1,0:T(8,128)(2,1)S(1)}, u32[]{:S(2)}, u32[]{:S(2)}) collective-permute-start(bf16[64,1536]{1,0:T(8,128)(2,1)S(1)} %get-tuple-element.143.refs_2_), channel_id=1, source_target_pairs={{96,0},{192,96},{288,192},{384,288},{480,384},{576,480},{672,576},... | collective-permute-start | bytes 589832 | tf_op jit(solution)/shard_map/ppermute | solution.py:272
  236.9 3.7 copy-start.3
  242.8 9.3 %collective-permute-start.12 = (bf16[64,1536]{1,0:T(8,128)(2,1)S(1)}, bf16[64,1536]{1,0:T(8,128)(2,1)S(1)}, u32[]{:S(2)}, u32[]{:S(2)}) collective-permute-start(bf16[64,1536]{1,0:T(8,128)(2,1)S(1)} %get-tuple-element.149.refs_2_), channel_id=1, source_target_pairs={{96,0},{192,96},{288,192},{384,288},{480,384},{576,480},{672,576},... | collective-permute-start | bytes 589832 | tf_op jit(solution)/shard_map/ppermute | solution.py:272
  255.8 10.5 %collective-permute-start.15 = (bf16[64,1536]{1,0:T(8,128)(2,1)S(1)}, bf16[64,1536]{1,0:T(8,128)(2,1)S(1)}, u32[]{:S(2)}, u32[]{:S(2)}) collective-permute-start(bf16[64,1536]{1,0:T(8,128)(2,1)S(1)} %get-tuple-element.153.refs_2_), channel_id=1, source_target_pairs={{96,0},{192,96},{288,192},{384,288},{480,384},{576,480},{672,576},... | collective-permute-start | bytes 589832 | tf_op jit(solution)/shard_map/ppermute | solution.py:272
  269.9 10.5 %collective-permute-start.16 = (bf16[64,1536]{1,0:T(8,128)(2,1)S(1)}, bf16[64,1536]{1,0:T(8,128)(2,1)S(1)}, u32[]{:S(2)}, u32[]{:S(2)}) collective-permute-start(bf16[64,1536]{1,0:T(8,128)(2,1)S(1)} %get-tuple-element.157.refs_2_), channel_id=1, source_target_pairs={{96,0},{192,96},{288,192},{384,288},{480,384},{576,480},{672,576},... | collective-permute-start | bytes 589832 | tf_op jit(solution)/shard_map/ppermute | solution.py:272
  284.0 9.8 %collective-permute-start.17 = (bf16[64,1536]{1,0:T(8,128)(2,1)S(1)}, bf16[64,1536]{1,0:T(8,128)(2,1)S(1)}, u32[]{:S(2)}, u32[]{:S(2)}) collective-permute-start(bf16[64,1536]{1,0:T(8,128)(2,1)S(1)} %get-tuple-element.161.refs_2_), channel_id=1, source_target_pairs={{96,0},{192,96},{288,192},{384,288},{480,384},{576,480},{672,576},... | collective-permute-start | bytes 589832 | tf_op jit(solution)/shard_map/ppermute | solution.py:272
  297.5 8.8 %collective-permute-start.18 = (bf16[64,1536]{1,0:T(8,128)(2,1)S(1)}, bf16[64,1536]{1,0:T(8,128)(2,1)S(1)}, u32[]{:S(2)}, u32[]{:S(2)}) collective-permute-start(bf16[64,1536]{1,0:T(8,128)(2,1)S(1)} %get-tuple-element.165), channel_id=1, source_target_pairs={{96,0},{192,96},{288,192},{384,288},{480,384},{576,480},{672,576},... | collective-permute-start | bytes 589832 | tf_op jit(solution)/shard_map/ppermute | solution.py:272
  323.2 40.4 %copy-start.1 = (bf16[128,1536]{1,0:T(8,128)(2,1)S(1)}, bf16[128,1536]{1,0:T(8,128)(2,1)}, u32[]{:S(2)}) copy-start(bf16[128,1536]{1,0:T(8,128)(2,1)} %param.8) | copy-start | bytes 1179652
Sparse Core Ops, SparseCore 0:
  20.8 74.1 all-gather.3
  243.0 61.0 all-gather.5

commit v4 on v3

--- a/solution.py
+++ b/solution.py
@@ -271,6 +271,7 @@
         if 0 <= behind and tick < ticks + SECTIONS - 2:
             grad = lax.ppermute(grad, "section", downward)
         if tick == ticks:
+            done, _ = lax.optimization_barrier((done, lead))
             moved.append(lax.ppermute(done, "zl", turns[2]))
         if tick == ticks - 1:
             done = acts[:micro]

time: 371 us -> 371 us (level)
  no operation moved by 1% of the time
where the time goes in v4:
time: 371 us; the launch traced here: 370 us
  Pallas kernels  115 us (31%)
  waiting for transfers between devices  102 us (27%)
  starting transfers between devices  64.6 us (17%)
  blocking collectives  63 us (17%)
  between operations  14.9 us (4%)
  local copies, waits for them, and re-layouts  5.63 us (2%)
  other arithmetic  4.52 us (1%)
    all_gather x1, waiting for transfers between devices, shards(): own = lax.all_gather(row, DEEP, axis=0, tiled=True)  74.3 us
    pallas_call x16, Pallas kernels, settle(): pl.pallas_call(settle_body, out_shape=tuple((pltpu.VMEM(v.shape, v.dtype)...  59.3 us
    pallas_call x16, Pallas kernels, run(): pl.pallas_call(body, out_shape=tuple((jax.ShapeDtypeStruct(v.shape, v.dty...  50.8 us
    ppermute x8, starting transfers between devices, shards(): block = lax.ppermute(block, 'section', upward)  40.4 us
    all_to_all x1, blocking collectives, shards(): spread = lax.all_to_all(partial, SHARD, 0, 0, tiled=True)  33.7 us
    ppermute x8, waiting for transfers between devices, shards(): grad = lax.ppermute(grad, 'section', downward)  24.9 us
    all_to_all x1, blocking collectives, shards(): theirs = lax.all_to_all(turned, ROW + ('zl',), 0, 0, tiled=True)  16.1 us
    ppermute x8, starting transfers between devices, shards(): grad = lax.ppermute(grad, 'section', downward)  15.6 us
  transfers between devices with their start and end apart: 21, of which 9 were waited for; matrix products, arithmetic and copies ran while one was open for 1% of the time, Pallas kernels for 21%

profile of v4, /device:TPU:24, one launch (start us, length us, event | category | flops | bytes accessed | tf_op | source)
XLA Modules:
  0.0 370.3 jit_solution(4769897361173716100)
XLA Ops:
  7.5 13.1 %all_to_all.32 = bf16[8,16,1536]{2,1,0:T(8,128)(2,1)} all-to-all(bf16[8,16,1536]{2,1,0:T(8,128)(2,1)S(1)} %bitcast.71), channel_id=1, replica_groups=mesh['section'=8,'zh'=4,'zl'=3,'x'=4,'core'=2] {'x','core'}, dimensions={0} | all-to-all | bytes 786432 | tf_op jit(solution)/shard_map/all_to_all | solution.py:217
  20.7 74.3 %all-gather.4.cloned.1.call-done.refs_0_ = bf16[1536,1536]{1,0:T(8,128)(2,1)} async-done(((bf16[128,1536]{1,0:T(8,128)(2,1)}), bf16[1536,1536]{1,0:T(8,128)(2,1)}) %all-gather.4.cloned.1.call-update) | async-done | bytes 4718608 | tf_op jit(solution)/shard_map/all_gather | solution.py:218
  95.0 1.9 collective-permute-start
  98.6 1.1 add_convert_fusion
  100.7 2.3 settle.16.own_ref
  103.1 2.1 collective-permute-done.refs_0_.refs_1_
  105.2 2.3 settle.17.other_ref
  107.7 2.4 layer_forward.7
  110.2 4.6 %collective-permute-start.1 = (bf16[64,1536]{1,0:T(8,128)(2,1)S(1)}, bf16[64,1536]{1,0:T(8,128)(2,1)S(1)}, u32[]{:S(2)}, u32[]{:S(2)}) collective-permute-start(bf16[64,1536]{1,0:T(8,128)(2,1)S(1)} %get-tuple-element.88.refs_2_), channel_id=1, source_target_pairs={{0,96},{96,192},{192,288},{288,384},{384,480},{480,576},{576,672},... | collective-permute-start | bytes 589832 | tf_op jit(solution)/shard_map/ppermute | solution.py:270
  114.9 3.8 %settle.18 = (bf16[1536,1536]{1,0:T(8,128)(2,1)S(1)}, bf16[1536,1536]{1,0:T(8,128)(2,1)S(1)}) custom-call(bf16[1536,1536]{1,0:T(8,128)(2,1)} %all-gather.4.cloned.1.call-done.refs_0_, bf16[1536,1536]{1,0:T(8,128)(2,1)} %collective-permute-done.refs_0_.refs_1_, bf16[64,1536]{1,0:T(8,128)(2,1)S(1)} %get-tuple-element.88.refs_2_), custom_call_target="tpu_custom_call" | custom-call | bytes 37748736 | tf_op jit(solution)/shard_map/settle/pallas_call | solution.py:46
  119.3 2.4 layer_forward.8
  121.7 5.6 %collective-permute-start.2 = (bf16[64,1536]{1,0:T(8,128)(2,1)S(1)}, bf16[64,1536]{1,0:T(8,128)(2,1)S(1)}, u32[]{:S(2)}, u32[]{:S(2)}) collective-permute-start(bf16[64,1536]{1,0:T(8,128)(2,1)S(1)} %get-tuple-element.94.refs_2_), channel_id=1, source_target_pairs={{0,96},{96,192},{192,288},{288,384},{384,480},{480,576},{576,672},... | collective-permute-start | bytes 589832 | tf_op jit(solution)/shard_map/ppermute | solution.py:270
  127.4 3.8 %settle.19 = (bf16[1536,1536]{1,0:T(8,128)(2,1)S(1)}, bf16[1536,1536]{1,0:T(8,128)(2,1)S(1)}) custom-call(bf16[1536,1536]{1,0:T(8,128)(2,1)} %all-gather.4.cloned.1.call-done.refs_0_, bf16[1536,1536]{1,0:T(8,128)(2,1)} %collective-permute-done.refs_0_.refs_1_, bf16[64,1536]{1,0:T(8,128)(2,1)S(1)} %get-tuple-element.94.refs_2_), custom_call_target="tpu_custom_call" | custom-call | bytes 37748736 | tf_op jit(solution)/shard_map/settle/pallas_call | solution.py:46
  131.2 2.4 layer_forward.9
  133.7 5.3 %collective-permute-start.3 = (bf16[64,1536]{1,0:T(8,128)(2,1)S(1)}, bf16[64,1536]{1,0:T(8,128)(2,1)S(1)}, u32[]{:S(2)}, u32[]{:S(2)}) collective-permute-start(bf16[64,1536]{1,0:T(8,128)(2,1)S(1)} %get-tuple-element.100.refs_2_), channel_id=1, source_target_pairs={{0,96},{96,192},{192,288},{288,384},{384,480},{480,576},{576,672},... | collective-permute-start | bytes 589832 | tf_op jit(solution)/shard_map/ppermute | solution.py:270
  139.1 3.8 %settle.20 = (bf16[1536,1536]{1,0:T(8,128)(2,1)S(1)}, bf16[1536,1536]{1,0:T(8,128)(2,1)S(1)}) custom-call(bf16[1536,1536]{1,0:T(8,128)(2,1)} %all-gather.4.cloned.1.call-done.refs_0_, bf16[1536,1536]{1,0:T(8,128)(2,1)} %collective-permute-done.refs_0_.refs_1_, bf16[64,1536]{1,0:T(8,128)(2,1)S(1)} %get-tuple-element.100.refs_2_), custom_call_target="tpu_custom_call" | custom-call | bytes 37748736 | tf_op jit(solution)/shard_map/settle/pallas_call | solution.py:46
  142.9 2.4 layer_forward.10
  145.4 4.9 %collective-permute-start.4 = (bf16[64,1536]{1,0:T(8,128)(2,1)S(1)}, bf16[64,1536]{1,0:T(8,128)(2,1)S(1)}, u32[]{:S(2)}, u32[]{:S(2)}) collective-permute-start(bf16[64,1536]{1,0:T(8,128)(2,1)S(1)} %get-tuple-element.106.refs_2_), channel_id=1, source_target_pairs={{0,96},{96,192},{192,288},{288,384},{384,480},{480,576},{576,672},... | collective-permute-start | bytes 589832 | tf_op jit(solution)/shard_map/ppermute | solution.py:270
  150.3 3.8 %settle.21 = (bf16[1536,1536]{1,0:T(8,128)(2,1)S(1)}, bf16[1536,1536]{1,0:T(8,128)(2,1)S(1)}) custom-call(bf16[1536,1536]{1,0:T(8,128)(2,1)} %all-gather.4.cloned.1.call-done.refs_0_, bf16[1536,1536]{1,0:T(8,128)(2,1)} %collective-permute-done.refs_0_.refs_1_, bf16[64,1536]{1,0:T(8,128)(2,1)S(1)} %get-tuple-element.106.refs_2_), custom_call_target="tpu_custom_call" | custom-call | bytes 37748736 | tf_op jit(solution)/shard_map/settle/pallas_call | solution.py:46
  154.1 2.4 layer_forward.11
  156.6 4.9 %collective-permute-start.5 = (bf16[64,1536]{1,0:T(8,128)(2,1)S(1)}, bf16[64,1536]{1,0:T(8,128)(2,1)S(1)}, u32[]{:S(2)}, u32[]{:S(2)}) collective-permute-start(bf16[64,1536]{1,0:T(8,128)(2,1)S(1)} %get-tuple-element.112.refs_2_), channel_id=1, source_target_pairs={{0,96},{96,192},{192,288},{288,384},{384,480},{480,576},{576,672},... | collective-permute-start | bytes 589832 | tf_op jit(solution)/shard_map/ppermute | solution.py:270
  161.5 3.8 %settle.22 = (bf16[1536,1536]{1,0:T(8,128)(2,1)S(1)}, bf16[1536,1536]{1,0:T(8,128)(2,1)S(1)}) custom-call(bf16[1536,1536]{1,0:T(8,128)(2,1)} %all-gather.4.cloned.1.call-done.refs_0_, bf16[1536,1536]{1,0:T(8,128)(2,1)} %collective-permute-done.refs_0_.refs_1_, bf16[64,1536]{1,0:T(8,128)(2,1)S(1)} %get-tuple-element.112.refs_2_), custom_call_target="tpu_custom_call" | custom-call | bytes 37748736 | tf_op jit(solution)/shard_map/settle/pallas_call | solution.py:46
  165.4 2.4 layer_forward.12
  167.8 4.9 %collective-permute-start.6 = (bf16[64,1536]{1,0:T(8,128)(2,1)S(1)}, bf16[64,1536]{1,0:T(8,128)(2,1)S(1)}, u32[]{:S(2)}, u32[]{:S(2)}) collective-permute-start(bf16[64,1536]{1,0:T(8,128)(2,1)S(1)} %get-tuple-element.118.refs_2_), channel_id=1, source_target_pairs={{0,96},{96,192},{192,288},{288,384},{384,480},{480,576},{576,672},... | collective-permute-start | bytes 589832 | tf_op jit(solution)/shard_map/ppermute | solution.py:270
  172.8 3.8 %settle.23 = (bf16[1536,1536]{1,0:T(8,128)(2,1)S(1)}, bf16[1536,1536]{1,0:T(8,128)(2,1)S(1)}) custom-call(bf16[1536,1536]{1,0:T(8,128)(2,1)} %all-gather.4.cloned.1.call-done.refs_0_, bf16[1536,1536]{1,0:T(8,128)(2,1)} %collective-permute-done.refs_0_.refs_1_, bf16[64,1536]{1,0:T(8,128)(2,1)S(1)} %get-tuple-element.118.refs_2_), custom_call_target="tpu_custom_call" | custom-call | bytes 37748736 | tf_op jit(solution)/shard_map/settle/pallas_call | solution.py:46
  176.6 2.4 layer_forward.13
  179.0 5.0 %collective-permute-start.7 = (bf16[64,1536]{1,0:T(8,128)(2,1)S(1)}, bf16[64,1536]{1,0:T(8,128)(2,1)S(1)}, u32[]{:S(2)}, u32[]{:S(2)}) collective-permute-start(bf16[64,1536]{1,0:T(8,128)(2,1)S(1)} %get-tuple-element.124.refs_2_), channel_id=1, source_target_pairs={{0,96},{96,192},{192,288},{288,384},{384,480},{480,576},{576,672},... | collective-permute-start | bytes 589832 | tf_op jit(solution)/shard_map/ppermute | solution.py:270
  184.2 3.8 %settle.24 = (bf16[1536,1536]{1,0:T(8,128)(2,1)S(1)}, bf16[1536,1536]{1,0:T(8,128)(2,1)S(1)}) custom-call(bf16[1536,1536]{1,0:T(8,128)(2,1)} %all-gather.4.cloned.1.call-done.refs_0_, bf16[1536,1536]{1,0:T(8,128)(2,1)} %collective-permute-done.refs_0_.refs_1_, bf16[64,1536]{1,0:T(8,128)(2,1)S(1)} %get-tuple-element.124.refs_2_), custom_call_target="tpu_custom_call" | custom-call | bytes 37748736 | tf_op jit(solution)/shard_map/settle/pallas_call | solution.py:46
  188.1 5.5 %layer_turn.2 = (bf16[64,1536]{1,0:T(8,128)(2,1)S(1)}, bf16[64,1536]{1,0:T(8,128)(2,1)S(1)}, bf16[3,64,1536]{2,1,0:T(8,128)(2,1)S(1)}, f32[3,64,1536]{2,1,0:T(8,...) custom-call(s32[5]{0:T(128)S(1)} %stack.236.meta, ...), custom_call_target="tpu_custom_call", output_to_operand_aliasing={{2}: (5, {}), {3}: (6, {}), {4}: (7, {}), {5}: (8, {})} | custom-call | tf_op jit(solution)/shard_map/layer_turn/pallas_call | solution.py:192
  194.3 1.9 collective-permute-start.9
  196.4 5.3 %collective-permute-start.8 = (bf16[64,1536]{1,0:T(8,128)(2,1)}, bf16[64,1536]{1,0:T(8,128)(2,1)S(1)}, u32[]{:S(2)}, u32[]{:S(2)}) collective-permute-start(bf16[64,1536]{1,0:T(8,128)(2,1)} %copy-done.2), channel_id=1, source_target_pairs={{0,96},{96,192},{192,288},{288,384},{384,480},{480,576},{576,672},... | collective-permute-start | bytes 589832 | tf_op jit(solution)/shard_map/ppermute | solution.py:270
  201.6 3.8 %settle.25 = (bf16[1536,1536]{1,0:T(8,128)(2,1)S(1)}, bf16[1536,1536]{1,0:T(8,128)(2,1)S(1)}) custom-call(bf16[1536,1536]{1,0:T(8,128)(2,1)} %all-gather.4.cloned.1.call-done.refs_0_, bf16[1536,1536]{1,0:T(8,128)(2,1)} %collective-permute-done.refs_0_.refs_1_, bf16[64,1536]{1,0:T(8,128)(2,1)S(1)} %get-tuple-element.131.refs_2_), custom_call_target="tpu_custom_call" | custom-call | bytes 37748736 | tf_op jit(solution)/shard_map/settle/pallas_call | solution.py:46
  205.5 5.5 %layer_turn.3 = (bf16[64,1536]{1,0:T(8,128)(2,1)}, bf16[64,1536]{1,0:T(8,128)(2,1)S(1)}, bf16[3,64,1536]{2,1,0:T(8,128)(2,1)S(1)}, f32[3,64,1536]{2,1,0:T(8,128)...) custom-call(s32[5]{0:T(128)S(1)} %stack.233.meta, ...), custom_call_target="tpu_custom_call", output_to_operand_aliasing={{2}: (5, {}), {3}: (6, {}), {4}: (7, {}), {5}: (8, {})} | custom-call | tf_op jit(solution)/shard_map/layer_turn/pallas_call | solution.py:192
  211.0 1.9 collective-permute-start.10
  213.8 3.0 collective-permute-start.13
  216.8 3.8 %settle.26 = (bf16[1536,1536]{1,0:T(8,128)(2,1)S(1)}, bf16[1536,1536]{1,0:T(8,128)(2,1)S(1)}) custom-call(bf16[1536,1536]{1,0:T(8,128)(2,1)} %all-gather.4.cloned.1.call-done.refs_0_, bf16[1536,1536]{1,0:T(8,128)(2,1)} %collective-permute-done.refs_0_.refs_1_, bf16[64,1536]{1,0:T(8,128)(2,1)S(1)} %get-tuple-element.138.refs_2_), custom_call_target="tpu_custom_call" | custom-call | bytes 37748736 | tf_op jit(solution)/shard_map/settle/pallas_call | solution.py:46
  220.6 3.6 layer_backward.6
  224.2 3.7 %collective-permute-start.14 = (bf16[2,64,1536]{2,1,0:T(8,128)(2,1)}, bf16[2,64,1536]{2,1,0:T(8,128)(2,1)}, u32[]{:S(2)}, u32[]{:S(2)}) collective-permute-start(bf16[2,64,1536]{2,1,0:T(8,128)(2,1)} %get-tuple-element.150), channel_id=1, source_target_pairs={{0,16},{8,0},{16,8},{1,17},{9,1},{17,9},{2,18},{10,2},{18,10},{3,1... | collective-permute-start | bytes 1179656 | tf_op jit(solution)/shard_map/ppermute | solution.py:275
  228.0 1.9 collective-permute-start.11
  230.0 3.8 %settle.27 = (bf16[1536,1536]{1,0:T(8,128)(2,1)S(1)}, bf16[1536,1536]{1,0:T(8,128)(2,1)S(1)}) custom-call(bf16[1536,1536]{1,0:T(8,128)(2,1)} %all-gather.4.cloned.1.call-done.refs_0_, bf16[1536,1536]{1,0:T(8,128)(2,1)} %collective-permute-done.refs_0_.refs_1_, bf16[64,1536]{1,0:T(8,128)(2,1)S(1)} %get-tuple-element.144.refs_2_), custom_call_target="tpu_custom_call" | custom-call | bytes 37748736 | tf_op jit(solution)/shard_map/settle/pallas_call | solution.py:46
  233.8 2.9 collective-permute-done.11.g_ref
  236.7 3.6 layer_backward.7
  240.4 2.3 pad_maximum_fusion
  242.7 1.9 collective-permute-start.12
  244.7 3.8 %settle.28 = (bf16[1536,1536]{1,0:T(8,128)(2,1)S(1)}, bf16[1536,1536]{1,0:T(8,128)(2,1)S(1)}) custom-call(bf16[1536,1536]{1,0:T(8,128)(2,1)} %all-gather.4.cloned.1.call-done.refs_0_, bf16[1536,1536]{1,0:T(8,128)(2,1)} %collective-permute-done.refs_0_.refs_1_, bf16[64,1536]{1,0:T(8,128)(2,1)S(1)} %get-tuple-element.151.refs_2_), custom_call_target="tpu_custom_call" | custom-call | bytes 37748736 | tf_op jit(solution)/shard_map/settle/pallas_call | solution.py:46
  248.5 3.5 collective-permute-done.12.g_ref
  252.0 3.6 layer_backward.8
  255.6 2.1 collective-permute-start.15
  257.9 4.9 %settle.29 = (bf16[1536,1536]{1,0:T(8,128)(2,1)S(1)}, bf16[1536,1536]{1,0:T(8,128)(2,1)S(1)}) custom-call(bf16[1536,1536]{1,0:T(8,128)(2,1)} %all-gather.4.cloned.1.call-done.refs_0_, bf16[1536,1536]{1,0:T(8,128)(2,1)} %collective-permute-done.refs_0_.refs_1_, bf16[64,1536]{1,0:T(8,128)(2,1)S(1)} %get-tuple-element.155.refs_2_), custom_call_target="tpu_custom_call" | custom-call | bytes 37748736 | tf_op jit(solution)/shard_map/settle/pallas_call | solution.py:46
  262.8 3.4 collective-permute-done.15.g_ref
  266.1 3.6 layer_backward.9
  269.8 1.9 collective-permute-start.16
  271.8 4.0 %settle.30 = (bf16[1536,1536]{1,0:T(8,128)(2,1)S(1)}, bf16[1536,1536]{1,0:T(8,128)(2,1)S(1)}) custom-call(bf16[1536,1536]{1,0:T(8,128)(2,1)} %all-gather.4.cloned.1.call-done.refs_0_, bf16[1536,1536]{1,0:T(8,128)(2,1)} %collective-permute-done.refs_0_.refs_1_, bf16[64,1536]{1,0:T(8,128)(2,1)S(1)} %get-tuple-element.159.refs_2_), custom_call_target="tpu_custom_call" | custom-call | bytes 37748736 | tf_op jit(solution)/shard_map/settle/pallas_call | solution.py:46
  275.8 4.5 %collective-permute-done.16.g_ref = bf16[64,1536]{1,0:T(8,128)(2,1)S(1)} collective-permute-done((bf16[64,1536]{1,0:T(8,128)(2,1)S(1)}, bf16[64,1536]{1,0:T(8,128)(2,1)S(1)}, u32[]{:S(2)}, u32[]{:S(2)}) %collective-permute-start.16) | collective-permute-done | bytes 196640 | tf_op jit(solution)/shard_map/ppermute | solution.py:272
  280.3 3.6 layer_backward.10
  283.9 1.9 collective-permute-start.17
  285.9 4.0 %settle.31 = (bf16[1536,1536]{1,0:T(8,128)(2,1)S(1)}, bf16[1536,1536]{1,0:T(8,128)(2,1)S(1)}) custom-call(bf16[1536,1536]{1,0:T(8,128)(2,1)} %all-gather.4.cloned.1.call-done.refs_0_, bf16[1536,1536]{1,0:T(8,128)(2,1)} %collective-permute-done.refs_0_.refs_1_, bf16[64,1536]{1,0:T(8,128)(2,1)S(1)} %get-tuple-element.163.refs_2_), custom_call_target="tpu_custom_call" | custom-call | bytes 37748736 | tf_op jit(solution)/shard_map/settle/pallas_call | solution.py:46
  289.9 3.8 %collective-permute-done.17.g_ref = bf16[64,1536]{1,0:T(8,128)(2,1)S(1)} collective-permute-done((bf16[64,1536]{1,0:T(8,128)(2,1)S(1)}, bf16[64,1536]{1,0:T(8,128)(2,1)S(1)}, u32[]{:S(2)}, u32[]{:S(2)}) %collective-permute-start.17) | collective-permute-done | bytes 196640 | tf_op jit(solution)/shard_map/ppermute | solution.py:272
  293.7 3.6 layer_backward.11
  297.4 1.9 collective-permute-start.18
  299.4 6.8 %collective-permute-done.18.g_ref = bf16[64,1536]{1,0:T(8,128)(2,1)S(1)} collective-permute-done((bf16[64,1536]{1,0:T(8,128)(2,1)S(1)}, bf16[64,1536]{1,0:T(8,128)(2,1)S(1)}, u32[]{:S(2)}, u32[]{:S(2)}) %collective-permute-start.18) | collective-permute-done | bytes 196640 | tf_op jit(solution)/shard_map/ppermute | solution.py:272
  307.0 16.1 %all_to_all.33 = bf16[24,64,128]{2,1,0:T(8,128)(2,1)S(1)} all-to-all(bf16[24,64,128]{2,1,0:T(8,128)(2,1)S(1)} %bitcast.66), channel_id=1, replica_groups=mesh['section'=8,'zh'=4,'zl'=3,'x'=4,'core'=2] {'x','core','zl'}, dimensions={0} | all-to-all | bytes 786432 | tf_op jit(solution)/shard_map/all_to_all | solution.py:283
  323.1 5.0 %weight_partials.1 = bf16[1536,128]{1,0:T(8,128)(2,1)S(1)} custom-call(s32[5]{0:T(128)S(1)} %stack.212.meta, bf16[1536,128]{1,0:T(8,128)(2,1)S(1)} %bitcast.64, bf16[3072,1536]{1,0:T(8,128)(2,1)} %bitcast.67), custom_call_target="tpu_custom_call" | custom-call | tf_op jit(solution)/shard_map/weight_partials/pallas_call | solution.py:161
  328.1 33.7 %all_to_all.34 = bf16[96,16,128]{2,1,0:T(8,128)(2,1)S(1)} all-to-all(bf16[96,16,128]{2,1,0:T(8,128)(2,1)S(1)} %bitcast.65), channel_id=1, replica_groups=mesh['section'=8,'zh'=4,'zl'=3,'x'=4,'core'=2] {'zh','zl','x','core'}, dimensions={0} | all-to-all | bytes 786432 | tf_op jit(solution)/shard_map/all_to_all | solution.py:285
  (60 shorter events, 9.2 us)
Async XLA Ops:
  6.5 91.2 %copy-start = (bf16[128,1536]{1,0:T(8,128)(2,1)S(1)}, bf16[128,1536]{1,0:T(8,128)(2,1)}, u32[]{:S(2)}) copy-start(bf16[128,1536]{1,0:T(8,128)(2,1)} %param.8) | copy-start | bytes 1179652
  6.5 88.5 %all-gather.4.cloned.1.call-start = ((), (), s32[]{:S(2)}) async-start(), calls=%async_computation.3 | async-start | bytes 5111808 | tf_op jit(solution)/shard_map/all_gather | solution.py:218
  20.7 302.4 %all-gather.6.cloned.1.call-start = ((), (), s32[]{:S(2)}) async-start(), calls=%async_computation.4 | async-start | bytes 10616832 | tf_op jit(solution)/shard_map/all_gather | solution.py:266
  95.0 10.1 %collective-permute-start = (bf16[1536,1536]{1,0:T(8,128)(2,1)}, bf16[1536,1536]{1,0:T(8,128)(2,1)}, u32[]{:S(2)}, u32[]{:S(2)}) collective-permute-start(bf16[1536,1536]{1,0:T(8,128)(2,1)} %all-gather.4.cloned.1.call-done.refs_0_), channel_id=1, source_target_pairs={{0,1},{1,0},{2,3},{3,2},{4,5},{5,4},{6,7},{7,6},{8,9},{9,8},{10,11... | collective-permute-start | bytes 14155784 | tf_op jit(solution)/shard_map/ppermute | solution.py:219
  110.2 9.1 %collective-permute-start.1 = (bf16[64,1536]{1,0:T(8,128)(2,1)S(1)}, bf16[64,1536]{1,0:T(8,128)(2,1)S(1)}, u32[]{:S(2)}, u32[]{:S(2)}) collective-permute-start(bf16[64,1536]{1,0:T(8,128)(2,1)S(1)} %get-tuple-element.88.refs_2_), channel_id=1, source_target_pairs={{0,96},{96,192},{192,288},{288,384},{384,480},{480,576},{576,672},... | collective-permute-start | bytes 589832 | tf_op jit(solution)/shard_map/ppermute | solution.py:270
  121.7 9.5 %collective-permute-start.2 = (bf16[64,1536]{1,0:T(8,128)(2,1)S(1)}, bf16[64,1536]{1,0:T(8,128)(2,1)S(1)}, u32[]{:S(2)}, u32[]{:S(2)}) collective-permute-start(bf16[64,1536]{1,0:T(8,128)(2,1)S(1)} %get-tuple-element.94.refs_2_), channel_id=1, source_target_pairs={{0,96},{96,192},{192,288},{288,384},{384,480},{480,576},{576,672},... | collective-permute-start | bytes 589832 | tf_op jit(solution)/shard_map/ppermute | solution.py:270
  133.7 9.2 %collective-permute-start.3 = (bf16[64,1536]{1,0:T(8,128)(2,1)S(1)}, bf16[64,1536]{1,0:T(8,128)(2,1)S(1)}, u32[]{:S(2)}, u32[]{:S(2)}) collective-permute-start(bf16[64,1536]{1,0:T(8,128)(2,1)S(1)} %get-tuple-element.100.refs_2_), channel_id=1, source_target_pairs={{0,96},{96,192},{192,288},{288,384},{384,480},{480,576},{576,672},... | collective-permute-start | bytes 589832 | tf_op jit(solution)/shard_map/ppermute | solution.py:270
  145.4 8.8 %collective-permute-start.4 = (bf16[64,1536]{1,0:T(8,128)(2,1)S(1)}, bf16[64,1536]{1,0:T(8,128)(2,1)S(1)}, u32[]{:S(2)}, u32[]{:S(2)}) collective-permute-start(bf16[64,1536]{1,0:T(8,128)(2,1)S(1)} %get-tuple-element.106.refs_2_), channel_id=1, source_target_pairs={{0,96},{96,192},{192,288},{288,384},{384,480},{480,576},{576,672},... | collective-permute-start | bytes 589832 | tf_op jit(solution)/shard_map/ppermute | solution.py:270
  156.6 8.8 %collective-permute-start.5 = (bf16[64,1536]{1,0:T(8,128)(2,1)S(1)}, bf16[64,1536]{1,0:T(8,128)(2,1)S(1)}, u32[]{:S(2)}, u32[]{:S(2)}) collective-permute-start(bf16[64,1536]{1,0:T(8,128)(2,1)S(1)} %get-tuple-element.112.refs_2_), channel_id=1, source_target_pairs={{0,96},{96,192},{192,288},{288,384},{384,480},{480,576},{576,672},... | collective-permute-start | bytes 589832 | tf_op jit(solution)/shard_map/ppermute | solution.py:270
  167.8 8.8 %collective-permute-start.6 = (bf16[64,1536]{1,0:T(8,128)(2,1)S(1)}, bf16[64,1536]{1,0:T(8,128)(2,1)S(1)}, u32[]{:S(2)}, u32[]{:S(2)}) collective-permute-start(bf16[64,1536]{1,0:T(8,128)(2,1)S(1)} %get-tuple-element.118.refs_2_), channel_id=1, source_target_pairs={{0,96},{96,192},{192,288},{288,384},{384,480},{480,576},{576,672},... | collective-permute-start | bytes 589832 | tf_op jit(solution)/shard_map/ppermute | solution.py:270
  176.6 7.5 %copy-start.3 = (bf16[2,1,64,1536]{3,2,1,0:T(8,128)(2,1)S(1)}, bf16[2,1,64,1536]{3,2,1,0:T(8,128)(2,1)}, u32[]{:S(2)}) copy-start(bf16[2,1,64,1536]{3,2,1,0:T(8,128)(2,1)} %param.11) | copy-start | bytes 1179652
  179.0 9.0 %collective-permute-start.7 = (bf16[64,1536]{1,0:T(8,128)(2,1)S(1)}, bf16[64,1536]{1,0:T(8,128)(2,1)S(1)}, u32[]{:S(2)}, u32[]{:S(2)}) collective-permute-start(bf16[64,1536]{1,0:T(8,128)(2,1)S(1)} %get-tuple-element.124.refs_2_), channel_id=1, source_target_pairs={{0,96},{96,192},{192,288},{288,384},{384,480},{480,576},{576,672},... | collective-permute-start | bytes 589832 | tf_op jit(solution)/shard_map/ppermute | solution.py:270
  193.6 0.7 copy-start.2
  194.3 11.2 %collective-permute-start.9 = (bf16[64,1536]{1,0:T(8,128)(2,1)S(1)}, bf16[64,1536]{1,0:T(8,128)(2,1)S(1)}, u32[]{:S(2)}, u32[]{:S(2)}) collective-permute-start(bf16[64,1536]{1,0:T(8,128)(2,1)S(1)} %get-tuple-element.131.refs_2_), channel_id=1, source_target_pairs={{96,0},{192,96},{288,192},{384,288},{480,384},{576,480},{672,576},... | collective-permute-start | bytes 589832 | tf_op jit(solution)/shard_map/ppermute | solution.py:272
  196.4 9.1 %copy-start.4 = (bf16[2,1,64,1536]{3,2,1,0:T(8,128)(2,1)S(1)}, bf16[2,1,64,1536]{3,2,1,0:T(8,128)(2,1)}, u32[]{:S(2)}) copy-start(bf16[2,1,64,1536]{3,2,1,0:T(8,128)(2,1)} %param.11) | copy-start | bytes 1179652
  196.4 9.1 %collective-permute-start.8 = (bf16[64,1536]{1,0:T(8,128)(2,1)}, bf16[64,1536]{1,0:T(8,128)(2,1)S(1)}, u32[]{:S(2)}, u32[]{:S(2)}) collective-permute-start(bf16[64,1536]{1,0:T(8,128)(2,1)} %copy-done.2), channel_id=1, source_target_pairs={{0,96},{96,192},{192,288},{288,384},{384,480},{480,576},{576,672},... | collective-permute-start | bytes 589832 | tf_op jit(solution)/shard_map/ppermute | solution.py:270
  211.0 9.6 %collective-permute-start.10 = (bf16[64,1536]{1,0:T(8,128)(2,1)S(1)}, bf16[64,1536]{1,0:T(8,128)(2,1)S(1)}, u32[]{:S(2)}, u32[]{:S(2)}) collective-permute-start(bf16[64,1536]{1,0:T(8,128)(2,1)S(1)} %get-tuple-element.138.refs_2_), channel_id=1, source_target_pairs={{96,0},{192,96},{288,192},{384,288},{480,384},{576,480},{672,576},... | collective-permute-start | bytes 589832 | tf_op jit(solution)/shard_map/ppermute | solution.py:272
  213.8 26.6 %collective-permute-start.13 = (bf16[2,64,1536]{2,1,0:T(8,128)(2,1)}, bf16[2,64,1536]{2,1,0:T(8,128)(2,1)}, u32[]{:S(2)}, u32[]{:S(2)}) collective-permute-start(bf16[2,64,1536]{2,1,0:T(8,128)(2,1)} %get-tuple-element.150), channel_id=1, source_target_pairs={{0,8},{8,16},{16,0},{1,9},{9,17},{17,1},{2,10},{10,18},{18,2},{3,1... | collective-permute-start | bytes 1179656 | tf_op jit(solution)/shard_map/ppermute | solution.py:279
  224.2 16.1 %collective-permute-start.14 = (bf16[2,64,1536]{2,1,0:T(8,128)(2,1)}, bf16[2,64,1536]{2,1,0:T(8,128)(2,1)}, u32[]{:S(2)}, u32[]{:S(2)}) collective-permute-start(bf16[2,64,1536]{2,1,0:T(8,128)(2,1)} %get-tuple-element.150), channel_id=1, source_target_pairs={{0,16},{8,0},{16,8},{1,17},{9,1},{17,9},{2,18},{10,2},{18,10},{3,1... | collective-permute-start | bytes 1179656 | tf_op jit(solution)/shard_map/ppermute | solution.py:275
  228.0 8.8 %collective-permute-start.11 = (bf16[64,1536]{1,0:T(8,128)(2,1)S(1)}, bf16[64,1536]{1,0:T(8,128)(2,1)S(1)}, u32[]{:S(2)}, u32[]{:S(2)}) collective-permute-start(bf16[64,1536]{1,0:T(8,128)(2,1)S(1)} %get-tuple-element.144.refs_2_), channel_id=1, source_target_pairs={{96,0},{192,96},{288,192},{384,288},{480,384},{576,480},{672,576},... | collective-permute-start | bytes 589832 | tf_op jit(solution)/shard_map/ppermute | solution.py:272
  242.7 9.3 %collective-permute-start.12 = (bf16[64,1536]{1,0:T(8,128)(2,1)S(1)}, bf16[64,1536]{1,0:T(8,128)(2,1)S(1)}, u32[]{:S(2)}, u32[]{:S(2)}) collective-permute-start(bf16[64,1536]{1,0:T(8,128)(2,1)S(1)} %get-tuple-element.151.refs_2_), channel_id=1, source_target_pairs={{96,0},{192,96},{288,192},{384,288},{480,384},{576,480},{672,576},... | collective-permute-start | bytes 589832 | tf_op jit(solution)/shard_map/ppermute | solution.py:272
  255.6 10.5 %collective-permute-start.15 = (bf16[64,1536]{1,0:T(8,128)(2,1)S(1)}, bf16[64,1536]{1,0:T(8,128)(2,1)S(1)}, u32[]{:S(2)}, u32[]{:S(2)}) collective-permute-start(bf16[64,1536]{1,0:T(8,128)(2,1)S(1)} %get-tuple-element.155.refs_2_), channel_id=1, source_target_pairs={{96,0},{192,96},{288,192},{384,288},{480,384},{576,480},{672,576},... | collective-permute-start | bytes 589832 | tf_op jit(solution)/shard_map/ppermute | solution.py:272
  269.8 10.5 %collective-permute-start.16 = (bf16[64,1536]{1,0:T(8,128)(2,1)S(1)}, bf16[64,1536]{1,0:T(8,128)(2,1)S(1)}, u32[]{:S(2)}, u32[]{:S(2)}) collective-permute-start(bf16[64,1536]{1,0:T(8,128)(2,1)S(1)} %get-tuple-element.159.refs_2_), channel_id=1, source_target_pairs={{96,0},{192,96},{288,192},{384,288},{480,384},{576,480},{672,576},... | collective-permute-start | bytes 589832 | tf_op jit(solution)/shard_map/ppermute | solution.py:272
  283.9 9.8 %collective-permute-start.17 = (bf16[64,1536]{1,0:T(8,128)(2,1)S(1)}, bf16[64,1536]{1,0:T(8,128)(2,1)S(1)}, u32[]{:S(2)}, u32[]{:S(2)}) collective-permute-start(bf16[64,1536]{1,0:T(8,128)(2,1)S(1)} %get-tuple-element.163.refs_2_), channel_id=1, source_target_pairs={{96,0},{192,96},{288,192},{384,288},{480,384},{576,480},{672,576},... | collective-permute-start | bytes 589832 | tf_op jit(solution)/shard_map/ppermute | solution.py:272
  297.4 8.8 %collective-permute-start.18 = (bf16[64,1536]{1,0:T(8,128)(2,1)S(1)}, bf16[64,1536]{1,0:T(8,128)(2,1)S(1)}, u32[]{:S(2)}, u32[]{:S(2)}) collective-permute-start(bf16[64,1536]{1,0:T(8,128)(2,1)S(1)} %get-tuple-element.167), channel_id=1, source_target_pairs={{96,0},{192,96},{288,192},{384,288},{480,384},{576,480},{672,576},... | collective-permute-start | bytes 589832 | tf_op jit(solution)/shard_map/ppermute | solution.py:272
  323.1 40.4 %copy-start.1 = (bf16[128,1536]{1,0:T(8,128)(2,1)S(1)}, bf16[128,1536]{1,0:T(8,128)(2,1)}, u32[]{:S(2)}) copy-start(bf16[128,1536]{1,0:T(8,128)(2,1)} %param.8) | copy-start | bytes 1179652
Sparse Core Ops, SparseCore 0:
  20.8 74.1 all-gather.3
  242.8 61.0 all-gather.5
